TPU v7x, 128 devices: a whole 4x4x4 slice. The times are simulated.
128 devices in a mesh: dp: 4 (over x), fsdp: 32 (over z, y, core).
Axes of the slice: x: 4, y: 4, z: 4, core: 2. Of those that a mesh axis runs over, the one named last changes fastest.
Arguments:
- mlp_input: bfloat16 [1024, 4096], P('dp', 'fsdp'), may hold values from -6 to 6
- residual_in: bfloat16 [1024, 4096], P(('dp', 'fsdp')), may hold values from -6 to 6
- gate_weight: bfloat16 [4096, 14336], P(None, 'fsdp'), may hold values from -0.09375 to 0.09375
- up_weight: bfloat16 [4096, 14336], P(None, 'fsdp'), may hold values from -0.09375 to 0.09375
- down_weight: bfloat16 [14336, 4096], P('fsdp'), may hold values from -0.046875 to 0.046875
- span_index: bfloat16 [65536, 4096], P(('dp', 'fsdp')), may hold values from -6 to 6
- positive_keys: bfloat16 [1024, 4096], P(('dp', 'fsdp')), may hold values from -6 to 6
- request_rows: int32 [128, 128, 8], P(None, ('dp', 'fsdp')), may hold values from 0 to 511, as said below
- request_counts: int32 [128, 128], P(None, ('dp', 'fsdp')), may hold values from 0 to 8, as said below
- negative_slots: int32 [1024, 64], P(('dp', 'fsdp')), may hold values from 0 to 1023, as said below
Outputs:
- query_loss: float32 [1024], P(('dp', 'fsdp'))
- input_grad: bfloat16 [1024, 4096], P('dp', 'fsdp')
- gate_grad: bfloat16 [4096, 14336], P('dp', 'fsdp')
- up_grad: bfloat16 [4096, 14336], P('dp', 'fsdp')
- down_grad: bfloat16 [14336, 4096], P('fsdp', 'dp')
Inputs may be any that keep to these rules, and one draw needn't show every extreme that they name: `request_rows`: entry [r, o, s] is a local row of shard o; it is read only where s < request_counts[r, o]. `request_counts`: for each requesting device r the counts over the 128 shards sum to 512, and some shard gets exactly 8. `negative_slots`: rows q of device r = q // 8; an entry o * 8 + s names slot s of shard o with s < request_counts[r, o]; the 512 entries of a device use each such slot exactly once.
All inputs are finite; a program needn't handle non-finite values.
Results may differ from a plain program's by a relative error of at most 0.017.
Values may be sent and summed in bfloat16 or wider, within the bound.
A program may use at most 128 MiB of HBM per device.

v0:
```python
import jax
import jax.numpy as jnp
from jax import lax
from jax.sharding import PartitionSpec as P

inverse_temp = 50.0
eps = 1e-06
contract_first = (((0,), (0,)), ((), ()))
contract_last = (((1,), (1,)), ((), ()))


def silu_grad(gate_act):
    sigmoid_gate = jax.nn.sigmoid(gate_act)
    return sigmoid_gate * (1.0 + gate_act * (1.0 - sigmoid_gate))


def contrast(unit_rows, row_norm, key_block):
    key_unit = key_block / jnp.sqrt(jnp.sum(key_block * key_block, axis=-1, keepdims=True) + eps)
    scores = inverse_temp * jnp.einsum(
        "qd,qnd->qn", unit_rows, key_unit, precision=lax.Precision.HIGHEST
    )
    weights = jnp.exp(scores)
    exp_total = jnp.sum(weights, axis=-1)
    query_loss = jnp.log(exp_total) - scores[:, 0]
    column = lax.broadcasted_iota(jnp.int32, scores.shape, 1)
    coeffs = weights / exp_total[:, None] - (column == 0).astype(scores.dtype)
    pull_term = inverse_temp * jnp.einsum(
        "qn,qnd->qd", coeffs, key_unit, precision=lax.Precision.HIGHEST
    )
    inner_term = jnp.sum(coeffs * scores, axis=-1)
    head_grad = ((pull_term - inner_term[:, None] * unit_rows) / row_norm[:, None]).astype(
        jnp.bfloat16
    )
    return (query_loss, head_grad)


def shards(
    mlp_input,
    residual_in,
    gate_weight,
    up_weight,
    down_weight,
    span_index,
    positive_keys,
    request_rows,
    request_counts,
    negative_slots,
):
    dp_count = lax.axis_size("dp")
    fsdp_count = lax.axis_size("fsdp")
    owners = dp_count * fsdp_count
    slot_cap = request_rows.shape[2]
    feature_width = span_index.shape[1]
    whole_input = lax.all_gather(mlp_input, "fsdp", axis=1, tiled=True)
    gate_act = jnp.dot(whole_input, gate_weight, preferred_element_type=jnp.float32)
    up_act = jnp.dot(whole_input, up_weight, preferred_element_type=jnp.float32)
    hidden = (jax.nn.silu(gate_act) * up_act).astype(jnp.bfloat16)
    branch = lax.psum_scatter(
        jnp.dot(hidden, down_weight, preferred_element_type=jnp.float32).astype(jnp.bfloat16),
        "fsdp",
        scatter_dimension=0,
        tiled=True,
    ).astype(jnp.float32)
    top_state = branch + residual_in.astype(jnp.float32)
    row_norm = jnp.sqrt(jnp.sum(top_state * top_state, axis=-1) + eps)
    unit_rows = top_state / row_norm[:, None]
    row_table = request_rows[:, 0, :]
    count_table = request_counts[:, 0]
    picked = jnp.take(span_index, row_table.reshape(-1), axis=0).reshape(
        owners, slot_cap, feature_width
    )
    live_mask = lax.broadcasted_iota(jnp.int32, (owners, slot_cap), 1) < count_table[:, None]
    picked = jnp.where(live_mask[..., None], picked, jnp.zeros_like(picked))
    buffer = lax.all_to_all(picked, ("dp", "fsdp"), split_axis=0, concat_axis=0, tiled=True)
    flat_buffer = buffer.reshape(owners * slot_cap, feature_width)
    fetched = jnp.take(flat_buffer, negative_slots.reshape(-1), axis=0)
    fetched = fetched.reshape(
        negative_slots.shape[0], negative_slots.shape[1], feature_width
    ).astype(jnp.float32)
    key_block = jnp.concatenate([positive_keys.astype(jnp.float32)[:, None, :], fetched], axis=1)
    query_loss, head_grad = contrast(unit_rows, row_norm, key_block)
    gathered_grad = lax.all_gather(head_grad, "fsdp", axis=0, tiled=True)
    hidden_grad = lax.dot_general(
        gathered_grad, down_weight, contract_last, preferred_element_type=jnp.float32
    )
    gate_grad_act = (hidden_grad * up_act * silu_grad(gate_act)).astype(jnp.bfloat16)
    up_grad_act = (hidden_grad * jax.nn.silu(gate_act)).astype(jnp.bfloat16)
    input_term = lax.dot_general(
        gate_grad_act, gate_weight, contract_last, preferred_element_type=jnp.float32
    ) + lax.dot_general(up_grad_act, up_weight, contract_last, preferred_element_type=jnp.float32)
    input_grad = lax.psum_scatter(
        input_term.astype(jnp.bfloat16), "fsdp", scatter_dimension=1, tiled=True
    )
    gate_term = lax.dot_general(
        whole_input, gate_grad_act, contract_first, preferred_element_type=jnp.float32
    )
    up_term = lax.dot_general(
        whole_input, up_grad_act, contract_first, preferred_element_type=jnp.float32
    )
    down_term = lax.dot_general(
        hidden, gathered_grad, contract_first, preferred_element_type=jnp.float32
    )
    gate_sum, up_sum = (
        lax.psum_scatter(
            gate_term.astype(jnp.bfloat16), "dp", scatter_dimension=0, tiled=True
        ).astype(jnp.float32),
        lax.psum_scatter(
            up_term.astype(jnp.bfloat16), "dp", scatter_dimension=0, tiled=True
        ).astype(jnp.float32),
    )
    down_sum = lax.psum_scatter(
        down_term.astype(jnp.bfloat16), "dp", scatter_dimension=1, tiled=True
    )
    gate_grad = gate_sum.astype(jnp.bfloat16)
    up_grad = up_sum.astype(jnp.bfloat16)
    return (query_loss, input_grad, gate_grad, up_grad, down_sum)


def solution(mesh):
    return jax.shard_map(
        shards,
        mesh=mesh,
        in_specs=(
            P("dp", "fsdp"),
            P(("dp", "fsdp"), None),
            P(None, "fsdp"),
            P(None, "fsdp"),
            P("fsdp", None),
            P(("dp", "fsdp"), None),
            P(("dp", "fsdp"), None),
            P(None, ("dp", "fsdp"), None),
            P(None, ("dp", "fsdp")),
            P(("dp", "fsdp"), None),
        ),
        out_specs=(
            P(("dp", "fsdp")),
            P("dp", "fsdp"),
            P("dp", "fsdp"),
            P("dp", "fsdp"),
            P("fsdp", "dp"),
        ),
        check_vma=False,
    )
```

profile of v0, /device:TPU:1, one launch (start us, length us, event | category | flops | bytes accessed | tf_op | source)
XLA Modules:
  0.0 547.2 jit_solution(9983815885430911765)
XLA Ops:
  7.2 0.0 all-gather.3.cloned.1.call-start
  7.2 0.7 all-gather.3.cloned.1.call-update
  7.9 0.8 copy.21
  8.7 0.1 reshape_squeeze.6
  8.8 0.7 iota_compare_fusion
  9.6 0.7 compare_and_fusion
  10.3 0.1 copy.20
  10.4 17.8 %gather_fusion = bf16[1024,4096]{1,0:T(8,128)(2,1)} fusion(bf16[512,4096]{1,0:T(8,128)(2,1)} %param.15, s32[1024]{0:T(1024)S(1)} %broadcast_clamp_fusion), kind=kCustom, calls=%fused_computation | custom fusion | bytes 16781312 | tf_op jit(solution)/shard_map/jit(_take)/gather | solution.py:69
  28.2 7.4 %fusion.1 = bf16[128,8,4096]{2,1,0:T(8,128)(2,1)} fusion(bf16[1024,4096]{1,0:T(8,128)(2,1)} %gather_fusion, pred[128,8]{1,0:T(8,128)(4,1)S(1)} %copy.20, pred[128,8]{1,0:T(8,128)(4,1)S(1)} %iota_compare_fusion), kind=kLoop, calls=%fused_computation.6 | loop fusion | flops 8388608 | bytes 16779264 | tf_op jit(solution)/shard_map/jit(_where)/select_n | solution.py:73
  35.6 11.9 %all-to-all-start = ((bf16[128,8,4096]{2,1,0:T(8,128)(2,1)}), bf16[128,8,4096]{2,1,0:T(8,128)(2,1)}, u32[]{:S(2)}, u32[]{:S(2)}) async-start(bf16[128,8,4096]{2,1,0:T(8,128)(2,1)} %fusion.1), calls=%async_computation.1 | async-start | bytes 16777216 | tf_op jit(solution)/shard_map/all_to_all | solution.py:74
  47.6 0.0 reduce-scatter.8.cloned.1.call-start
  47.6 94.3 %all-gather.3.cloned.1.call-done = bf16[256,4096]{1,0:T(8,128)(2,1)} async-done(((bf16[256,128]{1,0:T(8,128)(2,1)}), bf16[256,4096]{1,0:T(8,128)(2,1)}) %all-gather.3.cloned.1.call-update) | async-done | bytes 2097168 | tf_op jit(solution)/shard_map/all_gather | solution.py:54
  141.9 4.0 fusion.20
  145.9 0.0 copy-done.1
  145.9 0.4 copy-done.4
  146.3 1.9 multiply_convert_fusion.2
  148.3 0.1 copy-done.3
  148.4 2.6 convolution_convert_fusion.3
  151.0 0.0 reduce-scatter.8.cloned.1.call-update
  151.0 0.2 all-gather.5.cloned.1.call-start
  151.2 0.0 copy-done.10
  151.3 0.1 reshape.130
  151.3 0.0 copy-done.9
  151.3 0.1 copy.22
  151.5 80.2 %reduce-scatter.8.cloned.1.call-done = bf16[8,4096]{1,0:T(8,128)(2,1)} async-done(((bf16[256,4096]{1,0:T(8,128)(2,1)}), bf16[8,4096]{1,0:T(8,128)(2,1)}) %reduce-scatter.8.cloned.1.call-update) | async-done | bytes 65552 | tf_op jit(solution)/shard_map/reduce_scatter | solution.py:58
  231.7 1.0 multiply_reduce_fusion
  232.7 0.9 fusion.16
  233.6 0.0 all-to-all-done
  233.6 13.1 %gather_fusion.1 = bf16[512,4096]{1,0:T(8,128)(2,1)} fusion(bf16[1024,4096]{1,0:T(8,128)(2,1)} %bitcast.6, s32[1024]{0:T(1024)S(1)} %pad_clamp_fusion), kind=kCustom, calls=%fused_computation.1 | custom fusion | bytes 8390656 | tf_op jit(solution)/shard_map/jit(_take)/gather | solution.py:76
  246.7 2.6 broadcast_select_fusion
  249.3 0.0 copy-start
  249.3 2.2 fusion
  251.5 8.5 %fusion.3 = f32[8,1,65]{2,1,0:T(1,128)S(1)} fusion(f32[8,65]{1,0:T(8,128)S(1)} %add_sqrt_fusion, bf16[8,64,4096]{2,1,0:T(8,128)(2,1)S(1)} %broadcast_select_fusion, bf16[8,1,4096]{2,1,0:T(2,128)(2,1)S(1)} %copy.22, f32[8,4096,1]{1,0,2:T(8,128)S(1)} %fusion.16), kind=kOutput, calls=%fused_computation.8 | convolution fusion | flops 36208640 | bytes 4395072 | tf_op jit(solution)/shard_map/qd,qnd->qn/dot_general | solution.py:19
  260.0 0.1 copy.24
  260.2 0.1 multiply_reduce_fusion.1
  260.3 0.1 copy.25
  260.3 7.8 %fusion.2 = f32[8,1,4096]{2,1,0:T(1,128)S(1)} fusion(f32[8,65,1]{1,2,0:T(1,128)S(1)} %copy.25, f32[8,65]{1,0:T(8,128)S(1)} %add_sqrt_fusion, bf16[8,64,4096]{2,1,0:T(8,128)(2,1)} %copy-done, bf16[8,1,4096]{2,1,0:T(2,128)(2,1)S(1)} %copy.22), kind=kOutput, calls=%fused_computation.7 | convolution fusion | flops 36208640 | bytes 4395072 | tf_op jit(solution)/shard_map/qn,qnd->qd/dot_general | solution.py:27
  268.2 0.7 fusion.12
  268.9 0.0 all-gather.5.cloned.1.call-update
  268.9 0.0 reduce-scatter.16.cloned.1.call-start
  269.0 45.4 %all-gather.5.cloned.1.call-done = bf16[256,4096]{1,0:T(8,128)(2,1)} async-done(((bf16[8,4096]{1,0:T(8,128)(2,1)}), bf16[256,4096]{1,0:T(8,128)(2,1)}) %all-gather.5.cloned.1.call-update) | async-done | bytes 2097168 | tf_op jit(solution)/shard_map/all_gather | solution.py:82
  314.3 4.1 multiply_convert_fusion
  318.4 0.0 copy-start.5
  318.5 1.3 fusion.21
  319.8 0.7 copy-done.5
  320.5 2.7 fusion.6
  323.2 4.1 copy.27
  327.3 0.0 reduce-scatter.16.cloned.1.call-update
  327.3 0.0 reduce-scatter.10.cloned.1.call-start
  327.4 2.9 fusion.4
  330.3 0.0 reduce-scatter.10.cloned.1.call-update
  330.3 0.0 reduce-scatter.12.cloned.1.call-start
  330.4 2.9 fusion.5
  333.3 0.0 reduce-scatter.12.cloned.1.call-update
  333.3 0.0 reduce-scatter.14.cloned.1.call-start
  333.4 1.5 copy-done.6
  334.9 3.0 convolution_convert_fusion
  338.0 0.0 reduce-scatter.14.cloned.1.call-update
  338.0 0.5 fusion.17
  338.5 65.1 %reduce-scatter.16.cloned.1.call-done = bf16[128,256]{1,0:T(8,128)(2,1)} async-done(((bf16[4096,256]{1,0:T(8,128)(2,1)}), bf16[128,256]{1,0:T(8,128)(2,1)}) %reduce-scatter.16.cloned.1.call-update) | async-done | bytes 65552
  403.6 1.6 copy.28
  405.2 44.7 %reduce-scatter.10.cloned.1.call-done = bf16[1024,448]{0,1:T(8,128)(2,1)} async-done(((bf16[4096,448]{0,1:T(8,128)(2,1)}), bf16[1024,448]{0,1:T(8,128)(2,1)}) %reduce-scatter.10.cloned.1.call-update) | async-done | bytes 917520 | tf_op jit(solution)/shard_map/reduce_scatter | solution.py:104
  449.9 45.1 %reduce-scatter.12.cloned.1.call-done = bf16[1024,448]{0,1:T(8,128)(2,1)} async-done(((bf16[4096,448]{0,1:T(8,128)(2,1)}), bf16[1024,448]{0,1:T(8,128)(2,1)}) %reduce-scatter.12.cloned.1.call-update) | async-done | bytes 917520 | tf_op jit(solution)/shard_map/reduce_scatter | solution.py:107
  495.1 45.3 %reduce-scatter.14.cloned.1.call-done = bf16[448,1024]{1,0:T(8,128)(2,1)} async-done(((bf16[448,4096]{1,0:T(8,128)(2,1)}), bf16[448,1024]{1,0:T(8,128)(2,1)}) %reduce-scatter.14.cloned.1.call-update) | async-done | bytes 917520 | tf_op jit(solution)/shard_map/reduce_scatter | solution.py:111
  (22 shorter events, 0.1 us)
Async XLA Ops:
  7.2 134.8 %all-gather.3.cloned.1.call-start = ((), (), s32[]{:S(2)}) async-start(), calls=%async_computation.6 | async-start | bytes 2162688 | tf_op jit(solution)/shard_map/all_gather | solution.py:54
  35.6 198.0 %all-to-all-start = ((bf16[128,8,4096]{2,1,0:T(8,128)(2,1)}), bf16[128,8,4096]{2,1,0:T(8,128)(2,1)}, u32[]{:S(2)}, u32[]{:S(2)}) async-start(bf16[128,8,4096]{2,1,0:T(8,128)(2,1)} %fusion.1), calls=%async_computation.1 | async-start | bytes 16777216 | tf_op jit(solution)/shard_map/all_to_all | solution.py:74
  47.6 184.1 %reduce-scatter.8.cloned.1.call-start = ((), (), s32[]{:S(2)}) async-start(), calls=%async_computation.7 | async-start | bytes 2162688 | tf_op jit(solution)/shard_map/reduce_scatter | solution.py:58
  141.9 4.0 copy-start.1
  141.9 4.4 copy-start.4
  146.3 2.0 copy-start.3
  148.3 3.0 copy-start.10
  148.3 3.1 copy-start.9
  148.3 83.4 %copy-start.7 = (bf16[8,4096]{1,0:T(8,128)(2,1)S(1)}, bf16[8,4096]{1,0:T(8,128)(2,1)}, u32[]{:S(2)}) copy-start(bf16[8,4096]{1,0:T(8,128)(2,1)} %param.11) | copy-start | bytes 196612
  151.0 163.3 %all-gather.5.cloned.1.call-start = ((), (), s32[]{:S(2)}) async-start(), calls=%async_computation.8 | async-start | bytes 2162688 | tf_op jit(solution)/shard_map/all_gather | solution.py:82
  249.3 2.2 copy-start
  260.3 7.8 %copy-start.8 = (bf16[8,4096]{1,0:T(8,128)(2,1)S(1)}, bf16[8,4096]{1,0:T(8,128)(2,1)}, u32[]{:S(2)}) copy-start(bf16[8,4096]{1,0:T(8,128)(2,1)} %reduce-scatter.8.cloned.1.call-done) | copy-start | bytes 196612
  268.9 134.7 %reduce-scatter.16.cloned.1.call-start = ((), (), s32[]{:S(2)}) async-start(), calls=%async_computation.12 | async-start | bytes 2162688
  314.3 4.1 copy-start.2
  318.4 2.0 copy-start.5
  327.3 122.6 %reduce-scatter.10.cloned.1.call-start = ((), (), s32[]{:S(2)}) async-start(), calls=%async_computation.9 | async-start | bytes 4587520 | tf_op jit(solution)/shard_map/reduce_scatter | solution.py:104
  330.3 164.7 %reduce-scatter.12.cloned.1.call-start = ((), (), s32[]{:S(2)}) async-start(), calls=%async_computation.10 | async-start | bytes 4587520 | tf_op jit(solution)/shard_map/reduce_scatter | solution.py:107
  333.3 1.6 copy-start.6
  333.3 207.0 %reduce-scatter.14.cloned.1.call-start = ((), (), s32[]{:S(2)}) async-start(), calls=%async_computation.11 | async-start | bytes 4587520 | tf_op jit(solution)/shard_map/reduce_scatter | solution.py:111
Sparse Core Ops, SparseCore 0:
  10.2 131.7 all-gather.2
  151.1 80.5 reduce-scatter.7
  269.1 45.2 all-gather.4
  327.4 76.1 reduce-scatter.15
  406.5 43.4 reduce-scatter.9
  452.8 42.2 reduce-scatter.11
  498.0 42.2 reduce-scatter.13
where the time goes:
time: 548 us; the launch traced here: 547 us
  waiting for transfers between devices  421 us (77%)
  matrix products  41.9 us (8%)
  local copies, waits for them, and re-layouts  40.7 us (7%)
  other arithmetic  17 us (3%)
  between operations  14.3 us (3%)
  starting transfers between devices  12.4 us (2%)
    all_gather x1, waiting for transfers between devices, shards(): whole_input = lax.all_gather(mlp_input, 'fsdp', axis=1, tiled=True)  94.3 us
    reduce_scatter x1, waiting for transfers between devices, shards(): lax.psum_scatter(jnp.dot(hidden, down_weight, preferred_element_type=jnp....  80.2 us
    unnamed x8, waiting for transfers between devices  65.9 us
    all_gather x1, waiting for transfers between devices, shards(): gathered_grad = lax.all_gather(head_grad, 'fsdp', axis=0, tiled=True)  45.4 us
    reduce_scatter x1, waiting for transfers between devices, shards(): lax.psum_scatter(down_term.astype(jnp.bfloat16), 'dp', scatter_dimension=...  45.3 us
    reduce_scatter x1, waiting for transfers between devices, shards(): lax.psum_scatter(up_term.astype(jnp.bfloat16), 'dp', scatter_dimension=0,...  45.1 us
    reduce_scatter x1, waiting for transfers between devices, shards(): lax.psum_scatter(gate_term.astype(jnp.bfloat16), 'dp', scatter_dimension=...  44.7 us
    gather x1, local copies, waits for them, and re-layouts, shards(): jnp.take(span_index, row_table.reshape(-1), axis=0)  17.8 us
  transfers between devices with their start and end apart: 8, of which 7 were waited for; matrix products, arithmetic and copies ran while one was open for 9% of the time, Pallas kernels for 0%

commit v1 on v0

v1 whole, which is shorter than its diff:
```python
import jax
import jax.numpy as jnp
from jax import lax
from jax.sharding import PartitionSpec as P

inverse_temp = 50.0
eps = 1e-06
contract_first = (((0,), (0,)), ((), ()))
contract_last = (((1,), (1,)), ((), ()))


def split3(v):
    hi = lax.reduce_precision(v, 8, 7)
    mid = lax.reduce_precision(v - hi, 8, 7)
    return jnp.concatenate([hi, mid, v - hi - mid], axis=0).astype(jnp.bfloat16)


def contrast(top_state, positive_keys, buffer, negative_slots):
    rows = top_state.shape[0]
    slots = buffer.shape[0]
    row_norm = jnp.sqrt(jnp.sum(top_state * top_state, axis=-1) + eps)
    unit_rows = top_state / row_norm[:, None]
    positive = positive_keys.astype(jnp.float32)
    positive_unit = positive / jnp.sqrt(jnp.sum(positive * positive, axis=-1, keepdims=True) + eps)
    positive_score = inverse_temp * jnp.sum(unit_rows * positive_unit, axis=-1)

    wide = buffer.astype(jnp.float32)
    key_scale = lax.rsqrt(jnp.sum(wide * wide, axis=-1) + eps)
    raw = lax.dot_general(
        split3(unit_rows), buffer, contract_last, preferred_element_type=jnp.float32
    )
    raw = raw[:rows] + raw[rows : 2 * rows] + raw[2 * rows :]
    scores = inverse_temp * raw * key_scale[None, :]
    slot_ids = lax.broadcasted_iota(jnp.int32, (1, 1, slots), 2)
    uses = jnp.sum((negative_slots[:, :, None] == slot_ids).astype(jnp.float32), axis=1)
    weights = jnp.where(uses > 0, uses * jnp.exp(scores), 0.0)
    positive_weight = jnp.exp(positive_score)
    exp_total = jnp.sum(weights, axis=-1) + positive_weight
    query_loss = jnp.log(exp_total) - positive_score
    coeffs = weights / exp_total[:, None]
    positive_coeff = positive_weight / exp_total - 1.0
    pull = lax.dot_general(
        split3(coeffs * key_scale[None, :]),
        buffer,
        (((1,), (0,)), ((), ())),
        preferred_element_type=jnp.float32,
    )
    pull = pull[:rows] + pull[rows : 2 * rows] + pull[2 * rows :]
    pull = inverse_temp * (pull + positive_coeff[:, None] * positive_unit)
    inner = jnp.sum(coeffs * scores, axis=-1) + positive_coeff * positive_score
    head_grad = ((pull - inner[:, None] * unit_rows) / row_norm[:, None]).astype(jnp.bfloat16)
    return query_loss, head_grad


def shards(
    mlp_input,
    residual_in,
    gate_weight,
    up_weight,
    down_weight,
    span_index,
    positive_keys,
    request_rows,
    request_counts,
    negative_slots,
):
    owners = lax.axis_size("dp") * lax.axis_size("fsdp")
    slot_cap = request_rows.shape[2]
    width = span_index.shape[1]

    row_table = request_rows[:, 0, :]
    live = lax.broadcasted_iota(jnp.int32, row_table.shape, 1) < request_counts
    wanted = jnp.where(live, row_table, -1).reshape(-1)
    pick = (wanted[:, None] == lax.broadcasted_iota(jnp.int32, (1, span_index.shape[0]), 1)).astype(
        jnp.bfloat16
    )
    picked = jnp.dot(pick, span_index, preferred_element_type=jnp.bfloat16)
    buffer = lax.all_to_all(
        picked.reshape(owners, slot_cap, width),
        ("dp", "fsdp"),
        split_axis=0,
        concat_axis=0,
        tiled=True,
    ).reshape(owners * slot_cap, width)

    whole_input = lax.all_gather(mlp_input, "fsdp", axis=1, tiled=True)
    gate_act = jnp.dot(whole_input, gate_weight, preferred_element_type=jnp.float32)
    up_act = jnp.dot(whole_input, up_weight, preferred_element_type=jnp.float32)
    sigmoid_gate = jax.nn.sigmoid(gate_act)
    silu_gate = gate_act * sigmoid_gate
    hidden = (silu_gate * up_act).astype(jnp.bfloat16)
    branch = lax.psum_scatter(
        jnp.dot(hidden, down_weight, preferred_element_type=jnp.float32).astype(jnp.bfloat16),
        "fsdp",
        scatter_dimension=0,
        tiled=True,
    ).astype(jnp.float32)
    top_state = branch + residual_in.astype(jnp.float32)
    all_hidden = lax.all_gather(hidden, "dp", axis=0, tiled=True)
    input_cols = lax.all_to_all(whole_input, "dp", split_axis=1, concat_axis=0, tiled=True)

    query_loss, head_grad = contrast(top_state, positive_keys, buffer, negative_slots)

    gathered_grad = lax.all_gather(head_grad, "fsdp", axis=0, tiled=True)
    hidden_grad = lax.dot_general(
        gathered_grad, down_weight, contract_last, preferred_element_type=jnp.float32
    )
    silu_slope = sigmoid_gate * (1.0 + gate_act * (1.0 - sigmoid_gate))
    gate_grad_act = (hidden_grad * up_act * silu_slope).astype(jnp.bfloat16)
    up_grad_act = (hidden_grad * silu_gate).astype(jnp.bfloat16)
    both_acts = lax.all_gather(
        jnp.concatenate([gate_grad_act, up_grad_act], axis=1), "dp", axis=0, tiled=True
    )
    input_term = lax.dot_general(
        gate_grad_act, gate_weight, contract_last, preferred_element_type=jnp.float32
    ) + lax.dot_general(up_grad_act, up_weight, contract_last, preferred_element_type=jnp.float32)
    input_grad = lax.psum_scatter(
        input_term.astype(jnp.bfloat16), "fsdp", scatter_dimension=1, tiled=True
    )
    head_cols = lax.all_to_all(gathered_grad, "dp", split_axis=1, concat_axis=0, tiled=True)
    down_grad = lax.dot_general(
        all_hidden, head_cols, contract_first, preferred_element_type=jnp.float32
    ).astype(jnp.bfloat16)
    units = gate_weight.shape[1]
    gate_grad = lax.dot_general(
        input_cols, both_acts[:, :units], contract_first, preferred_element_type=jnp.float32
    ).astype(jnp.bfloat16)
    up_grad = lax.dot_general(
        input_cols, both_acts[:, units:], contract_first, preferred_element_type=jnp.float32
    ).astype(jnp.bfloat16)
    return (query_loss, input_grad, gate_grad, up_grad, down_grad)


def solution(mesh):
    return jax.shard_map(
        shards,
        mesh=mesh,
        in_specs=(
            P("dp", "fsdp"),
            P(("dp", "fsdp"), None),
            P(None, "fsdp"),
            P(None, "fsdp"),
            P("fsdp", None),
            P(("dp", "fsdp"), None),
            P(("dp", "fsdp"), None),
            P(None, ("dp", "fsdp"), None),
            P(None, ("dp", "fsdp")),
            P(("dp", "fsdp"), None),
        ),
        out_specs=(
            P(("dp", "fsdp")),
            P("dp", "fsdp"),
            P("dp", "fsdp"),
            P("dp", "fsdp"),
            P("fsdp", "dp"),
        ),
        check_vma=False,
    )
```

time: 548 us -> 432 us (0.79)
  waiting for transfers between devices: 421 us -> 293 us
  blocking collectives: 0 us -> 32.2 us
  local copies, waits for them, and re-layouts: 40.7 us -> 12.9 us
  starting transfers between devices: 12.4 us -> 21.3 us
  other arithmetic: 17 us -> 11 us
    reduce_scatter x3 -> x0, waiting for transfers between devices: 135 us -> none  [the longest x1 45.3 us: shards(): lax.psum_scatter(down_term.astype(jnp.bfloat16), 'dp', scatter_dimension=...]
    all_gather x0 -> x1, blocking collectives: none -> 32.2 us  [shards(): all_hidden = lax.all_gather(hidden, 'dp', axis=0, tiled=True)]
    gather x2 -> x0, local copies, waits for them, and re-layouts: 30.9 us -> none  [the longest x1 17.8 us: shards(): jnp.take(span_index, row_table.reshape(-1), axis=0)]
    unnamed x8 -> x6, waiting for transfers between devices: 65.9 us -> 39.4 us
    all_to_all x1 -> x3, waiting for transfers between devices: 0.01 us -> 25.5 us  [the longest x1 25.5 us: shards(): lax.all_to_all(whole_input, 'dp', split_axis=1, concat_axis=0, tiled=True)]
    all_gather x1, waiting for transfers between devices: 94.3 us -> 107 us  [shards(): whole_input = lax.all_gather(mlp_input, 'fsdp', axis=1, tiled=True)]
    select_n x4 -> x1, other arithmetic: 10 us -> 0.01 us  [shards(): wanted = jnp.where(live, row_table, -1).reshape(-1)]
    all_to_all x1 -> x3, starting transfers between devices: 11.9 us -> 20.9 us  [the longest x1 12 us: shards(): lax.all_to_all(picked.reshape(owners, slot_cap, width), ('dp', 'fsdp'), s...]
  transfers between devices with their start and end apart: 8 -> 8, of which waited for: 7 -> 5; matrix products, arithmetic and copies ran while one was open for 9% -> 11% of each run, Pallas kernels for 0% -> 0%
where the time goes in v1:
time: 432 us; the launch traced here: 431 us
  waiting for transfers between devices  293 us (68%)
  matrix products  46.6 us (11%)
  blocking collectives  32.2 us (7%)
  starting transfers between devices  21.3 us (5%)
  between operations  14 us (3%)
  local copies, waits for them, and re-layouts  12.9 us (3%)
  other arithmetic  11 us (3%)
    all_gather x1, waiting for transfers between devices, shards(): whole_input = lax.all_gather(mlp_input, 'fsdp', axis=1, tiled=True)  107 us
    reduce_scatter x1, waiting for transfers between devices, shards(): lax.psum_scatter(jnp.dot(hidden, down_weight, preferred_element_type=jnp....  75.2 us
    all_gather x1, waiting for transfers between devices, shards(): gathered_grad = lax.all_gather(head_grad, 'fsdp', axis=0, tiled=True)  45.1 us
    unnamed x6, waiting for transfers between devices  39.4 us
    all_gather x1, blocking collectives, shards(): all_hidden = lax.all_gather(hidden, 'dp', axis=0, tiled=True)  32.2 us
    all_to_all x1, waiting for transfers between devices, shards(): lax.all_to_all(whole_input, 'dp', split_axis=1, concat_axis=0, tiled=True)  25.5 us
    all_to_all x1, starting transfers between devices, shards(): lax.all_to_all(picked.reshape(owners, slot_cap, width), ('dp', 'fsdp'), s...  12 us
    dot_general x1, matrix products, shards(): picked = jnp.dot(pick, span_index, preferred_element_type=jnp.bfloat16)  9.02 us
  transfers between devices with their start and end apart: 8, of which 5 were waited for; matrix products, arithmetic and copies ran while one was open for 11% of the time, Pallas kernels for 0%

profile of v1, /device:TPU:1, one launch (start us, length us, event | category | flops | bytes accessed | tf_op | source)
XLA Modules:
  0.0 430.7 jit_solution(6093604471115959801)
XLA Ops:
  7.2 0.0 all-gather.4.cloned.1.call-start
  7.2 1.6 copy.25
  8.8 0.0 all-gather.4.cloned.1.call-update
  8.8 0.7 iota_compare_fusion.3
  9.6 0.1 lt.20
  9.7 0.8 copy.26
  10.4 0.1 squeeze.3
  10.6 9.0 %convolution_bitcast_fusion = bf16[128,8,4096]{2,1,0:T(8,128)(2,1)} fusion(bf16[512,4096]{1,0:T(8,128)(2,1)} %param.15, s32[1024]{0:T(1024)S(1)} %broadcast_select_fusion), kind=kOutput, calls=%fused_computation.5 | convolution fusion | flops 4295491584 | bytes 12587008 | tf_op jit(solution)/shard_map/dot_general | solution.py:77
  19.6 12.0 %all-to-all-start = ((bf16[128,8,4096]{2,1,0:T(8,128)(2,1)}), bf16[128,8,4096]{2,1,0:T(8,128)(2,1)}, u32[]{:S(2)}, u32[]{:S(2)}) async-start(bf16[128,8,4096]{2,1,0:T(8,128)(2,1)} %convolution_bitcast_fusion), calls=%async_computation.1 | async-start | bytes 16777216 | tf_op jit(solution)/shard_map/all_to_all | solution.py:78
  31.5 0.0 reduce-scatter.5.cloned.1.call-start
  31.6 107.5 %all-gather.4.cloned.1.call-done = bf16[256,4096]{0,1:T(8,128)(2,1)} async-done(((bf16[256,128]{0,1:T(8,128)(2,1)}), bf16[256,4096]{0,1:T(8,128)(2,1)}) %all-gather.4.cloned.1.call-update) | async-done | bytes 2097168 | tf_op jit(solution)/shard_map/all_gather | solution.py:86
  139.1 4.0 fusion.36
  143.0 0.0 copy-done.1
  143.0 0.0 copy-start
  143.1 2.9 multiply_convert_fusion.2
  146.0 0.0 copy-done
  146.0 0.0 copy-start.4
  146.0 0.0 copy-start.6
  146.0 0.0 copy-start.3
  146.0 2.6 convolution_convert_fusion
  148.6 0.0 reduce-scatter.5.cloned.1.call-update
  148.6 0.0 all-gather.6.cloned.1.call-start
  148.7 0.0 copy-done.4
  148.7 0.1 fusion.16
  148.9 0.0 copy-done.6
  148.9 0.4 convert_reduce_fusion
  149.3 75.2 %reduce-scatter.5.cloned.1.call-done = bf16[8,4096]{1,0:T(8,128)(2,1)} async-done(((bf16[256,4096]{1,0:T(8,128)(2,1)}), bf16[8,4096]{1,0:T(8,128)(2,1)}) %reduce-scatter.5.cloned.1.call-update) | async-done | bytes 65552 | tf_op jit(solution)/shard_map/reduce_scatter | solution.py:92
  224.5 0.0 copy-done.3
  224.5 1.0 multiply_reduce_fusion.2
  225.5 1.1 reduce-precision_convert_fusion.1
  226.6 0.0 all-to-all-done
  226.6 5.1 %multiply_reduce_fusion = f32[128,8]{1,0:T(8,128)S(1)} fusion(bf16[128,8,4096]{2,1,0:T(8,128)(2,1)} %all-to-all-done), kind=kLoop, calls=%fused_computation | loop fusion | flops 12581888 | bytes 8392704 | tf_op jit(solution)/shard_map/reduce_sum | solution.py:28
  231.7 0.1 rsqrt.11
  231.8 5.7 %fusion.2 = f32[24,1024]{1,0:T(8,128)S(1)} fusion(bf16[128,8,4096]{2,1,0:T(8,128)(2,1)} %all-to-all-done, bf16[8,4096]{1,0:T(8,128)(2,1)S(1)} %get-tuple-element.16, bf16[8,4096]{1,0:T(8,128)(2,1)S(1)} %get-tuple-element.14, bf16[8,4096]{1,0:T(8,128)(2,1)S(1)} %get-tuple-element.13), kind=kOutput, calls=%fused_computation.3 | convolution fusion | flops 201916416 | bytes 8683520 | tf_op jit(solution)/shard_map/dot_general | solution.py:29
  237.5 0.1 fusion.31
  237.6 0.2 multiply_reduce_fusion.3
  237.8 0.5 multiply_add_fusion
  238.4 0.0 copy-start.5
  238.4 4.6 %fusion = f32[24,4096]{1,0:T(8,128)S(1)} fusion(bf16[128,8,4096]{2,1,0:T(8,128)(2,1)} %all-to-all-done, bf16[8,1024]{1,0:T(8,128)(2,1)S(1)} %get-tuple-element.19, bf16[8,1024]{1,0:T(8,128)(2,1)S(1)} %get-tuple-element.18, bf16[8,1024]{1,0:T(8,128)(2,1)S(1)} %get-tuple-element.17), kind=kOutput, calls=%fused_computation.1 | convolution fusion | flops 201474048 | bytes 8830976 | tf_op jit(solution)/shard_map/dot_general | solution.py:42
  243.0 0.8 fusion.22
  243.8 0.0 all-gather.6.cloned.1.call-update
  243.8 0.2 all-gather.8.cloned.1.call-start
  244.0 45.1 %all-gather.6.cloned.1.call-done = bf16[256,4096]{1,0:T(8,128)(2,1)} async-done(((bf16[8,4096]{1,0:T(8,128)(2,1)}), bf16[256,4096]{1,0:T(8,128)(2,1)}) %all-gather.6.cloned.1.call-update) | async-done | bytes 2097168 | tf_op jit(solution)/shard_map/all_gather | solution.py:104
  289.2 3.9 multiply_convert_fusion
  293.0 0.8 pad_maximum_fusion
  293.8 0.0 all-gather.8.cloned.1.call-update
  293.9 4.5 %all-to-all-start.1 = ((bf16[256,4,1024]{0,2,1:T(8,128)(2,1)}), bf16[256,4,1024]{0,2,1:T(8,128)(2,1)}, u32[]{:S(2)}, u32[]{:S(2)}) async-start(bf16[256,4,1024]{0,2,1:T(8,128)(2,1)} %bitcast.3), calls=%async_computation.2 | async-start | bytes 4194304 | tf_op jit(solution)/shard_map/all_to_all | solution.py:100
  298.3 0.0 reduce-scatter.7.cloned.1.call-start
  298.4 0.0 copy-start.2
  298.4 3.5 fusion.35
  301.9 1.4 fusion.4
  303.3 2.5 copy.29
  305.8 0.0 reduce-scatter.7.cloned.1.call-update
  305.8 3.2 copy.33
  308.9 25.5 %all-to-all-done.1 = bf16[256,4,1024]{0,2,1:T(8,128)(2,1)} async-done(((bf16[256,4,1024]{0,2,1:T(8,128)(2,1)}), bf16[256,4,1024]{0,2,1:T(8,128)(2,1)}, u32[]{:S(2)}, u32[]{:S(2)}) %all-to-all-start.1) | async-done | bytes 2097184 | tf_op jit(solution)/shard_map/all_to_all | solution.py:100
  334.4 4.5 %all-to-all-start.2 = ((bf16[256,4,1024]{2,0,1:T(8,128)(2,1)}), bf16[256,4,1024]{2,0,1:T(8,128)(2,1)}, u32[]{:S(2)}, u32[]{:S(2)}) async-start(bf16[256,4,1024]{2,0,1:T(8,128)(2,1)} %bitcast.42), calls=%async_computation.3 | async-start | bytes 4194304 | tf_op jit(solution)/shard_map/all_to_all | solution.py:120
  338.9 32.2 %all_gather.15 = bf16[1024,448]{0,1:T(8,128)(2,1)S(1)} all-gather(bf16[256,448]{0,1:T(8,128)(2,1)S(1)} %get-tuple-element.21), channel_id=1, replica_groups=mesh['dp'=4,'fsdp'=32] {'dp'}, dimensions={0}, use_global_device_ids=true | all-gather | bytes 1146880 | tf_op jit(solution)/shard_map/all_gather | solution.py:99
  371.2 3.0 copy.27
  374.2 0.0 all-to-all-done.2
  374.2 3.7 convolution_convert_fusion.1
  377.9 3.4 fusion.5
  381.2 2.1 fusion.6
  383.3 39.3 %reduce-scatter.7.cloned.1.call-done = bf16[128,256]{1,0:T(8,128)(2,1)} async-done(((bf16[4096,256]{1,0:T(8,128)(2,1)}), bf16[128,256]{1,0:T(8,128)(2,1)}) %reduce-scatter.7.cloned.1.call-update) | async-done | bytes 65552
  422.6 1.6 copy.30
  (13 shorter events, 0.1 us)
Async XLA Ops:
  7.2 131.9 %all-gather.4.cloned.1.call-start = ((), (), s32[]{:S(2)}) async-start(), calls=%async_computation.5 | async-start | bytes 2162688 | tf_op jit(solution)/shard_map/all_gather | solution.py:86
  19.6 207.0 %all-to-all-start = ((bf16[128,8,4096]{2,1,0:T(8,128)(2,1)}), bf16[128,8,4096]{2,1,0:T(8,128)(2,1)}, u32[]{:S(2)}, u32[]{:S(2)}) async-start(bf16[128,8,4096]{2,1,0:T(8,128)(2,1)} %convolution_bitcast_fusion), calls=%async_computation.1 | async-start | bytes 16777216 | tf_op jit(solution)/shard_map/all_to_all | solution.py:78
  31.5 193.0 %reduce-scatter.5.cloned.1.call-start = ((), (), s32[]{:S(2)}) async-start(), calls=%async_computation.6 | async-start | bytes 2162688 | tf_op jit(solution)/shard_map/reduce_scatter | solution.py:92
  139.1 4.0 copy-start.1
  143.0 2.9 copy-start
  146.0 2.7 copy-start.4
  146.0 2.9 copy-start.6
  146.0 78.5 %copy-start.3 = (bf16[8,4096]{1,0:T(8,128)(2,1)S(1)}, bf16[8,4096]{1,0:T(8,128)(2,1)}, u32[]{:S(2)}) copy-start(bf16[8,4096]{1,0:T(8,128)(2,1)} %param.11) | copy-start | bytes 196612
  148.6 140.5 %all-gather.6.cloned.1.call-start = ((), (), s32[]{:S(2)}) async-start(), calls=%async_computation.7 | async-start | bytes 2162688 | tf_op jit(solution)/shard_map/all_gather | solution.py:104
  238.4 4.6 %copy-start.5 = (bf16[8,4096]{1,0:T(8,128)(2,1)S(1)}, bf16[8,4096]{1,0:T(8,128)(2,1)}, u32[]{:S(2)}) copy-start(bf16[8,4096]{1,0:T(8,128)(2,1)} %reduce-scatter.5.cloned.1.call-done) | copy-start | bytes 196612
  243.8 134.1 %all-gather.8.cloned.1.call-start = ((), (), s32[]{:S(2)}) async-start(), calls=%async_computation.8 | async-start | bytes 2293760 | tf_op jit(solution)/shard_map/all_gather | solution.py:111
  293.9 40.6 %all-to-all-start.1 = ((bf16[256,4,1024]{0,2,1:T(8,128)(2,1)}), bf16[256,4,1024]{0,2,1:T(8,128)(2,1)}, u32[]{:S(2)}, u32[]{:S(2)}) async-start(bf16[256,4,1024]{0,2,1:T(8,128)(2,1)} %bitcast.3), calls=%async_computation.2 | async-start | bytes 4194304 | tf_op jit(solution)/shard_map/all_to_all | solution.py:100
  298.3 124.3 %reduce-scatter.7.cloned.1.call-start = ((), (), s32[]{:S(2)}) async-start(), calls=%async_computation.9 | async-start | bytes 2162688
  298.4 3.5 copy-start.2
  334.4 39.7 %all-to-all-start.2 = ((bf16[256,4,1024]{2,0,1:T(8,128)(2,1)}), bf16[256,4,1024]{2,0,1:T(8,128)(2,1)}, u32[]{:S(2)}, u32[]{:S(2)}) async-start(bf16[256,4,1024]{2,0,1:T(8,128)(2,1)} %bitcast.42), calls=%async_computation.3 | async-start | bytes 4194304 | tf_op jit(solution)/shard_map/all_to_all | solution.py:120
  377.9 3.4 copy-start.7
Sparse Core Ops, SparseCore 0:
  10.8 128.1 all-gather.3
  148.8 75.7 reduce-scatter.4
  243.9 45.2 all-gather.5
  294.0 46.0 all-gather.7
  343.5 79.0 reduce-scatter.6

commit v2 on v1

--- a/solution.py
+++ b/solution.py
@@ -1,12 +1,378 @@
+import functools
+
 import jax
 import jax.numpy as jnp
 from jax import lax
+from jax.experimental import pallas as pl
+from jax.experimental.pallas import tpu as pltpu
 from jax.sharding import PartitionSpec as P
 
 inverse_temp = 50.0
 eps = 1e-06
 contract_first = (((0,), (0,)), ((), ()))
 contract_last = (((1,), (1,)), ((), ()))
+ANY = pl.BlockSpec(memory_space=pl.ANY)
+VMEM = pl.BlockSpec(memory_space=pltpu.VMEM)
+DMA = pltpu.SemaphoreType.DMA
+near_first = (1, 3, 2)
+
+
+class Place:
+    def __init__(self):
+        self.x = lax.axis_index("dp")
+        self.f = lax.axis_index("fsdp")
+        self.z = self.f // 8
+        self.y = (self.f // 2) % 4
+        self.c = self.f % 2
+        self.a = self.y * (1 - self.c) + self.z * self.c
+        self.b = self.z * (1 - self.c) + self.y * self.c
+        self.partner = self.f + 1 - 2 * self.c
+
+    def at(self, b, a, c):
+        z = b * (1 - c) + a * c
+        y = a * (1 - c) + b * c
+        return (z * 4 + y) * 2 + c
+
+    def a_peer(self, j):
+        return self.at(self.b, (self.a + j) % 4, self.c)
+
+    def b_peer(self, j):
+        return self.at((self.b + j) % 4, self.a, self.c)
+
+
+def copy_to(src, dst, send, recv, x, f):
+    return pltpu.make_async_remote_copy(
+        src_ref=src,
+        dst_ref=dst,
+        send_sem=send,
+        recv_sem=recv,
+        device_id=(x, f),
+        device_id_type=pl.DeviceIdType.MESH,
+    )
+
+
+def meet(place, across):
+    barrier = pltpu.get_barrier_semaphore()
+    peers = [(place.x, place.partner)]
+    peers += [(place.x, place.a_peer(j)) for j in near_first]
+    peers += [(place.x, place.b_peer(j)) for j in near_first]
+    if across:
+        peers += [((place.x + j) % 4, place.f) for j in near_first]
+    for x, f in peers:
+        pl.semaphore_signal(barrier, inc=1, device_id=(x, f), device_id_type=pl.DeviceIdType.MESH)
+    pl.semaphore_wait(barrier, len(peers))
+
+
+class PlaneGather:
+    copies = 32
+
+    def __init__(self, place, src, out, view, send, recv):
+        self.place, self.src, self.out, self.view = place, src, out, view
+        self.send, self.recv = send, recv
+        self.sent = []
+
+    def push(self, ref, origin, f):
+        copy = copy_to(
+            ref,
+            self.view(self.out, origin),
+            self.send.at[len(self.sent)],
+            self.recv.at[origin],
+            self.place.x,
+            f,
+        )
+        copy.start()
+        self.sent.append(copy)
+
+    def arrive(self, origin):
+        block = self.view(self.out, origin)
+        copy_to(
+            block, block, self.send.at[31], self.recv.at[origin], self.place.x, self.place.partner
+        ).wait_recv()
+        return block
+
+    def start(self):
+        p = self.place
+        self.own = pltpu.make_async_copy(self.src, self.view(self.out, p.f), self.send.at[31])
+        for j in near_first:
+            self.push(self.src, p.f, p.a_peer(j))
+        for j in near_first:
+            self.push(self.src, p.f, p.b_peer(j))
+        self.push(self.src, p.f, p.partner)
+        self.own.start()
+
+    def relay(self):
+        p = self.place
+        for j in near_first:
+            origin = p.a_peer(j)
+            block = self.arrive(origin)
+            for i in near_first:
+                self.push(block, origin, p.b_peer(i))
+            self.push(block, origin, p.partner)
+
+    def finish(self):
+        p = self.place
+        for j in (0,) + near_first:
+            for i in near_first:
+                origin = p.at((p.b + i) % 4, (p.a + j) % 4, p.c)
+                self.push(self.arrive(origin), origin, p.partner)
+        for j in (0,) + near_first:
+            for i in (0,) + near_first:
+                z, y = (p.z + i) % 4, (p.y + j) % 4
+                self.arrive((z * 4 + y) * 2 + 1 - p.c)
+        self.own.wait()
+        for copy in self.sent:
+            copy.wait_send()
+
+
+class PlaneScatter:
+    def __init__(self, place, src, view, scratch):
+        self.place, self.src, self.view = place, src, view
+        (self.got1, self.sum1, self.got2, self.sum2, self.got3, self.send1, self.recv1,
+         self.send2, self.recv2, self.send3, self.recv3) = scratch
+
+    @staticmethod
+    def scratch(block):
+        wide = lambda *lead: pltpu.VMEM(lead + block, jnp.bfloat16)
+        return [wide(16), wide(4, 4), wide(4, 4), wide(4), wide(4), DMA((16,)), DMA((16,)),
+                DMA((4,)), DMA((4,)), DMA((4,)), DMA((4,))]
+
+    def start(self):
+        p = self.place
+        self.sent1 = []
+        for i in (2, 1, 3, 0):
+            for a in range(4):
+                b = (p.a + i) % 4
+                k = b * 4 + a
+                copy = copy_to(
+                    self.view(self.src, p.at(b, a, 1 - p.c)),
+                    self.got1.at[k],
+                    self.send1.at[k],
+                    self.recv1.at[k],
+                    p.x,
+                    p.partner,
+                )
+                copy.start()
+                self.sent1.append(copy)
+
+    def middle(self):
+        p = self.place
+        sent2 = []
+        for i in (2, 1, 3, 0):
+            b = (p.b + i) % 4
+            for a in range(4):
+                k = b * 4 + a
+                copy_to(
+                    self.got1.at[k], self.got1.at[k], self.send1.at[k], self.recv1.at[k],
+                    p.x, p.partner,
+                ).wait_recv()
+                own = self.view(self.src, p.at(b, a, p.c))[...].astype(jnp.float32)
+                self.sum1[b, a] = (own + self.got1[k].astype(jnp.float32)).astype(jnp.bfloat16)
+            if i:
+                copy = copy_to(
+                    self.sum1.at[b], self.got2.at[p.b], self.send2.at[i], self.recv2.at[p.b],
+                    p.x, p.b_peer(i),
+                )
+                copy.start()
+                sent2.append(copy)
+        for i in near_first:
+            b = (p.b + i) % 4
+            copy_to(
+                self.got2.at[b], self.got2.at[b], self.send2.at[i], self.recv2.at[b],
+                p.x, p.b_peer(i),
+            ).wait_recv()
+        sent3 = []
+        for j in (2, 1, 3, 0):
+            a = (p.a + j) % 4
+            total = self.sum1[p.b, a].astype(jnp.float32)
+            for i in near_first:
+                total += self.got2[(p.b + i) % 4, a].astype(jnp.float32)
+            if j:
+                self.sum2[a] = total.astype(jnp.bfloat16)
+                copy = copy_to(
+                    self.sum2.at[a], self.got3.at[p.a], self.send3.at[j], self.recv3.at[p.a],
+                    p.x, p.a_peer(j),
+                )
+                copy.start()
+                sent3.append(copy)
+        for j in near_first:
+            a = (p.a + j) % 4
+            copy_to(
+                self.got3.at[a], self.got3.at[a], self.send3.at[j], self.recv3.at[a],
+                p.x, p.a_peer(j),
+            ).wait_recv()
+            total += self.got3[a].astype(jnp.float32)
+        for copy in self.sent1 + sent2 + sent3:
+            copy.wait_send()
+        return total
+
+
+def across_gather(place, src, out, send, recv):
+    own = pltpu.make_async_copy(src, out.at[place.x], send.at[0])
+    own.start()
+    sent = []
+    for j in near_first:
+        copy = copy_to(src, out.at[place.x], send.at[j], recv.at[place.x], (place.x + j) % 4, place.f)
+        copy.start()
+        sent.append(copy)
+
+    def finish():
+        for j in near_first:
+            x = (place.x + j) % 4
+            copy_to(out.at[x], out.at[x], send.at[j], recv.at[x], x, place.f).wait_recv()
+        own.wait()
+        for copy in sent:
+            copy.wait_send()
+
+    return finish
+
+
+def params(collective_id):
+    return pltpu.CompilerParams(
+        collective_id=collective_id, has_side_effects=True, vmem_limit_bytes=40 * 1024 * 1024
+    )
+
+
+def column_block(ref, f):
+    return ref.at[:, pl.ds(pl.multiple_of(f * 128, 128), 128)]
+
+
+def row_block(ref, f):
+    return ref.at[f]
+
+
+def gather_input(mlp_input):
+    def kernel(src, out, send, recv):
+        place = Place()
+        meet(place, False)
+        gather = PlaneGather(place, src, out, column_block, send, recv)
+        gather.start()
+        gather.relay()
+        gather.finish()
+
+    rows, cols = mlp_input.shape
+    return pl.pallas_call(
+        kernel,
+        out_shape=jax.ShapeDtypeStruct((rows, cols * 32), jnp.bfloat16),
+        in_specs=[ANY],
+        out_specs=ANY,
+        scratch_shapes=[DMA((32,)), DMA((32,))],
+        compiler_params=params(0),
+        name="gather_input",
+    )(mlp_input)
+
+
+def scatter_branch(partial):
+    def kernel(src, out, *scratch):
+        place = Place()
+        meet(place, False)
+        scatter = PlaneScatter(place, src, row_block, scratch)
+        scatter.start()
+        out[...] = scatter.middle()
+
+    return pl.pallas_call(
+        kernel,
+        out_shape=jax.ShapeDtypeStruct((8, 4096), jnp.float32),
+        in_specs=[VMEM],
+        out_specs=VMEM,
+        scratch_shapes=PlaneScatter.scratch((8, 4096)),
+        compiler_params=params(1),
+        name="scatter_branch",
+    )(partial.reshape(32, 8, 4096))
+
+
+def gather_head(head_grad, hidden, whole_input):
+    def kernel(head, hid, inp, out, head_x, hid_x, inp_x, send, recv, hx_send, hx_recv,
+               h_send, h_recv, i_send, i_recv, pair_send, pair_recv):
+        place = Place()
+        p = place
+        meet(place, True)
+        gather = PlaneGather(place, head, out, row_block, send, recv)
+        gather.start()
+        wide = lambda x: pl.ds(pl.multiple_of(x * 1024, 1024), 1024)
+        half = lambda c: pl.ds(pl.multiple_of(c * 512, 512), 512)
+        own_h = pltpu.make_async_copy(head.at[:, wide(p.x)], head_x.at[p.x], hx_send.at[0])
+        own_h.start()
+        own_i = pltpu.make_async_copy(inp.at[:, wide(p.x)], inp_x.at[p.x], i_send.at[0])
+        own_i.start()
+        sent = []
+        for j in near_first:
+            x = (p.x + j) % 4
+            copy = copy_to(head.at[:, wide(x)], head_x.at[p.x], hx_send.at[j], hx_recv.at[p.x], x, p.f)
+            copy.start()
+            sent.append(copy)
+        finish_hidden = across_gather(place, hid, hid_x, h_send, h_recv)
+        for j in near_first:
+            x = (p.x + j) % 4
+            copy = copy_to(
+                inp.at[:, pl.ds(pl.multiple_of(x * 1024 + p.c * 512, 512), 512)],
+                inp_x.at[p.x, :, half(p.c)], i_send.at[j], i_recv.at[p.x], x, p.f,
+            )
+            copy.start()
+            sent.append(copy)
+        gather.relay()
+        gather.finish()
+        for j in near_first:
+            x = (p.x + j) % 4
+            copy_to(
+                head_x.at[x], head_x.at[x], hx_send.at[j], hx_recv.at[x], x, p.f
+            ).wait_recv()
+        for j in near_first:
+            x = (p.x + j) % 4
+            region = inp_x.at[x, :, half(p.c)]
+            copy_to(region, region, i_send.at[j], i_recv.at[x], x, p.f).wait_recv()
+            copy = copy_to(region, region, pair_send.at[j], pair_recv.at[x], p.x, p.partner)
+            copy.start()
+            sent.append(copy)
+        for j in near_first:
+            x = (p.x + j) % 4
+            region = inp_x.at[x, :, half(1 - p.c)]
+            copy_to(region, region, pair_send.at[j], pair_recv.at[x], p.x, p.partner).wait_recv()
+        finish_hidden()
+        own_h.wait()
+        own_i.wait()
+        for copy in sent:
+            copy.wait_send()
+
+    bf = lambda *shape: jax.ShapeDtypeStruct(shape, jnp.bfloat16)
+    out, head_x, hid_x, inp_x = pl.pallas_call(
+        kernel,
+        out_shape=(bf(32, 8, 4096), bf(4, 8, 1024), bf(4, *hidden.shape), bf(4, 256, 1024)),
+        in_specs=[ANY] * 3,
+        out_specs=[ANY] * 4,
+        scratch_shapes=[DMA((32,)), DMA((32,))] + [DMA((4,))] * 8,
+        compiler_params=params(2),
+        name="gather_head",
+    )(head_grad, hidden, whole_input)
+    return out.reshape(256, 4096), head_x, hid_x, inp_x
+
+
+def finish_links(partial, acts, head_x):
+    def kernel(src, act, hx, out, act_x, head_cols, send, recv, x_send, x_recv, *scratch):
+        place = Place()
+        meet(place, True)
+        finish_acts = across_gather(place, act, act_x, x_send, x_recv)
+        scatter = PlaneScatter(place, src, column_block, scratch)
+        scatter.start()
+        gather = PlaneGather(
+            place, hx, head_cols, lambda ref, f: ref.at[:, f], send, recv
+        )
+        out[...] = scatter.middle().astype(jnp.bfloat16)
+        gather.start()
+        gather.relay()
+        gather.finish()
+        finish_acts()
+
+    bf = lambda *shape: jax.ShapeDtypeStruct(shape, jnp.bfloat16)
+    return pl.pallas_call(
+        kernel,
+        out_shape=(bf(256, 128), bf(4, *acts.shape), bf(4, 32, 8, 1024)),
+        in_specs=[VMEM, ANY, ANY],
+        out_specs=[VMEM, ANY, ANY],
+        scratch_shapes=[DMA((32,)), DMA((32,)), DMA((4,)), DMA((4,))]
+        + PlaneScatter.scratch((256, 128)),
+        compiler_params=params(3),
+        name="finish_links",
+    )(partial, acts, head_x)
 
 
 def split3(v):
@@ -83,52 +449,41 @@
         tiled=True,
     ).reshape(owners * slot_cap, width)
 
-    whole_input = lax.all_gather(mlp_input, "fsdp", axis=1, tiled=True)
+    whole_input = gather_input(mlp_input)
     gate_act = jnp.dot(whole_input, gate_weight, preferred_element_type=jnp.float32)
     up_act = jnp.dot(whole_input, up_weight, preferred_element_type=jnp.float32)
     sigmoid_gate = jax.nn.sigmoid(gate_act)
     silu_gate = gate_act * sigmoid_gate
     hidden = (silu_gate * up_act).astype(jnp.bfloat16)
-    branch = lax.psum_scatter(
-        jnp.dot(hidden, down_weight, preferred_element_type=jnp.float32).astype(jnp.bfloat16),
-        "fsdp",
-        scatter_dimension=0,
-        tiled=True,
-    ).astype(jnp.float32)
+    branch = scatter_branch(jnp.dot(hidden, down_weight, preferred_element_type=jnp.bfloat16))
     top_state = branch + residual_in.astype(jnp.float32)
-    all_hidden = lax.all_gather(hidden, "dp", axis=0, tiled=True)
-    input_cols = lax.all_to_all(whole_input, "dp", split_axis=1, concat_axis=0, tiled=True)
 
     query_loss, head_grad = contrast(top_state, positive_keys, buffer, negative_slots)
 
-    gathered_grad = lax.all_gather(head_grad, "fsdp", axis=0, tiled=True)
+    gathered_grad, head_x, hidden_x, input_x = gather_head(head_grad, hidden.T, whole_input)
     hidden_grad = lax.dot_general(
         gathered_grad, down_weight, contract_last, preferred_element_type=jnp.float32
     )
     silu_slope = sigmoid_gate * (1.0 + gate_act * (1.0 - sigmoid_gate))
     gate_grad_act = (hidden_grad * up_act * silu_slope).astype(jnp.bfloat16)
     up_grad_act = (hidden_grad * silu_gate).astype(jnp.bfloat16)
-    both_acts = lax.all_gather(
-        jnp.concatenate([gate_grad_act, up_grad_act], axis=1), "dp", axis=0, tiled=True
-    )
     input_term = lax.dot_general(
         gate_grad_act, gate_weight, contract_last, preferred_element_type=jnp.float32
     ) + lax.dot_general(up_grad_act, up_weight, contract_last, preferred_element_type=jnp.float32)
-    input_grad = lax.psum_scatter(
-        input_term.astype(jnp.bfloat16), "fsdp", scatter_dimension=1, tiled=True
-    )
-    head_cols = lax.all_to_all(gathered_grad, "dp", split_axis=1, concat_axis=0, tiled=True)
+    input_grad, acts_x, head_cols = finish_links(
+        input_term.astype(jnp.bfloat16),
+        jnp.concatenate([gate_grad_act.T, up_grad_act.T], axis=0),
+        head_x,
+    )
+    units = gate_weight.shape[1]
+    over_groups = (((0, 2), (0, 1)), ((), ()))
     down_grad = lax.dot_general(
-        all_hidden, head_cols, contract_first, preferred_element_type=jnp.float32
+        hidden_x, head_cols.reshape(4, 256, 1024), over_groups, preferred_element_type=jnp.float32
     ).astype(jnp.bfloat16)
-    units = gate_weight.shape[1]
-    gate_grad = lax.dot_general(
-        input_cols, both_acts[:, :units], contract_first, preferred_element_type=jnp.float32
+    both = lax.dot_general(
+        acts_x, input_x, over_groups, preferred_element_type=jnp.float32
     ).astype(jnp.bfloat16)
-    up_grad = lax.dot_general(
-        input_cols, both_acts[:, units:], contract_first, preferred_element_type=jnp.float32
-    ).astype(jnp.bfloat16)
-    return (query_loss, input_grad, gate_grad, up_grad, down_grad)
+    return (query_loss, input_grad, both[:units].T, both[units:].T, down_grad)
 
 
 def solution(mesh):

time: 432 us -> 255 us (0.59)
  waiting for transfers between devices: 293 us -> 0.01 us
  Pallas kernels: 0 us -> 192 us
  blocking collectives: 32.2 us -> 0 us
  matrix products: 46.6 us -> 33.3 us
  between operations: 14 us -> 0.85 us
  starting transfers between devices: 21.3 us -> 12 us
  local copies, waits for them, and re-layouts: 12.9 us -> 6.27 us
    pallas_call x0 -> x4, Pallas kernels: none -> 192 us  [the longest x1 111 us: gather_input(): pl.pallas_call(kernel, out_shape=jax.ShapeDtypeStruct((rows, cols * 32),...]
    all_gather x3 -> x0, waiting for transfers between devices: 153 us -> none  [the longest x1 107 us: shards(): whole_input = lax.all_gather(mlp_input, 'fsdp', axis=1, tiled=True)]
    reduce_scatter x1 -> x0, waiting for transfers between devices: 75.2 us -> none  [shards(): lax.psum_scatter(jnp.dot(hidden, down_weight, preferred_element_type=jnp....]
    unnamed x6 -> x0, waiting for transfers between devices: 39.4 us -> none
    all_gather x1 -> x0, blocking collectives: 32.2 us -> none  [shards(): all_hidden = lax.all_gather(hidden, 'dp', axis=0, tiled=True)]
    all_to_all x2 -> x0, waiting for transfers between devices: 25.5 us -> none  [the longest x1 25.5 us: shards(): lax.all_to_all(whole_input, 'dp', split_axis=1, concat_axis=0, tiled=True)]
    all_to_all x2 -> x0, starting transfers between devices: 8.93 us -> none  [the longest x1 4.47 us: shards(): lax.all_to_all(whole_input, 'dp', split_axis=1, concat_axis=0, tiled=True)]
    dot_general x4 -> x3, matrix products: 11.7 us -> 5.41 us  [the longest x1 2.06 us: shards(): lax.dot_general(acts_x, input_x, over_groups, preferred_element_type=jnp....]
  transfers between devices with their start and end apart: 8 -> 1, of which waited for: 5 -> 0; matrix products, arithmetic and copies ran while one was open for 11% -> 3% of each run, Pallas kernels for 0% -> 50%
where the time goes in v2:
time: 255 us; the launch traced here: 254 us
  Pallas kernels  192 us (75%)
  matrix products  33.3 us (13%)
  starting transfers between devices  12 us (5%)
  other arithmetic  9.77 us (4%)
  local copies, waits for them, and re-layouts  6.27 us (2%)
    pallas_call x1, Pallas kernels, gather_input(): pl.pallas_call(kernel, out_shape=jax.ShapeDtypeStruct((rows, cols * 32),...  111 us
    pallas_call x1, Pallas kernels, gather_head(): pl.pallas_call(kernel, out_shape=(bf(32, 8, 4096), bf(4, 8, 1024), bf(4,...  34.1 us
    pallas_call x1, Pallas kernels, finish_links(): pl.pallas_call(kernel, out_shape=(bf(256, 128), bf(4, *acts.shape), bf(4,...  30.2 us
    pallas_call x1, Pallas kernels, scatter_branch(): pl.pallas_call(kernel, out_shape=jax.ShapeDtypeStruct((8, 4096), jnp.floa...  16.9 us
    all_to_all x1, starting transfers between devices, shards(): lax.all_to_all(picked.reshape(owners, slot_cap, width), ('dp', 'fsdp'), s...  12 us
    dot_general x1, matrix products, shards(): picked = jnp.dot(pick, span_index, preferred_element_type=jnp.bfloat16)  9.04 us
    dot_general x1, matrix products, contrast(): lax.dot_general(split3(unit_rows), buffer, contract_last, preferred_eleme...  5.73 us
  transfers between devices with their start and end apart: 1, of which 0 were waited for; matrix products, arithmetic and copies ran while one was open for 3% of the time, Pallas kernels for 50%

profile of v2, /device:TPU:1, one launch (start us, length us, event | category | flops | bytes accessed | tf_op | source)
XLA Modules:
  0.0 254.4 jit_solution(6673847926326411723)
XLA Ops:
  0.6 0.7 iota_compare_fusion.3
  1.4 0.1 lt.20
  1.5 0.8 copy.16
  2.3 0.1 squeeze.3
  2.4 9.0 %convolution_bitcast_fusion = bf16[128,8,4096]{2,1,0:T(8,128)(2,1)} fusion(bf16[512,4096]{1,0:T(8,128)(2,1)} %param.15, s32[1024]{0:T(1024)S(1)} %broadcast_select_fusion), kind=kOutput, calls=%fused_computation.5 | convolution fusion | flops 4295491584 | bytes 12587008 | tf_op jit(solution)/shard_map/dot_general | solution.py:443
  11.4 0.0 copy-start
  11.4 12.0 %all-to-all-start = ((bf16[128,8,4096]{2,1,0:T(8,128)(2,1)}), bf16[128,8,4096]{2,1,0:T(8,128)(2,1)}, u32[]{:S(2)}, u32[]{:S(2)}) async-start(bf16[128,8,4096]{2,1,0:T(8,128)(2,1)} %convolution_bitcast_fusion), calls=%async_computation | async-start | bytes 16777216 | tf_op jit(solution)/shard_map/all_to_all | solution.py:444
  23.4 0.0 copy-done
  23.4 111.1 %gather_input.1.inp = bf16[256,4096]{1,0:T(8,128)(2,1)S(1)} custom-call(bf16[256,128]{1,0:T(8,128)(2,1)S(1)} %copy-done), custom_call_target="tpu_custom_call" | custom-call | tf_op jit(solution)/shard_map/gather_input/pallas_call | solution.py:253
  134.5 0.0 copy-start.2
  134.5 3.3 %fusion.54 = f32[256,448]{0,1:T(8,128)S(1)} fusion(bf16[256,4096]{1,0:T(8,128)(2,1)S(1)} %gather_input.1.inp, bf16[4096,448]{0,1:T(8,128)(2,1)} %param.12), kind=kOutput, calls=%fused_computation.101 | convolution fusion | flops 939524096 | bytes 6225920 | tf_op jit(solution)/shard_map/dot_general | solution.py:453
  137.8 0.0 copy-done.2
  137.8 0.0 copy-start.7
  137.9 1.2 fusion.15
  139.0 0.9 copy-done.7
  139.9 0.0 copy-start.4
  139.9 0.0 copy-start.5
  139.9 0.0 copy-start.6
  139.9 1.3 convolution_bitcast_fusion.1.src
  141.2 16.9 %scatter_branch.1 = f32[8,4096]{1,0:T(8,128)S(1)} custom-call(bf16[32,8,4096]{2,1,0:T(8,128)(2,1)S(1)} %convolution_bitcast_fusion.1.src), custom_call_target="tpu_custom_call" | custom-call | tf_op jit(solution)/shard_map/scatter_branch/pallas_call | solution.py:272
  158.1 0.0 copy-done.4
  158.1 0.1 fusion.29
  158.2 0.0 copy-done.5
  158.3 0.1 multiply_reduce_fusion.2
  158.4 0.0 copy-done.6
  158.4 0.4 convert_reduce_fusion
  158.9 0.7 reduce-precision_convert_fusion.1
  159.6 0.8 reduce-precision_convert_fusion
  160.4 0.0 all-to-all-done
  160.4 5.1 %multiply_reduce_fusion = f32[128,8]{1,0:T(8,128)S(1)} fusion(bf16[128,8,4096]{2,1,0:T(8,128)(2,1)} %all-to-all-done), kind=kLoop, calls=%fused_computation | loop fusion | flops 12581888 | bytes 8392704 | tf_op jit(solution)/shard_map/reduce_sum | solution.py:394
  165.5 0.6 add_rsqrt_fusion
  166.1 0.9 rsqrt.11
  167.0 5.7 %fusion.2 = f32[24,1024]{1,0:T(8,128)S(1)} fusion(bf16[128,8,4096]{2,1,0:T(8,128)(2,1)} %all-to-all-done, bf16[8,4096]{1,0:T(8,128)(2,1)} %get-tuple-element.33, bf16[8,4096]{1,0:T(8,128)(2,1)S(1)} %get-tuple-element.31, bf16[8,4096]{1,0:T(8,128)(2,1)} %get-tuple-element.25), kind=kOutput, calls=%fused_computation.3 | convolution fusion | flops 201916416 | bytes 8683520 | tf_op jit(solution)/shard_map/dot_general | solution.py:395
  172.8 0.1 fusion.46
  172.9 0.2 multiply_reduce_fusion.3
  173.1 0.5 multiply_add_fusion
  173.7 0.0 copy-start.8
  173.7 4.7 %fusion = f32[24,4096]{1,0:T(8,128)S(1)} fusion(bf16[128,8,4096]{2,1,0:T(8,128)(2,1)} %all-to-all-done, bf16[8,1024]{1,0:T(8,128)(2,1)S(1)} %get-tuple-element.36, bf16[8,1024]{1,0:T(8,128)(2,1)S(1)} %get-tuple-element.35, bf16[8,1024]{1,0:T(8,128)(2,1)S(1)} %get-tuple-element.34), kind=kOutput, calls=%fused_computation.1 | convolution fusion | flops 201474048 | bytes 8830976 | tf_op jit(solution)/shard_map/dot_general | solution.py:408
  178.4 0.1 fusion.35.head
  178.6 34.1 %gather_head.1 = (bf16[32,8,4096]{2,1,0:T(8,128)(2,1)S(1)}, bf16[4,8,1024]{2,1,0:T(8,128)(2,1)S(1)}, bf16[4,448,256]{2,1,0:T(8,128)(2,1)S(1)}, bf16[4,256,1024]{2,1,0:T(8,128)(2,1)S(1)}) custom-call(bf16[8,4096]{1,0:T(8,128)(2,1)S(1)} %fusion.35.head, bf16[448,256]{1,0:T(8,128)(2,1)S(1)} %get-tuple-element.38.hid, bf16[256,4096]{1,0:T(8,128)(2,1)S(1)} %gather_input.1.inp), custom_call_target="tpu_custom_call" | custom-call | tf_op jit(solution)/shard_map/gather_head/pallas_call | solution.py:337
  212.6 0.0 copy-done.8
  212.6 0.0 copy-start.1
  212.7 1.2 fusion.13
  213.9 0.8 copy-done.1
  214.7 0.0 copy-start.3
  214.7 1.4 fusion.22
  216.1 0.6 copy-done.3
  216.7 1.3 fusion.4.src
  218.1 30.2 %finish_links.1 = (bf16[256,128]{1,0:T(8,128)(2,1)S(1)}, bf16[4,896,256]{2,1,0:T(8,128)(2,1)S(1)}, bf16[4,32,8,1024]{3,2,1,0:T(8,128)(2,1)S(1)}) custom-call(bf16[256,4096]{1,0:T(8,128)(2,1)S(1)} %fusion.4.src, bf16[896,256]{1,0:T(8,128)(2,1)S(1)} %pad_maximum_fusion.act, bf16[4,8,1024]{2,1,0:T(8,128)(2,1)S(1)} %get-tuple-element.13.hx), custom_call_target="tpu_custom_call" | custom-call | tf_op jit(solution)/shard_map/finish_links/pallas_call | solution.py:366
  248.3 2.1 bitcast_convert_fusion
  250.4 1.4 slice_bitcast_fusion
  251.7 2.0 bitcast_convert_fusion.1
  253.8 0.6 copy.18
  (6 shorter events, 0.1 us)
Async XLA Ops:
  11.4 12.0 %copy-start = (bf16[256,128]{1,0:T(8,128)(2,1)S(1)}, bf16[256,128]{1,0:T(8,128)(2,1)}, u32[]{:S(2)}) copy-start(bf16[256,128]{1,0:T(8,128)(2,1)} %src.1) | copy-start | bytes 196612
  11.4 149.0 %all-to-all-start = ((bf16[128,8,4096]{2,1,0:T(8,128)(2,1)}), bf16[128,8,4096]{2,1,0:T(8,128)(2,1)}, u32[]{:S(2)}, u32[]{:S(2)}) async-start(bf16[128,8,4096]{2,1,0:T(8,128)(2,1)} %convolution_bitcast_fusion), calls=%async_computation | async-start | bytes 16777216 | tf_op jit(solution)/shard_map/all_to_all | solution.py:444
  134.5 3.4 %copy-start.2 = (bf16[4096,448]{0,1:T(8,128)(2,1)S(1)}, bf16[4096,448]{0,1:T(8,128)(2,1)}, u32[]{:S(2)}) copy-start(bf16[4096,448]{0,1:T(8,128)(2,1)} %param.13) | copy-start | bytes 11010052
  137.8 2.0 copy-start.7
  139.9 18.2 %copy-start.4 = (bf16[8,4096]{1,0:T(8,128)(2,1)S(1)}, bf16[8,4096]{1,0:T(8,128)(2,1)}, u32[]{:S(2)}) copy-start(bf16[8,4096]{1,0:T(8,128)(2,1)} %param.16) | copy-start | bytes 196612
  139.9 18.4 %copy-start.5 = (bf16[8,4096]{1,0:T(8,128)(2,1)S(1)}, bf16[8,4096]{1,0:T(8,128)(2,1)}, u32[]{:S(2)}) copy-start(bf16[8,4096]{1,0:T(8,128)(2,1)} %param.11) | copy-start | bytes 196612
  139.9 18.5 %copy-start.6 = (s32[8,64]{1,0:T(8,128)S(1)}, s32[8,64]{1,0:T(8,128)}, u32[]{:S(2)}) copy-start(s32[8,64]{1,0:T(8,128)} %param.19) | copy-start | bytes 6148
  173.7 39.0 %copy-start.8 = (bf16[448,4096]{1,0:T(8,128)(2,1)S(1)}, bf16[448,4096]{1,0:T(8,128)(2,1)}, u32[]{:S(2)}) copy-start(bf16[448,4096]{1,0:T(8,128)(2,1)} %param.14) | copy-start | bytes 11010052
  212.6 2.0 copy-start.1
  214.7 2.0 copy-start.3

commit v3 on v2

--- a/solution.py
+++ b/solution.py
@@ -131,8 +131,8 @@
          self.send2, self.recv2, self.send3, self.recv3) = scratch
 
     @staticmethod
-    def scratch(block):
-        wide = lambda *lead: pltpu.VMEM(lead + block, jnp.bfloat16)
+    def scratch(block, dtype=jnp.bfloat16):
+        wide = lambda *lead: pltpu.VMEM(lead + block, dtype)
         return [wide(16), wide(4, 4), wide(4, 4), wide(4), wide(4), DMA((16,)), DMA((16,)),
                 DMA((4,)), DMA((4,)), DMA((4,)), DMA((4,))]
 
@@ -166,7 +166,7 @@
                     p.x, p.partner,
                 ).wait_recv()
                 own = self.view(self.src, p.at(b, a, p.c))[...].astype(jnp.float32)
-                self.sum1[b, a] = (own + self.got1[k].astype(jnp.float32)).astype(jnp.bfloat16)
+                self.sum1[b, a] = (own + self.got1[k].astype(jnp.float32)).astype(self.sum1.dtype)
             if i:
                 copy = copy_to(
                     self.sum1.at[b], self.got2.at[p.b], self.send2.at[i], self.recv2.at[p.b],
@@ -187,7 +187,7 @@
             for i in near_first:
                 total += self.got2[(p.b + i) % 4, a].astype(jnp.float32)
             if j:
-                self.sum2[a] = total.astype(jnp.bfloat16)
+                self.sum2[a] = total.astype(self.sum2.dtype)
                 copy = copy_to(
                     self.sum2.at[a], self.got3.at[p.a], self.send3.at[j], self.recv3.at[p.a],
                     p.x, p.a_peer(j),
@@ -280,26 +280,22 @@
     )(partial.reshape(32, 8, 4096))
 
 
-def gather_head(head_grad, hidden, whole_input):
-    def kernel(head, hid, inp, out, head_x, hid_x, inp_x, send, recv, hx_send, hx_recv,
+def gather_queries(unit_rows, hidden, whole_input):
+    def kernel(unit, hid, inp, out, unit_x, hid_x, inp_x, send, recv, u_send, u_recv,
                h_send, h_recv, i_send, i_recv, pair_send, pair_recv):
         place = Place()
         p = place
         meet(place, True)
-        gather = PlaneGather(place, head, out, row_block, send, recv)
+        finish_unit = across_gather(place, unit, unit_x, u_send, u_recv)
+        finish_unit()
+        gather = PlaneGather(place, unit_x, out, row_block, send, recv)
         gather.start()
-        wide = lambda x: pl.ds(pl.multiple_of(x * 1024, 1024), 1024)
         half = lambda c: pl.ds(pl.multiple_of(c * 512, 512), 512)
-        own_h = pltpu.make_async_copy(head.at[:, wide(p.x)], head_x.at[p.x], hx_send.at[0])
-        own_h.start()
-        own_i = pltpu.make_async_copy(inp.at[:, wide(p.x)], inp_x.at[p.x], i_send.at[0])
+        own_i = pltpu.make_async_copy(
+            inp.at[:, pl.ds(pl.multiple_of(p.x * 1024, 1024), 1024)], inp_x.at[p.x], i_send.at[0]
+        )
         own_i.start()
         sent = []
-        for j in near_first:
-            x = (p.x + j) % 4
-            copy = copy_to(head.at[:, wide(x)], head_x.at[p.x], hx_send.at[j], hx_recv.at[p.x], x, p.f)
-            copy.start()
-            sent.append(copy)
         finish_hidden = across_gather(place, hid, hid_x, h_send, h_recv)
         for j in near_first:
             x = (p.x + j) % 4
@@ -313,11 +309,6 @@
         gather.finish()
         for j in near_first:
             x = (p.x + j) % 4
-            copy_to(
-                head_x.at[x], head_x.at[x], hx_send.at[j], hx_recv.at[x], x, p.f
-            ).wait_recv()
-        for j in near_first:
-            x = (p.x + j) % 4
             region = inp_x.at[x, :, half(p.c)]
             copy_to(region, region, i_send.at[j], i_recv.at[x], x, p.f).wait_recv()
             copy = copy_to(region, region, pair_send.at[j], pair_recv.at[x], p.x, p.partner)
@@ -328,22 +319,120 @@
             region = inp_x.at[x, :, half(1 - p.c)]
             copy_to(region, region, pair_send.at[j], pair_recv.at[x], p.x, p.partner).wait_recv()
         finish_hidden()
-        own_h.wait()
         own_i.wait()
         for copy in sent:
             copy.wait_send()
 
     bf = lambda *shape: jax.ShapeDtypeStruct(shape, jnp.bfloat16)
-    out, head_x, hid_x, inp_x = pl.pallas_call(
+    out, _, hid_x, inp_x = pl.pallas_call(
         kernel,
-        out_shape=(bf(32, 8, 4096), bf(4, 8, 1024), bf(4, *hidden.shape), bf(4, 256, 1024)),
+        out_shape=(bf(32, 4, 8, 4096), bf(4, 8, 4096), bf(4, *hidden.shape), bf(4, 256, 1024)),
         in_specs=[ANY] * 3,
         out_specs=[ANY] * 4,
         scratch_shapes=[DMA((32,)), DMA((32,))] + [DMA((4,))] * 8,
+        compiler_params=params(4),
+        name="gather_queries",
+    )(unit_rows, hidden, whole_input)
+    return out.reshape(1024, 4096), hid_x, inp_x
+
+
+def across_sum(place, total, stage, got, send, recv):
+    stage[...] = total.astype(stage.dtype)
+    sent = []
+    for j in near_first:
+        x = (place.x + j) % 4
+        copy = copy_to(stage.at[x], got.at[place.x], send.at[j], recv.at[place.x], x, place.f)
+        copy.start()
+        sent.append(copy)
+
+    def finish():
+        own = stage[place.x].astype(jnp.float32)
+        for j in near_first:
+            x = (place.x + j) % 4
+            copy_to(got.at[x], got.at[x], send.at[j], recv.at[x], x, place.f).wait_recv()
+            own += got[x].astype(jnp.float32)
+        for copy in sent:
+            copy.wait_send()
+        return own
+
+    return finish
+
+
+def scatter_pull(pull, sums):
+    n = 11
+
+    def kernel(pull_ref, sums_ref, pull_out, sums_out, stage_p, got_p, sp, rp, stage_s, got_s, ss,
+               rs, *scratch):
+        place = Place()
+        meet(place, True)
+        first = PlaneScatter(place, pull_ref, row_block, scratch[:n])
+        second = PlaneScatter(place, sums_ref, row_block, scratch[n:])
+        first.start()
+        second.start()
+        finish_p = across_sum(place, first.middle(), stage_p, got_p, sp, rp)
+        finish_s = across_sum(place, second.middle(), stage_s, got_s, ss, rs)
+        pull_out[...] = finish_p()
+        sums_out[...] = finish_s()
+
+    return pl.pallas_call(
+        kernel,
+        out_shape=(
+            jax.ShapeDtypeStruct((8, 4096), jnp.float32),
+            jax.ShapeDtypeStruct((8, 128), jnp.float32),
+        ),
+        in_specs=[VMEM, VMEM],
+        out_specs=[VMEM, VMEM],
+        scratch_shapes=[
+            pltpu.VMEM((4, 8, 4096), jnp.bfloat16), pltpu.VMEM((4, 8, 4096), jnp.bfloat16),
+            DMA((4,)), DMA((4,)),
+            pltpu.VMEM((4, 8, 128), jnp.float32), pltpu.VMEM((4, 8, 128), jnp.float32),
+            DMA((4,)), DMA((4,)),
+        ]
+        + PlaneScatter.scratch((4, 8, 4096))
+        + PlaneScatter.scratch((4, 8, 128), jnp.float32),
+        compiler_params=params(5),
+        name="scatter_pull",
+    )(pull, sums)
+
+
+def gather_head(head_grad):
+    def kernel(head, out, head_x, send, recv, hx_send, hx_recv):
+        place = Place()
+        p = place
+        meet(place, True)
+        gather = PlaneGather(place, head, out, row_block, send, recv)
+        gather.start()
+        wide = lambda x: pl.ds(pl.multiple_of(x * 1024, 1024), 1024)
+        own = pltpu.make_async_copy(head.at[:, wide(p.x)], head_x.at[p.x], hx_send.at[0])
+        own.start()
+        sent = []
+        for j in near_first:
+            x = (p.x + j) % 4
+            copy = copy_to(head.at[:, wide(x)], head_x.at[p.x], hx_send.at[j], hx_recv.at[p.x], x, p.f)
+            copy.start()
+            sent.append(copy)
+        gather.relay()
+        gather.finish()
+        for j in near_first:
+            x = (p.x + j) % 4
+            copy_to(
+                head_x.at[x], head_x.at[x], hx_send.at[j], hx_recv.at[x], x, p.f
+            ).wait_recv()
+        own.wait()
+        for copy in sent:
+            copy.wait_send()
+
+    bf = lambda *shape: jax.ShapeDtypeStruct(shape, jnp.bfloat16)
+    out, head_x = pl.pallas_call(
+        kernel,
+        out_shape=(bf(32, 8, 4096), bf(4, 8, 1024)),
+        in_specs=[ANY],
+        out_specs=[ANY] * 2,
+        scratch_shapes=[DMA((32,)), DMA((32,)), DMA((4,)), DMA((4,))],
         compiler_params=params(2),
         name="gather_head",
-    )(head_grad, hidden, whole_input)
-    return out.reshape(256, 4096), head_x, hid_x, inp_x
+    )(head_grad)
+    return out.reshape(256, 4096), head_x
 
 
 def finish_links(partial, acts, head_x):
@@ -356,9 +445,9 @@
         gather = PlaneGather(
             place, hx, head_cols, lambda ref, f: ref.at[:, f], send, recv
         )
-        out[...] = scatter.middle().astype(jnp.bfloat16)
         gather.start()
         gather.relay()
+        out[...] = scatter.middle().astype(jnp.bfloat16)
         gather.finish()
         finish_acts()
 
@@ -375,47 +464,29 @@
     )(partial, acts, head_x)
 
 
-def split3(v):
-    hi = lax.reduce_precision(v, 8, 7)
-    mid = lax.reduce_precision(v - hi, 8, 7)
-    return jnp.concatenate([hi, mid, v - hi - mid], axis=0).astype(jnp.bfloat16)
-
-
-def contrast(top_state, positive_keys, buffer, negative_slots):
-    rows = top_state.shape[0]
-    slots = buffer.shape[0]
-    row_norm = jnp.sqrt(jnp.sum(top_state * top_state, axis=-1) + eps)
-    unit_rows = top_state / row_norm[:, None]
-    positive = positive_keys.astype(jnp.float32)
-    positive_unit = positive / jnp.sqrt(jnp.sum(positive * positive, axis=-1, keepdims=True) + eps)
-    positive_score = inverse_temp * jnp.sum(unit_rows * positive_unit, axis=-1)
-
-    wide = buffer.astype(jnp.float32)
+def owner_sums(unit_rows, span_index, codes):
+    shard_rows = span_index.shape[0]
+    wide = span_index.astype(jnp.float32)
     key_scale = lax.rsqrt(jnp.sum(wide * wide, axis=-1) + eps)
     raw = lax.dot_general(
-        split3(unit_rows), buffer, contract_last, preferred_element_type=jnp.float32
-    )
-    raw = raw[:rows] + raw[rows : 2 * rows] + raw[2 * rows :]
+        unit_rows, span_index, contract_last, preferred_element_type=jnp.float32
+    )
     scores = inverse_temp * raw * key_scale[None, :]
-    slot_ids = lax.broadcasted_iota(jnp.int32, (1, 1, slots), 2)
-    uses = jnp.sum((negative_slots[:, :, None] == slot_ids).astype(jnp.float32), axis=1)
-    weights = jnp.where(uses > 0, uses * jnp.exp(scores), 0.0)
-    positive_weight = jnp.exp(positive_score)
-    exp_total = jnp.sum(weights, axis=-1) + positive_weight
-    query_loss = jnp.log(exp_total) - positive_score
-    coeffs = weights / exp_total[:, None]
-    positive_coeff = positive_weight / exp_total - 1.0
-    pull = lax.dot_general(
-        split3(coeffs * key_scale[None, :]),
-        buffer,
-        (((1,), (0,)), ((), ())),
-        preferred_element_type=jnp.float32,
-    )
-    pull = pull[:rows] + pull[rows : 2 * rows] + pull[2 * rows :]
-    pull = inverse_temp * (pull + positive_coeff[:, None] * positive_unit)
-    inner = jnp.sum(coeffs * scores, axis=-1) + positive_coeff * positive_score
-    head_grad = ((pull - inner[:, None] * unit_rows) / row_norm[:, None]).astype(jnp.bfloat16)
-    return query_loss, head_grad
+    groups, slots = codes.shape
+    queries = unit_rows.shape[0] // groups
+    here = lax.broadcasted_iota(jnp.int32, (groups, queries, shard_rows), 2)
+    here += shard_rows * lax.broadcasted_iota(jnp.int32, (groups, queries, shard_rows), 1)
+    uses = jnp.zeros(here.shape, jnp.float32)
+    for slot in range(slots):
+        uses += (codes[:, slot][:, None, None] == here).astype(jnp.float32)
+    uses = uses.reshape(raw.shape)
+    weights = uses * jnp.exp(scores)
+    pull = jnp.dot(
+        (weights * key_scale[None, :]).astype(jnp.bfloat16),
+        span_index,
+        preferred_element_type=jnp.bfloat16,
+    )
+    return pull, jnp.sum(weights, axis=-1), jnp.sum(weights * scores, axis=-1)
 
 
 def shards(
@@ -430,24 +501,22 @@
     request_counts,
     negative_slots,
 ):
-    owners = lax.axis_size("dp") * lax.axis_size("fsdp")
+    dp_count = lax.axis_size("dp")
+    fsdp_count = lax.axis_size("fsdp")
+    owners = dp_count * fsdp_count
     slot_cap = request_rows.shape[2]
-    width = span_index.shape[1]
-
+    rows, width = positive_keys.shape
+
+    slot_ids = lax.broadcasted_iota(jnp.int32, (1, 1, owners * slot_cap), 2)
+    used = jnp.any(negative_slots[:, :, None] == slot_ids, axis=1).astype(jnp.int32)
+    ranks = lax.broadcasted_iota(jnp.int32, used.shape, 0) + 1
+    user = (jnp.sum(used * ranks, axis=0) - 1).reshape(owners, slot_cap)
+    user = lax.all_to_all(user, ("dp", "fsdp"), split_axis=0, concat_axis=0, tiled=True)
     row_table = request_rows[:, 0, :]
     live = lax.broadcasted_iota(jnp.int32, row_table.shape, 1) < request_counts
-    wanted = jnp.where(live, row_table, -1).reshape(-1)
-    pick = (wanted[:, None] == lax.broadcasted_iota(jnp.int32, (1, span_index.shape[0]), 1)).astype(
-        jnp.bfloat16
-    )
-    picked = jnp.dot(pick, span_index, preferred_element_type=jnp.bfloat16)
-    buffer = lax.all_to_all(
-        picked.reshape(owners, slot_cap, width),
-        ("dp", "fsdp"),
-        split_axis=0,
-        concat_axis=0,
-        tiled=True,
-    ).reshape(owners * slot_cap, width)
+    codes = jnp.where(live & (user >= 0), row_table + span_index.shape[0] * user, -1)
+    codes = codes.reshape(dp_count, fsdp_count, slot_cap).transpose(1, 0, 2)
+    codes = codes.reshape(owners, slot_cap)
 
     whole_input = gather_input(mlp_input)
     gate_act = jnp.dot(whole_input, gate_weight, preferred_element_type=jnp.float32)
@@ -457,10 +526,31 @@
     hidden = (silu_gate * up_act).astype(jnp.bfloat16)
     branch = scatter_branch(jnp.dot(hidden, down_weight, preferred_element_type=jnp.bfloat16))
     top_state = branch + residual_in.astype(jnp.float32)
-
-    query_loss, head_grad = contrast(top_state, positive_keys, buffer, negative_slots)
-
-    gathered_grad, head_x, hidden_x, input_x = gather_head(head_grad, hidden.T, whole_input)
+    row_norm = jnp.sqrt(jnp.sum(top_state * top_state, axis=-1) + eps)
+    unit_rows = top_state / row_norm[:, None]
+    positive = positive_keys.astype(jnp.float32)
+    positive_unit = positive / jnp.sqrt(jnp.sum(positive * positive, axis=-1, keepdims=True) + eps)
+    positive_score = inverse_temp * jnp.sum(unit_rows * positive_unit, axis=-1)
+
+    all_units, hidden_x, input_x = gather_queries(
+        unit_rows.astype(jnp.bfloat16), hidden.T, whole_input
+    )
+    pull, exps, inners = owner_sums(all_units, span_index, codes)
+    lanes = lax.broadcasted_iota(jnp.int32, (exps.shape[0], 128), 1)
+    sums = jnp.where(lanes == 0, exps[:, None], jnp.where(lanes == 1, inners[:, None], 0.0))
+    pull, sums = scatter_pull(
+        pull.reshape(fsdp_count, dp_count, rows, width),
+        sums.reshape(fsdp_count, dp_count, rows, 128),
+    )
+    positive_weight = jnp.exp(positive_score)
+    exp_total = sums[:, 0] + positive_weight
+    query_loss = jnp.log(exp_total) - positive_score
+    positive_coeff = positive_weight / exp_total - 1.0
+    inner = sums[:, 1] / exp_total + positive_coeff * positive_score
+    pull = inverse_temp * (pull / exp_total[:, None] + positive_coeff[:, None] * positive_unit)
+    head_grad = ((pull - inner[:, None] * unit_rows) / row_norm[:, None]).astype(jnp.bfloat16)
+
+    gathered_grad, head_x = gather_head(head_grad)
     hidden_grad = lax.dot_general(
         gathered_grad, down_weight, contract_last, preferred_element_type=jnp.float32
     )

time: 255 us -> 252 us (0.988)
  local copies, waits for them, and re-layouts: 6.27 us -> 14.7 us
  Pallas kernels: 192 us -> 186 us
  other arithmetic: 9.77 us -> 4.7 us
    pallas_call x1, Pallas kernels: 111 us -> 17.6 us  [gather_input(): pl.pallas_call(kernel, out_shape=jax.ShapeDtypeStruct((rows, cols * 32),...]
    pallas_call x1 -> x3, Pallas kernels: 34.1 us -> 122 us  [the longest x1 56.1 us: scatter_pull(): pl.pallas_call(kernel, out_shape=(jax.ShapeDtypeStruct((8, 4096), jnp.flo...]
    unnamed x20 -> x40, local copies, waits for them, and re-layouts: 3.78 us -> 9.27 us
    reduce_sum x6 -> x4, other arithmetic: 6.17 us -> 1.27 us  [the longest x1 0.89 us: owner_sums(): key_scale = lax.rsqrt(jnp.sum(wide * wide, axis=-1) + eps)]
    dot_general x3 -> x2, matrix products: 19.5 us -> 19.2 us  [the longest x1 10.1 us: owner_sums(): lax.dot_general(unit_rows, span_index, contract_last, preferred_element_t...]
  transfers between devices with their start and end apart: 1 -> 1, of which waited for: 0 -> 0; matrix products, arithmetic and copies ran while one was open for 3% -> 3% of each run, Pallas kernels for 50% -> 31%
where the time goes in v3:
time: 252 us
  Pallas kernels  186 us (74%)
  matrix products  33.1 us (13%)
  local copies, waits for them, and re-layouts  14.7 us (6%)
  starting transfers between devices  12 us (5%)
  other arithmetic  4.7 us (2%)
    pallas_call x1, Pallas kernels, scatter_pull(): pl.pallas_call(kernel, out_shape=(jax.ShapeDtypeStruct((8, 4096), jnp.flo...  56.1 us
    pallas_call x1, Pallas kernels, gather_queries(): pl.pallas_call(kernel, out_shape=(bf(32, 4, 8, 4096), bf(4, 8, 4096), bf(...  43.3 us
    pallas_call x1, Pallas kernels, finish_links(): pl.pallas_call(kernel, out_shape=(bf(256, 128), bf(4, *acts.shape), bf(4,...  30.6 us
    pallas_call x1, Pallas kernels, gather_head(): pl.pallas_call(kernel, out_shape=(bf(32, 8, 4096), bf(4, 8, 1024)), in_sp...  22.3 us
    pallas_call x1, Pallas kernels, gather_input(): pl.pallas_call(kernel, out_shape=jax.ShapeDtypeStruct((rows, cols * 32),...  17.6 us
    pallas_call x1, Pallas kernels, scatter_branch(): pl.pallas_call(kernel, out_shape=jax.ShapeDtypeStruct((8, 4096), jnp.floa...  16.3 us
    all_to_all x1, starting transfers between devices, shards(): lax.all_to_all(user, ('dp', 'fsdp'), split_axis=0, concat_axis=0, tiled=T...  12 us
    dot_general x1, matrix products, owner_sums(): lax.dot_general(unit_rows, span_index, contract_last, preferred_element_t...  10.1 us
  transfers between devices with their start and end apart: 1, of which 0 were waited for; matrix products, arithmetic and copies ran while one was open for 3% of the time, Pallas kernels for 31%

profile of v3, /device:TPU:1, one launch (start us, length us, event | category | flops | bytes accessed | tf_op | source)
XLA Modules:
  0.0 251.9 jit_solution(17054064548324723594)
XLA Ops:
  0.6 1.2 fusion.13
  1.9 0.1 select_reduce_fusion
  2.0 0.7 sub.22
  2.7 12.0 %all-to-all-start = ((s32[128,1,8]{2,1,0:T(1,128)}), s32[128,1,8]{2,1,0:T(1,128)}, u32[]{:S(2)}, u32[]{:S(2)}) async-start(s32[128,1,8]{2,1,0:T(1,128)} %bitcast), calls=%async_computation | async-start | bytes 131072 | tf_op jit(solution)/shard_map/all_to_all | solution.py:514
  14.7 0.8 copy-done
  15.5 17.6 %gather_input.1.inp = bf16[256,4096]{1,0:T(8,128)(2,1)S(1)} custom-call(bf16[256,128]{1,0:T(8,128)(2,1)S(1)} %copy-done), custom_call_target="tpu_custom_call" | custom-call | tf_op jit(solution)/shard_map/gather_input/pallas_call | solution.py:253
  33.2 3.3 %fusion.42 = f32[256,448]{0,1:T(8,128)S(1)} fusion(bf16[256,4096]{1,0:T(8,128)(2,1)S(1)} %gather_input.1.inp, bf16[4096,448]{0,1:T(8,128)(2,1)} %param.12), kind=kOutput, calls=%fused_computation.96 | convolution fusion | flops 939524096 | bytes 6225920 | tf_op jit(solution)/shard_map/dot_general | solution.py:522
  36.5 1.1 fusion.21
  37.7 1.2 copy-done.16
  38.9 1.3 convolution_bitcast_fusion.src
  40.2 16.3 %scatter_branch.1 = f32[8,4096]{1,0:T(8,128)S(1)} custom-call(bf16[32,8,4096]{2,1,0:T(8,128)(2,1)S(1)} %convolution_bitcast_fusion.src), custom_call_target="tpu_custom_call" | custom-call | tf_op jit(solution)/shard_map/scatter_branch/pallas_call | solution.py:272
  56.6 0.1 fusion.30
  56.8 0.9 multiply_reduce_fusion
  57.7 0.1 multiply_reduce_fusion.3
  57.8 0.2 fusion.40
  58.1 0.5 broadcast.164
  58.6 0.7 reduce.27
  59.3 0.1 lt.11
  59.4 0.1 iota.119
  59.5 0.1 copy.55
  59.5 43.3 %gather_queries.1 = (bf16[32,4,8,4096]{3,2,1,0:T(8,128)(2,1)S(1)}, bf16[4,8,4096]{2,1,0:T(8,128)(2,1)}, bf16[4,448,256]{2,1,0:T(8,128)(2,1)S(1)}, bf16[4,256,1024]{2,1,0:T(8,128)(2,1)S(1)}) custom-call(bf16[8,4096]{1,0:T(8,128)(2,1)S(1)} %get-tuple-element.43.unit, bf16[448,256]{1,0:T(8,128)(2,1)S(1)} %get-tuple-element.47.hid, ...), custom_call_target="tpu_custom_call" | custom-call | tf_op jit(solution)/shard_map/gather_queries/pallas_call | solution.py:327
  102.9 3.2 %copy-done.1 = bf16[32,4,8,4096]{3,2,1,0:T(8,128)(2,1)} copy-done((bf16[32,4,8,4096]{3,2,1,0:T(8,128)(2,1)}, bf16[32,4,8,4096]{3,2,1,0:T(8,128)(2,1)S(1)}, u32[]{:S(2)}) %copy-start.1) | copy-done | bytes 8388632
  106.1 1.4 copy-done.2
  107.5 0.9 copy.52
  108.4 0.1 add.136
  108.5 0.1 ge.12
  108.6 0.1 copy.54
  108.7 0.4 slice_reduce_fusion.7
  109.1 0.1 eq.151
  109.2 0.1 eq.152
  109.3 0.1 eq.156
  109.3 0.1 eq.157
  109.4 0.1 eq.161
  109.5 0.1 eq.162
  109.6 0.1 eq.166
  109.7 0.1 eq.167
  109.8 0.1 eq.171
  109.9 0.1 eq.172
  110.0 0.1 eq.176
  110.1 0.1 eq.177
  110.2 0.1 eq.181
  110.2 0.1 eq.182
  110.3 0.1 eq.186
  110.4 0.1 eq.187
  110.5 10.1 %fusion.41 = (f32[1024]{0:T(1024)S(1)}, f32[1024]{0:T(1024)S(1)}, f32[1024,512]{0,1:T(8,128)S(1)}) fusion(f32[512]{0:T(512)S(1)} %get-tuple-element.45, s32[1024]{0:T(1024)S(1)} %eq.187, s32[1024]{0:T(1024)S(1)} %eq.182, s32[1024]{0:T(1024)S(1)} %eq.177, s32[1024]{0:T(1024)S(1)} %eq.172, s32[1024]{0:T(1024)S(1)} %eq.167, s32[1024]{0:T(1024)S(1)} %eq.162, ...), kind=kOutput, calls=%fused_computation.95 | convolution fusion | flops 4310169600 | bytes 14727168 | tf_op jit(solution)/shard_map/dot_general | solution.py:471
  120.7 0.1 broadcast_in_dim.40
  120.8 0.1 broadcast_in_dim.42
  120.9 9.1 %fusion.16 = bf16[1024,4096]{1,0:T(8,128)(2,1)S(1)} fusion(bf16[512,4096]{1,0:T(8,128)(2,1)} %param.15, f32[512]{0:T(512)S(1)} %get-tuple-element.46, f32[1024,512]{0,1:T(8,128)S(1)} %get-tuple-element.49, f32[512]{0:T(512)S(1)} %get-tuple-element.45, s32[1024]{0:T(1024)S(1)} %eq.187, s32[1024]{0:T(1024)S(1)} %eq.182, s32[1024]{0:T(1024)S(1)} %eq.177, ...), kind=kOutput, calls=%fused_computation.24 | convolution fusion | flops 4309647360 | bytes 14721024 | tf_op jit(solution)/shard_map/dot_general | solution.py:484
  130.0 0.3 select_select_fusion.sums_ref
  130.4 56.1 %scatter_pull.1 = (f32[8,4096]{1,0:T(8,128)S(1)}, f32[8,128]{1,0:T(8,128)S(1)}) custom-call(bf16[32,4,8,4096]{3,2,1,0:T(8,128)(2,1)S(1)} %bitcast.85, f32[32,4,8,128]{3,2,1,0:T(8,128)S(1)} %select_select_fusion.sums_ref), custom_call_target="tpu_custom_call" | custom-call | tf_op jit(solution)/shard_map/scatter_pull/pallas_call | solution.py:377
  186.5 0.2 fusion.36
  186.7 0.1 divide_convert_fusion.head
  186.8 22.3 %gather_head.1 = (bf16[32,8,4096]{2,1,0:T(8,128)(2,1)S(1)}, bf16[4,8,1024]{2,1,0:T(8,128)(2,1)S(1)}) custom-call(bf16[8,4096]{1,0:T(8,128)(2,1)S(1)} %divide_convert_fusion.head), custom_call_target="tpu_custom_call" | custom-call | tf_op jit(solution)/shard_map/gather_head/pallas_call | solution.py:426
  209.2 1.2 fusion.19
  210.4 0.8 copy-done.4
  211.2 1.4 fusion.28
  212.6 0.6 copy-done.7
  213.3 1.3 fusion.src
  214.6 30.6 %finish_links.1 = (bf16[256,128]{1,0:T(8,128)(2,1)S(1)}, bf16[4,896,256]{2,1,0:T(8,128)(2,1)S(1)}, bf16[4,32,8,1024]{3,2,1,0:T(8,128)(2,1)S(1)}) custom-call(bf16[256,4096]{1,0:T(8,128)(2,1)S(1)} %fusion.src, bf16[896,256]{1,0:T(8,128)(2,1)S(1)} %pad_maximum_fusion.act, bf16[4,8,1024]{2,1,0:T(8,128)(2,1)S(1)} %get-tuple-element.19.hx), custom_call_target="tpu_custom_call" | custom-call | tf_op jit(solution)/shard_map/finish_links/pallas_call | solution.py:455
  245.2 2.1 bitcast_convert_fusion
  247.3 1.4 slice_bitcast_fusion
  248.7 0.5 log_subtract_fusion
  249.2 2.0 bitcast_convert_fusion.1
  251.3 0.6 copy.58
  (45 shorter events, 0.2 us)
Async XLA Ops:
  2.7 104.8 %all-to-all-start = ((s32[128,1,8]{2,1,0:T(1,128)}), s32[128,1,8]{2,1,0:T(1,128)}, u32[]{:S(2)}, u32[]{:S(2)}) async-start(s32[128,1,8]{2,1,0:T(1,128)} %bitcast), calls=%async_computation | async-start | bytes 131072 | tf_op jit(solution)/shard_map/all_to_all | solution.py:514
  14.7 0.8 copy-start
  33.1 3.4 %copy-start.6 = (bf16[4096,448]{0,1:T(8,128)(2,1)S(1)}, bf16[4096,448]{0,1:T(8,128)(2,1)}, u32[]{:S(2)}) copy-start(bf16[4096,448]{0,1:T(8,128)(2,1)} %param.13) | copy-start | bytes 11010052
  36.5 1.2 copy-start.8
  36.5 2.4 copy-start.16
  37.7 2.5 %copy-start.10 = (f32[256,448]{0,1:T(8,128)}, f32[256,448]{0,1:T(8,128)S(1)}, u32[]{:S(2)}) copy-start(f32[256,448]{0,1:T(8,128)S(1)} %get-tuple-element.48) | copy-start | bytes 1376260
  38.9 17.8 %copy-start.5 = (bf16[512,4096]{1,0:T(8,128)(2,1)S(1)}, bf16[512,4096]{1,0:T(8,128)(2,1)}, u32[]{:S(2)}) copy-start(bf16[512,4096]{1,0:T(8,128)(2,1)} %param.15) | copy-start | bytes 12582916
  40.2 16.3 %copy-start.13 = (bf16[8,4096]{1,0:T(8,128)(2,1)S(1)}, bf16[8,4096]{1,0:T(8,128)(2,1)}, u32[]{:S(2)}) copy-start(bf16[8,4096]{1,0:T(8,128)(2,1)} %param.16) | copy-start | bytes 196612
  56.7 0.9 copy-start.12
  56.7 1.9 copy-start.18
  57.6 50.8 %copy-start.15 = (s32[128,1,8]{0,2,1:T(8,128)S(1)}, s32[128,1,8]{0,2,1:T(8,128)}, u32[]{:S(2)}) copy-start(s32[128,1,8]{0,2,1:T(8,128)} %param.17) | copy-start | bytes 12292
  102.9 3.2 %copy-start.1 = (bf16[32,4,8,4096]{3,2,1,0:T(8,128)(2,1)}, bf16[32,4,8,4096]{3,2,1,0:T(8,128)(2,1)S(1)}, u32[]{:S(2)}) copy-start(bf16[32,4,8,4096]{3,2,1,0:T(8,128)(2,1)S(1)} %get-tuple-element.15) | copy-start | bytes 25165828
  106.1 1.4 copy-start.2
  130.3 56.3 %copy-start.14 = (bf16[8,4096]{1,0:T(8,128)(2,1)S(1)}, bf16[8,4096]{1,0:T(8,128)(2,1)}, u32[]{:S(2)}) copy-start(bf16[8,4096]{1,0:T(8,128)(2,1)} %param.16) | copy-start | bytes 196612
  130.4 78.8 %copy-start.9 = (f32[256,448]{0,1:T(8,128)S(1)}, f32[256,448]{0,1:T(8,128)}, u32[]{:S(2)}) copy-start(f32[256,448]{0,1:T(8,128)} %copy-done.8) | copy-start | bytes 1376260
  130.4 78.8 %copy-start.11 = (f32[256,448]{0,1:T(8,128)S(1)}, f32[256,448]{0,1:T(8,128)}, u32[]{:S(2)}) copy-start(f32[256,448]{0,1:T(8,128)} %copy-done.10) | copy-start | bytes 1376260
  130.4 78.8 %copy-start.17 = (bf16[448,4096]{1,0:T(8,128)(2,1)S(1)}, bf16[448,4096]{1,0:T(8,128)(2,1)}, u32[]{:S(2)}) copy-start(bf16[448,4096]{1,0:T(8,128)(2,1)} %param.14) | copy-start | bytes 11010052
  209.2 2.0 copy-start.4
  211.2 2.0 copy-start.7
  214.6 30.6 %copy-start.3 = (bf16[4,256,1024]{2,1,0:T(8,128)(2,1)S(1)}, bf16[4,256,1024]{2,1,0:T(8,128)(2,1)}, u32[]{:S(2)}) copy-start(bf16[4,256,1024]{2,1,0:T(8,128)(2,1)} %copy-done.2) | copy-start | bytes 6291460

commit v4 on v3

--- a/solution.py
+++ b/solution.py
@@ -226,9 +226,9 @@
     return finish
 
 
-def params(collective_id):
+def params(collective_id, mib):
     return pltpu.CompilerParams(
-        collective_id=collective_id, has_side_effects=True, vmem_limit_bytes=40 * 1024 * 1024
+        collective_id=collective_id, has_side_effects=True, vmem_limit_bytes=mib * 1024 * 1024
     )
 
 
@@ -240,25 +240,33 @@
     return ref.at[f]
 
 
-def gather_input(mlp_input):
-    def kernel(src, out, send, recv):
+def gather_input(mlp_input, table):
+    def kernel(src, tab, out, tab_x, tab_all, send, recv, x_send, x_recv, t_send, t_recv):
         place = Place()
-        meet(place, False)
+        meet(place, True)
+        finish_table = across_gather(place, tab, tab_x, x_send, x_recv)
         gather = PlaneGather(place, src, out, column_block, send, recv)
         gather.start()
+        finish_table()
+        tables = PlaneGather(place, tab_x, tab_all, row_block, t_send, t_recv)
+        tables.start()
         gather.relay()
+        tables.relay()
         gather.finish()
+        tables.finish()
 
     rows, cols = mlp_input.shape
-    return pl.pallas_call(
+    ints = lambda *lead: jax.ShapeDtypeStruct(lead + table.shape, jnp.int32)
+    out, _, tables = pl.pallas_call(
         kernel,
-        out_shape=jax.ShapeDtypeStruct((rows, cols * 32), jnp.bfloat16),
-        in_specs=[ANY],
-        out_specs=ANY,
-        scratch_shapes=[DMA((32,)), DMA((32,))],
-        compiler_params=params(0),
+        out_shape=(jax.ShapeDtypeStruct((rows, cols * 32), jnp.bfloat16), ints(4), ints(32, 4)),
+        in_specs=[ANY] * 2,
+        out_specs=[ANY] * 3,
+        scratch_shapes=[DMA((32,)), DMA((32,)), DMA((4,)), DMA((4,)), DMA((32,)), DMA((32,))],
+        compiler_params=params(0, 4),
         name="gather_input",
-    )(mlp_input)
+    )(mlp_input, table)
+    return out, tables
 
 
 def scatter_branch(partial):
@@ -275,7 +283,7 @@
         in_specs=[VMEM],
         out_specs=VMEM,
         scratch_shapes=PlaneScatter.scratch((8, 4096)),
-        compiler_params=params(1),
+        compiler_params=params(1, 12),
         name="scatter_branch",
     )(partial.reshape(32, 8, 4096))
 
@@ -330,7 +338,7 @@
         in_specs=[ANY] * 3,
         out_specs=[ANY] * 4,
         scratch_shapes=[DMA((32,)), DMA((32,))] + [DMA((4,))] * 8,
-        compiler_params=params(4),
+        compiler_params=params(4, 4),
         name="gather_queries",
     )(unit_rows, hidden, whole_input)
     return out.reshape(1024, 4096), hid_x, inp_x
@@ -358,13 +366,14 @@
     return finish
 
 
-def scatter_pull(pull, sums):
+def scatter_pull(pull, sums, factors):
     n = 11
 
-    def kernel(pull_ref, sums_ref, pull_out, sums_out, stage_p, got_p, sp, rp, stage_s, got_s, ss,
-               rs, *scratch):
+    def kernel(pull_ref, sums_ref, fac, pull_out, sums_out, fac_x, f_send, f_recv,
+               stage_p, got_p, sp, rp, stage_s, got_s, ss, rs, *scratch):
         place = Place()
         meet(place, True)
+        finish_factors = across_gather(place, fac, fac_x, f_send, f_recv)
         first = PlaneScatter(place, pull_ref, row_block, scratch[:n])
         second = PlaneScatter(place, sums_ref, row_block, scratch[n:])
         first.start()
@@ -373,16 +382,19 @@
         finish_s = across_sum(place, second.middle(), stage_s, got_s, ss, rs)
         pull_out[...] = finish_p()
         sums_out[...] = finish_s()
+        finish_factors()
 
     return pl.pallas_call(
         kernel,
         out_shape=(
             jax.ShapeDtypeStruct((8, 4096), jnp.float32),
             jax.ShapeDtypeStruct((8, 128), jnp.float32),
+            jax.ShapeDtypeStruct((4,) + factors.shape, jnp.bfloat16),
         ),
-        in_specs=[VMEM, VMEM],
-        out_specs=[VMEM, VMEM],
+        in_specs=[VMEM, VMEM, ANY],
+        out_specs=[VMEM, VMEM, ANY],
         scratch_shapes=[
+            DMA((4,)), DMA((4,)),
             pltpu.VMEM((4, 8, 4096), jnp.bfloat16), pltpu.VMEM((4, 8, 4096), jnp.bfloat16),
             DMA((4,)), DMA((4,)),
             pltpu.VMEM((4, 8, 128), jnp.float32), pltpu.VMEM((4, 8, 128), jnp.float32),
@@ -390,9 +402,9 @@
         ]
         + PlaneScatter.scratch((4, 8, 4096))
         + PlaneScatter.scratch((4, 8, 128), jnp.float32),
-        compiler_params=params(5),
+        compiler_params=params(5, 20),
         name="scatter_pull",
-    )(pull, sums)
+    )(pull, sums, factors)
 
 
 def gather_head(head_grad):
@@ -429,7 +441,7 @@
         in_specs=[ANY],
         out_specs=[ANY] * 2,
         scratch_shapes=[DMA((32,)), DMA((32,)), DMA((4,)), DMA((4,))],
-        compiler_params=params(2),
+        compiler_params=params(2, 4),
         name="gather_head",
     )(head_grad)
     return out.reshape(256, 4096), head_x
@@ -459,7 +471,7 @@
         out_specs=[VMEM, ANY, ANY],
         scratch_shapes=[DMA((32,)), DMA((32,)), DMA((4,)), DMA((4,))]
         + PlaneScatter.scratch((256, 128)),
-        compiler_params=params(3),
+        compiler_params=params(3, 12),
         name="finish_links",
     )(partial, acts, head_x)
 
@@ -507,18 +519,27 @@
     slot_cap = request_rows.shape[2]
     rows, width = positive_keys.shape
 
-    slot_ids = lax.broadcasted_iota(jnp.int32, (1, 1, owners * slot_cap), 2)
-    used = jnp.any(negative_slots[:, :, None] == slot_ids, axis=1).astype(jnp.int32)
-    ranks = lax.broadcasted_iota(jnp.int32, used.shape, 0) + 1
-    user = (jnp.sum(used * ranks, axis=0) - 1).reshape(owners, slot_cap)
-    user = lax.all_to_all(user, ("dp", "fsdp"), split_axis=0, concat_axis=0, tiled=True)
-    row_table = request_rows[:, 0, :]
-    live = lax.broadcasted_iota(jnp.int32, row_table.shape, 1) < request_counts
-    codes = jnp.where(live & (user >= 0), row_table + span_index.shape[0] * user, -1)
-    codes = codes.reshape(dp_count, fsdp_count, slot_cap).transpose(1, 0, 2)
-    codes = codes.reshape(owners, slot_cap)
-
-    whole_input = gather_input(mlp_input)
+    shape = (1, 1, slot_cap, owners)
+    slot_ids = lax.broadcasted_iota(jnp.int32, shape, 3) * slot_cap
+    slot_ids += lax.broadcasted_iota(jnp.int32, shape, 2)
+    used = jnp.any(negative_slots[:, :, None, None] == slot_ids, axis=1).astype(jnp.int32)
+    table = jnp.sum(used * (lax.broadcasted_iota(jnp.int32, used.shape, 0) + 1), axis=0) - 1
+    whole_input, tables = gather_input(mlp_input, table)
+
+    me = lax.axis_index("dp") * fsdp_count + lax.axis_index("fsdp")
+    mine = lax.broadcasted_iota(jnp.int32, tables.shape, 3) == me
+    user = jnp.sum(jnp.where(mine, tables, 0), axis=3).reshape(owners, slot_cap)
+    requests = jnp.where(
+        lax.broadcasted_iota(jnp.int32, (owners, slot_cap), 1) < request_counts,
+        request_rows[:, 0, :],
+        -1,
+    )
+    requests = requests.reshape(dp_count, fsdp_count, slot_cap).transpose(1, 0, 2)
+    requests = requests.reshape(owners, slot_cap)
+    codes = jnp.where(
+        (requests >= 0) & (user >= 0), requests + span_index.shape[0] * user, -1
+    )
+
     gate_act = jnp.dot(whole_input, gate_weight, preferred_element_type=jnp.float32)
     up_act = jnp.dot(whole_input, up_weight, preferred_element_type=jnp.float32)
     sigmoid_gate = jax.nn.sigmoid(gate_act)
@@ -538,9 +559,11 @@
     pull, exps, inners = owner_sums(all_units, span_index, codes)
     lanes = lax.broadcasted_iota(jnp.int32, (exps.shape[0], 128), 1)
     sums = jnp.where(lanes == 0, exps[:, None], jnp.where(lanes == 1, inners[:, None], 0.0))
-    pull, sums = scatter_pull(
+    gate_factor = up_act * (sigmoid_gate * (1.0 + gate_act * (1.0 - sigmoid_gate)))
+    pull, sums, factors_x = scatter_pull(
         pull.reshape(fsdp_count, dp_count, rows, width),
         sums.reshape(fsdp_count, dp_count, rows, 128),
+        jnp.stack([gate_factor.T, silu_gate.T]).astype(jnp.bfloat16),
     )
     positive_weight = jnp.exp(positive_score)
     exp_total = sums[:, 0] + positive_weight
@@ -554,26 +577,29 @@
     hidden_grad = lax.dot_general(
         gathered_grad, down_weight, contract_last, preferred_element_type=jnp.float32
     )
-    silu_slope = sigmoid_gate * (1.0 + gate_act * (1.0 - sigmoid_gate))
-    gate_grad_act = (hidden_grad * up_act * silu_slope).astype(jnp.bfloat16)
+    gate_grad_act = (hidden_grad * gate_factor).astype(jnp.bfloat16)
     up_grad_act = (hidden_grad * silu_gate).astype(jnp.bfloat16)
     input_term = lax.dot_general(
         gate_grad_act, gate_weight, contract_last, preferred_element_type=jnp.float32
     ) + lax.dot_general(up_grad_act, up_weight, contract_last, preferred_element_type=jnp.float32)
-    input_grad, acts_x, head_cols = finish_links(
-        input_term.astype(jnp.bfloat16),
-        jnp.concatenate([gate_grad_act.T, up_grad_act.T], axis=0),
-        head_x,
-    )
-    units = gate_weight.shape[1]
+    input_grad, hidden_grad_x, head_cols = finish_links(
+        input_term.astype(jnp.bfloat16), hidden_grad.T.astype(jnp.bfloat16), head_x
+    )
     over_groups = (((0, 2), (0, 1)), ((), ()))
+    hidden_grad_x = hidden_grad_x.astype(jnp.float32)
+    weight_grads = [
+        lax.dot_general(
+            (hidden_grad_x * factors_x[:, k].astype(jnp.float32)).astype(jnp.bfloat16),
+            input_x,
+            over_groups,
+            preferred_element_type=jnp.float32,
+        ).astype(jnp.bfloat16)
+        for k in range(2)
+    ]
     down_grad = lax.dot_general(
         hidden_x, head_cols.reshape(4, 256, 1024), over_groups, preferred_element_type=jnp.float32
     ).astype(jnp.bfloat16)
-    both = lax.dot_general(
-        acts_x, input_x, over_groups, preferred_element_type=jnp.float32
-    ).astype(jnp.bfloat16)
-    return (query_loss, input_grad, both[:units].T, both[units:].T, down_grad)
+    return (query_loss, input_grad, weight_grads[0].T, weight_grads[1].T, down_grad)
 
 
 def solution(mesh):

time: 252 us -> 241 us (0.956)
  starting transfers between devices: 12 us -> 0 us
  other arithmetic: 4.7 us -> 11.8 us
  Pallas kernels: 186 us -> 179 us
    all_to_all x1 -> x0, starting transfers between devices: 12 us -> none  [shards(): lax.all_to_all(user, ('dp', 'fsdp'), split_axis=0, concat_axis=0, tiled=T...]
    pallas_call x1, Pallas kernels: 17.6 us -> 23.1 us  [gather_input(): pl.pallas_call(kernel, out_shape=(jax.ShapeDtypeStruct((rows, cols * 32),...]
    pallas_call x1, Pallas kernels: 22.3 us -> 18 us  [gather_head(): pl.pallas_call(kernel, out_shape=(bf(32, 8, 4096), bf(4, 8, 1024)), in_sp...]
    pallas_call x1, Pallas kernels: 56.1 us -> 52.4 us  [scatter_pull(): pl.pallas_call(kernel, out_shape=(jax.ShapeDtypeStruct((8, 4096), jnp.flo...]
    unnamed x40 -> x50, local copies, waits for them, and re-layouts: 9.27 us -> 10.7 us
  transfers between devices with their start and end apart: 1 -> 0, of which waited for: 0 -> 0; matrix products, arithmetic and copies ran while one was open for 3% -> 0% of each run, Pallas kernels for 31% -> 0%
where the time goes in v4:
time: 241 us
  Pallas kernels  179 us (74%)
  matrix products  35.5 us (15%)
  local copies, waits for them, and re-layouts  13.2 us (5%)
  other arithmetic  11.8 us (5%)
    pallas_call x1, Pallas kernels, scatter_pull(): pl.pallas_call(kernel, out_shape=(jax.ShapeDtypeStruct((8, 4096), jnp.flo...  52.4 us
    pallas_call x1, Pallas kernels, gather_queries(): pl.pallas_call(kernel, out_shape=(bf(32, 4, 8, 4096), bf(4, 8, 4096), bf(...  41.1 us
    pallas_call x1, Pallas kernels, finish_links(): pl.pallas_call(kernel, out_shape=(bf(256, 128), bf(4, *acts.shape), bf(4,...  28.6 us
    pallas_call x1, Pallas kernels, gather_input(): pl.pallas_call(kernel, out_shape=(jax.ShapeDtypeStruct((rows, cols * 32),...  23.1 us
    pallas_call x1, Pallas kernels, gather_head(): pl.pallas_call(kernel, out_shape=(bf(32, 8, 4096), bf(4, 8, 1024)), in_sp...  18 us
    pallas_call x1, Pallas kernels, scatter_branch(): pl.pallas_call(kernel, out_shape=jax.ShapeDtypeStruct((8, 4096), jnp.floa...  15.8 us
    unnamed x50, local copies, waits for them, and re-layouts  10.7 us
    dot_general x1, matrix products, owner_sums(): jnp.dot((weights * key_scale[None, :]).astype(jnp.bfloat16), span_index,...  10.3 us

profile of v4, /device:TPU:1, one launch (start us, length us, event | category | flops | bytes accessed | tf_op | source)
XLA Modules:
  0.0 240.6 jit_solution(8563377033013622722)
XLA Ops:
  0.6 1.0 fusion.32
  1.6 1.4 compare_reduce_fusion
  3.1 0.1 select_reduce_fusion.1
  3.1 0.8 copy-done.1
  4.0 23.1 %gather_input.1 = (bf16[256,4096]{1,0:T(8,128)(2,1)S(1)}, s32[4,8,128]{2,1,0:T(8,128)}, s32[32,4,8,128]{3,2,1,0:T(8,128)S(1)}) custom-call(bf16[256,128]{1,0:T(8,128)(2,1)S(1)} %copy-done.1, s32[8,128]{1,0:T(8,128)S(1)} %broadcast_add_fusion.tab), custom_call_target="tpu_custom_call" | custom-call | tf_op jit(solution)/shard_map/gather_input/pallas_call | solution.py:260
  27.1 3.3 %fusion.47 = f32[256,448]{0,1:T(8,128)S(1)} fusion(bf16[256,4096]{1,0:T(8,128)(2,1)S(1)} %get-tuple-element.19.inp, bf16[4096,448]{0,1:T(8,128)(2,1)} %param.13), kind=kOutput, calls=%fused_computation.106 | convolution fusion | flops 939524096 | bytes 6225920 | tf_op jit(solution)/shard_map/dot_general | solution.py:544
  30.5 1.1 fusion.46
  31.6 1.0 copy-done.21
  32.7 1.3 convolution_bitcast_fusion.src
  34.0 15.8 %scatter_branch.1 = f32[8,4096]{1,0:T(8,128)S(1)} custom-call(bf16[32,8,4096]{2,1,0:T(8,128)(2,1)S(1)} %convolution_bitcast_fusion.src), custom_call_target="tpu_custom_call" | custom-call | tf_op jit(solution)/shard_map/scatter_branch/pallas_call | solution.py:280
  49.9 0.1 multiply_reduce_fusion.3
  50.0 0.2 fusion.44
  50.3 0.6 copy-done.19
  50.8 0.1 copy.34
  50.9 3.1 %multiply_reduce_fusion = f32[512]{0:T(512)S(1)} fusion(bf16[512,4096]{1,0:T(8,128)(2,1)} %param.15), kind=kLoop, calls=%fused_computation | loop fusion | flops 6290944 | bytes 4196352 | tf_op jit(solution)/shard_map/reduce_sum | solution.py:482
  54.0 0.6 broadcast_multiply_fusion
  54.6 2.3 select_reduce_fusion
  56.9 0.1 squeeze.4
  57.0 0.1 copy.33
  57.1 0.5 broadcast.180
  57.6 0.7 reduce.27
  58.3 0.1 lt.11
  58.4 0.1 copy.32
  58.5 0.1 fusion.36
  58.6 0.4 slice_reduce_fusion.7
  59.0 0.1 eq.196
  59.1 0.1 eq.190
  59.2 0.1 eq.191
  59.3 0.1 eq.185
  59.4 0.1 eq.186
  59.5 0.1 eq.180
  59.6 0.1 eq.181
  59.7 0.1 eq.175
  59.8 0.1 eq.176
  59.9 0.1 eq.170
  59.9 0.1 eq.171
  60.1 0.1 eq.166
  60.2 0.1 iota.137
  60.4 0.1 eq.161
  60.5 0.9 fusion.31
  61.4 41.1 %gather_queries.1 = (bf16[32,4,8,4096]{3,2,1,0:T(8,128)(2,1)S(1)}, bf16[4,8,4096]{2,1,0:T(8,128)(2,1)}, bf16[4,448,256]{2,1,0:T(8,128)(2,1)S(1)}, bf16[4,256,1024]{2,1,0:T(8,128)(2,1)S(1)}) custom-call(bf16[8,4096]{1,0:T(8,128)(2,1)S(1)} %get-tuple-element.48.unit, bf16[448,256]{1,0:T(8,128)(2,1)S(1)} %get-tuple-element.46.hid, ...), custom_call_target="tpu_custom_call" | custom-call | tf_op jit(solution)/shard_map/gather_queries/pallas_call | solution.py:335
  102.5 1.4 copy-done.2
  103.9 0.9 copy-done.4
  104.9 9.1 %fusion.45 = (f32[1024]{0:T(1024)S(1)}, f32[1024]{0:T(1024)S(1)}, f32[1024,512]{0,1:T(8,128)S(1)}) fusion(f32[512]{0:T(512)} %get-tuple-element.50, s32[1024]{0:T(1024)S(1)} %eq.196, s32[1024]{0:T(1024)S(1)} %eq.191, s32[1024]{0:T(1024)S(1)} %eq.186, s32[1024]{0:T(1024)S(1)} %eq.181, s32[1024]{0:T(1024)S(1)} %eq.176, s32[1024]{0:T(1024)S(1)} %eq.171, ...), kind=kOutput, calls=%fused_computation.104 | convolution fusion | flops 4310169600 | bytes 14727168 | tf_op jit(solution)/shard_map/dot_general | solution.py:483
  114.0 10.3 %fusion.17 = bf16[1024,4096]{1,0:T(8,128)(2,1)} fusion(bf16[512,4096]{1,0:T(8,128)(2,1)S(1)} %copy-done.8, f32[512]{0:T(512)S(1)} %copy-done.18, f32[1024,512]{0,1:T(8,128)S(1)} %get-tuple-element.52, f32[512]{0:T(512)S(1)} %copy-done.17, s32[1024]{0:T(1024)S(1)} %eq.196, s32[1024]{0:T(1024)S(1)} %eq.191, s32[1024]{0:T(1024)S(1)} %eq.186, ...), kind=kOutput, calls=%fused_computation.28 | convolution fusion | flops 4309647360 | bytes 14721024 | tf_op jit(solution)/shard_map/dot_general | solution.py:496
  124.4 0.1 broadcast_in_dim.51
  124.5 0.1 broadcast_in_dim.49
  124.6 0.3 select_select_fusion.sums_ref
  125.0 3.4 %copy-done = bf16[1024,4096]{1,0:T(8,128)(2,1)S(1)} copy-done((bf16[1024,4096]{1,0:T(8,128)(2,1)S(1)}, bf16[1024,4096]{1,0:T(8,128)(2,1)}, u32[]{:S(2)}) %copy-start) | copy-done | bytes 8388632
  128.4 52.4 %scatter_pull.1 = (f32[8,4096]{1,0:T(8,128)S(1)}, f32[8,128]{1,0:T(8,128)S(1)}, bf16[4,2,448,256]{3,2,1,0:T(8,128)(2,1)S(1)}) custom-call(bf16[32,4,8,4096]{3,2,1,0:T(8,128)(2,1)S(1)} %bitcast.100, f32[32,4,8,128]{3,2,1,0:T(8,128)S(1)} %select_select_fusion.sums_ref, bf16[2,448,256]{2,1,0:T(8,128)(2,1)S(1)} %pad_maximum_fusion.fac), custom_call_target="tpu_custom_call" | custom-call | tf_op jit(solution)/shard_map/scatter_pull/pallas_call | solution.py:387
  180.9 0.2 fusion.40
  181.1 0.5 log_subtract_fusion
  181.6 0.1 divide_convert_fusion.head
  181.7 18.0 %gather_head.1 = (bf16[32,8,4096]{2,1,0:T(8,128)(2,1)S(1)}, bf16[4,8,1024]{2,1,0:T(8,128)(2,1)S(1)}) custom-call(bf16[8,4096]{1,0:T(8,128)(2,1)S(1)} %divide_convert_fusion.head), custom_call_target="tpu_custom_call" | custom-call | tf_op jit(solution)/shard_map/gather_head/pallas_call | solution.py:438
  199.7 1.3 fusion.3
  201.0 0.7 copy-done.7
  201.7 1.4 fusion.29
  203.2 0.6 copy-done.9
  203.8 1.3 fusion.src
  205.2 28.6 %finish_links.1 = (bf16[256,128]{1,0:T(8,128)(2,1)S(1)}, bf16[4,448,256]{2,1,0:T(8,128)(2,1)S(1)}, bf16[4,32,8,1024]{3,2,1,0:T(8,128)(2,1)S(1)}) custom-call(bf16[256,4096]{1,0:T(8,128)(2,1)S(1)} %fusion.src, bf16[448,256]{1,0:T(8,128)(2,1)S(1)} %convert_bitcast_fusion.act, bf16[4,8,1024]{2,1,0:T(8,128)(2,1)S(1)} %get-tuple-element.24.hx), custom_call_target="tpu_custom_call" | custom-call | tf_op jit(solution)/shard_map/finish_links/pallas_call | solution.py:467
  233.8 2.1 bitcast_convert_fusion.2
  235.9 2.1 bitcast_convert_fusion.1
  238.0 2.0 bitcast_convert_fusion
  240.0 0.6 copy.45
  (55 shorter events, 0.4 us)
Async XLA Ops:
  3.1 0.8 copy-start.1
  27.1 3.4 %copy-start.6 = (bf16[4096,448]{0,1:T(8,128)(2,1)S(1)}, bf16[4096,448]{0,1:T(8,128)(2,1)}, u32[]{:S(2)}) copy-start(bf16[4096,448]{0,1:T(8,128)(2,1)} %param.12) | copy-start | bytes 11010052
  30.5 1.2 copy-start.10
  30.5 2.2 copy-start.21
  34.0 15.8 %copy-start.13 = (bf16[8,4096]{1,0:T(8,128)(2,1)S(1)}, bf16[8,4096]{1,0:T(8,128)(2,1)}, u32[]{:S(2)}) copy-start(bf16[8,4096]{1,0:T(8,128)(2,1)} %param.11) | copy-start | bytes 196612
  34.0 16.0 %copy-start.14 = (bf16[8,4096]{1,0:T(8,128)(2,1)S(1)}, bf16[8,4096]{1,0:T(8,128)(2,1)}, u32[]{:S(2)}) copy-start(bf16[8,4096]{1,0:T(8,128)(2,1)} %param.16) | copy-start | bytes 196612
  50.3 0.6 copy-start.19
  50.9 6.0 %copy-start.16 = (s32[128,1,8]{0,2,1:T(8,128)S(1)}, s32[128,1,8]{0,2,1:T(8,128)}, u32[]{:S(2)}) copy-start(s32[128,1,8]{0,2,1:T(8,128)} %param.17) | copy-start | bytes 12292
  50.9 6.7 %copy-start.23 = (s32[128,1]{0,1:T(1,128)S(1)}, s32[128,1]{0,1:T(1,128)}, u32[]{:S(2)}) copy-start(s32[128,1]{0,1:T(1,128)} %param.18) | copy-start | bytes 1540
  56.9 3.6 %copy-start.11 = (f32[256,448]{0,1:T(8,128)S(1)}, f32[256,448]{0,1:T(8,128)}, u32[]{:S(2)}) copy-start(f32[256,448]{0,1:T(8,128)} %copy-done.10) | copy-start | bytes 1376260
  102.5 1.4 copy-start.2
  103.9 0.9 copy-start.4
  104.8 9.1 %copy-start.8 = (bf16[512,4096]{1,0:T(8,128)(2,1)S(1)}, bf16[512,4096]{1,0:T(8,128)(2,1)}, u32[]{:S(2)}) copy-start(bf16[512,4096]{1,0:T(8,128)(2,1)} %param.15) | copy-start | bytes 12582916
  104.8 9.2 %copy-start.17 = (f32[512]{0:T(512)S(1)}, f32[512]{0:T(512)}, u32[]{:S(2)}) copy-start(f32[512]{0:T(512)} %get-tuple-element.50) | copy-start | bytes 6148
  104.8 9.2 %copy-start.18 = (f32[512]{0:T(512)S(1)}, f32[512]{0:T(512)}, u32[]{:S(2)}) copy-start(f32[512]{0:T(512)} %get-tuple-element.51) | copy-start | bytes 6148
  114.0 10.9 %copy-start.12 = (bf16[1,448,256]{2,1,0:T(8,128)(2,1)S(1)}, bf16[1,448,256]{2,1,0:T(8,128)(2,1)}, u32[]{:S(2)}) copy-start(bf16[1,448,256]{2,1,0:T(8,128)(2,1)} %get-tuple-element.47) | copy-start | bytes 688132
  125.0 3.4 %copy-start = (bf16[1024,4096]{1,0:T(8,128)(2,1)S(1)}, bf16[1024,4096]{1,0:T(8,128)(2,1)}, u32[]{:S(2)}) copy-start(bf16[1024,4096]{1,0:T(8,128)(2,1)} %fusion.17) | copy-start | bytes 25165828
  128.4 52.7 %copy-start.20 = (f32[8]{0:T(128)S(1)}, f32[8]{0:T(128)}, u32[]{:S(2)}) copy-start(f32[8]{0:T(128)} %copy-done.19) | copy-start | bytes 100
  128.4 53.2 %copy-start.15 = (bf16[8,4096]{1,0:T(8,128)(2,1)S(1)}, bf16[8,4096]{1,0:T(8,128)(2,1)}, u32[]{:S(2)}) copy-start(bf16[8,4096]{1,0:T(8,128)(2,1)} %param.16) | copy-start | bytes 196612
  128.4 71.3 %copy-start.22 = (bf16[448,4096]{1,0:T(8,128)(2,1)S(1)}, bf16[448,4096]{1,0:T(8,128)(2,1)}, u32[]{:S(2)}) copy-start(bf16[448,4096]{1,0:T(8,128)(2,1)} %param.14) | copy-start | bytes 11010052
  199.7 2.0 copy-start.7
  201.7 2.0 copy-start.9
  205.1 28.7 %copy-start.3 = (bf16[4,256,1024]{2,1,0:T(8,128)(2,1)S(1)}, bf16[4,256,1024]{2,1,0:T(8,128)(2,1)}, u32[]{:S(2)}) copy-start(bf16[4,256,1024]{2,1,0:T(8,128)(2,1)} %copy-done.2) | copy-start | bytes 6291460
  235.9 2.1 copy-start.5

commit v5 on v4

--- a/solution.py
+++ b/solution.py
@@ -288,23 +288,184 @@
     )(partial.reshape(32, 8, 4096))
 
 
-def gather_queries(unit_rows, hidden, whole_input):
-    def kernel(unit, hid, inp, out, unit_x, hid_x, inp_x, send, recv, u_send, u_recv,
-               h_send, h_recv, i_send, i_recv, pair_send, pair_recv):
-        place = Place()
-        p = place
+def near_order(m):
+    return m + m // 2 - 2 * (m // 3)
+
+
+def owner_block(rows, query_ref, index_ref, scale_ref, code_ref, pull_ref, sums_ref):
+    count = rows.size
+    raw = lax.dot_general(
+        query_ref[rows, :], index_ref[...], contract_last, preferred_element_type=jnp.float32
+    )
+    scale = scale_ref[...]
+    scores = inverse_temp * raw * scale
+    here = lax.broadcasted_iota(jnp.int32, scores.shape, 1)
+    uses = jnp.zeros(scores.shape, jnp.float32)
+    codes = code_ref[rows, :]
+    for slot in range(8):
+        uses += jnp.where(codes[:, slot : slot + 1] == here, 1.0, 0.0)
+    weights = uses * jnp.exp(scores)
+    exps = jnp.sum(weights, axis=1, keepdims=True)
+    inners = jnp.sum(weights * scores, axis=1, keepdims=True)
+    lane = lax.broadcasted_iota(jnp.int32, (count, 128), 1)
+    sums_ref[rows, :] = jnp.where(lane == 0, exps, jnp.where(lane == 1, inners, 0.0))
+    weights = (weights * scale).astype(jnp.bfloat16)
+    for part in range(4):
+        cols = pl.ds(part * 1024, 1024)
+        pull_ref[rows, cols] = jnp.dot(
+            weights, index_ref[:, cols], preferred_element_type=jnp.float32
+        ).astype(jnp.bfloat16)
+
+
+class AllSum:
+    def __init__(self, place, src, scratch):
+        self.place, self.src = place, src
+        (self.got1, self.sum1, self.got2, self.sum2, self.got3, self.stage, self.got4, self.send1,
+         self.recv1, self.send2, self.recv2, self.send3, self.recv3, self.send4,
+         self.recv4) = scratch
+
+    @staticmethod
+    def scratch(width, dtype):
+        wide = lambda *lead: pltpu.VMEM(lead + (32, width), dtype)
+        last = pltpu.VMEM((4, 8, width), dtype)
+        return [wide(16), wide(4, 4), wide(4, 4), wide(4), wide(4), last, last,
+                DMA((16,)), DMA((16,))] + [DMA((4,))] * 6
+
+    def rows(self, k, c):
+        return self.src.at[pl.ds(pl.multiple_of(k * 64 + c * 32, 32), 32), :]
+
+    def to_partner(self, k):
+        p = self.place
+        return copy_to(self.rows(k, 1 - p.c), self.got1.at[k], self.send1.at[k], self.recv1.at[k],
+                       p.x, p.partner)
+
+    def to_b(self, i):
+        p = self.place
+        return copy_to(self.sum1.at[(p.b + i) % 4], self.got2.at[p.b], self.send2.at[i],
+                       self.recv2.at[p.b], p.x, p.b_peer(i))
+
+    def to_a(self, j):
+        p = self.place
+        return copy_to(self.sum2.at[(p.a + j) % 4], self.got3.at[p.a], self.send3.at[j],
+                       self.recv3.at[p.a], p.x, p.a_peer(j))
+
+    def to_x(self, j):
+        p = self.place
+        x = (p.x + j) % 4
+        return copy_to(self.stage.at[x], self.got4.at[p.x], self.send4.at[j], self.recv4.at[p.x],
+                       x, p.f)
+
+    def group(self, i):
+        p = self.place
+        b = (p.b + i) % 4
+
+        def add(a, carry):
+            k = p.at(b, a, p.c) // 2
+            got = self.got1.at[k]
+            copy_to(got, got, self.send1.at[k], self.recv1.at[k], p.x, p.partner).wait_recv()
+            own = self.rows(k, p.c)[...].astype(jnp.float32)
+            self.sum1[b, a] = (own + got[...].astype(jnp.float32)).astype(self.sum1.dtype)
+            return carry
+
+        lax.fori_loop(0, 4, add, 0)
+        if i:
+            self.to_b(i).start()
+
+    def second(self):
+        p = self.place
+        for i in near_first:
+            got = self.got2.at[(p.b + i) % 4]
+            copy_to(got, got, self.send2.at[i], self.recv2.at[(p.b + i) % 4], p.x,
+                    p.b_peer(i)).wait_recv()
+        for j in (2, 1, 3, 0):
+            a = (p.a + j) % 4
+            total = self.sum1[p.b, a].astype(jnp.float32)
+            for i in near_first:
+                total += self.got2[(p.b + i) % 4, a].astype(jnp.float32)
+            self.sum2[a] = total.astype(self.sum2.dtype)
+            if j:
+                self.to_a(j).start()
+
+    def third(self):
+        p = self.place
+        total = self.sum2[p.a].astype(jnp.float32)
+        for j in near_first:
+            a = (p.a + j) % 4
+            got = self.got3.at[a]
+            copy_to(got, got, self.send3.at[j], self.recv3.at[a], p.x, p.a_peer(j)).wait_recv()
+            total += got[...].astype(jnp.float32)
+        for x in range(4):
+            self.stage[x] = total[8 * x : 8 * x + 8].astype(self.stage.dtype)
+        for j in near_first:
+            self.to_x(j).start()
+
+    def last(self):
+        p = self.place
+        own = self.stage[p.x].astype(jnp.float32)
+        for j in near_first:
+            x = (p.x + j) % 4
+            got = self.got4.at[x]
+            copy_to(got, got, self.send4.at[j], self.recv4.at[x], x, p.f).wait_recv()
+            own += got[...].astype(jnp.float32)
+        for j in near_first:
+            self.to_b(j).wait_send()
+            self.to_a(j).wait_send()
+            self.to_x(j).wait_send()
+
+        def sent(k, carry):
+            self.to_partner(k).wait_send()
+            return carry
+
+        lax.fori_loop(0, 16, sent, 0)
+        return own
+
+
+def attend(unit_rows, span_index, key_scale, codes, hidden, factors, whole_input):
+    n = 15
+
+    def kernel(unit, index, scale, code, hid, fac, inp,
+               pull_out, sums_out, hid_x, fac_x, inp_x,
+               unit_x, query, pull, sums, u_send, u_recv, a_send, b_send, d_send, recv,
+               h_send, h_recv, f_send, f_recv, i_send, i_recv, pair_send, pair_recv, *scratch):
+        p = place = Place()
         meet(place, True)
+
         finish_unit = across_gather(place, unit, unit_x, u_send, u_recv)
-        finish_unit()
-        gather = PlaneGather(place, unit_x, out, row_block, send, recv)
-        gather.start()
+        block = lambda f: query.at[pl.ds(pl.multiple_of(f * 32, 32), 32), :]
         half = lambda c: pl.ds(pl.multiple_of(c * 512, 512), 512)
         own_i = pltpu.make_async_copy(
             inp.at[:, pl.ds(pl.multiple_of(p.x * 1024, 1024), 1024)], inp_x.at[p.x], i_send.at[0]
         )
         own_i.start()
+        finish_unit()
+        block(p.f)[...] = jnp.concatenate(
+            [unit_x[x].astype(jnp.float32) for x in range(4)], axis=0
+        ).astype(jnp.bfloat16)
+
+        def push(origin, f, send):
+            copy = copy_to(block(origin), block(origin), send, recv.at[origin], p.x, f)
+            copy.start()
+            return copy
+
+        def arrive(origin):
+            copy_to(block(origin), block(origin), d_send.at[origin], recv.at[origin], p.x,
+                    p.partner).wait_recv()
+
         sent = []
+        for j in near_first:
+            sent.append(push(p.f, p.a_peer(j), a_send.at[j]))
+        for j in near_first:
+            sent.append(push(p.f, p.b_peer(j), b_send.at[j]))
+        push(p.f, p.partner, d_send.at[p.f])
+        for j in near_first:
+            origin = p.a_peer(j)
+            arrive(origin)
+            for i in near_first:
+                sent.append(push(origin, p.b_peer(i), b_send.at[4 * j + i]))
+            push(origin, p.partner, d_send.at[origin])
+
         finish_hidden = across_gather(place, hid, hid_x, h_send, h_recv)
+        finish_factors = across_gather(place, fac, fac_x, f_send, f_recv)
         for j in near_first:
             x = (p.x + j) % 4
             copy = copy_to(
@@ -313,8 +474,46 @@
             )
             copy.start()
             sent.append(copy)
-        gather.relay()
-        gather.finish()
+
+        first = AllSum(place, pull, scratch[:n])
+        second = AllSum(place, sums, scratch[n:])
+
+        for stage, group in enumerate((None, 1, 3, 2)):
+
+            def chip(turn, carry):
+                base, other = near_order(stage), near_order(stage + turn // 2)
+                swap = turn % 2
+                z = (p.z + base + (other - base) * swap) % 4
+                y = (p.y + base + (other - base) * (1 - swap)) % 4
+                k = z * 4 + y
+                origin = k * 2 + p.c
+
+                def forward():
+                    arrive(origin)
+                    push(origin, p.partner, d_send.at[origin])
+
+                if stage:
+                    forward()
+                else:
+                    pl.when(jnp.logical_and(turn > 1, (swap + p.c) % 2 == 1))(forward)
+                arrive(k * 2 + 1 - p.c)
+                rows = pl.ds(pl.multiple_of(k * 64, 64), 64)
+                owner_block(rows, query, index, scale, code, pull, sums)
+                first.to_partner(k).start()
+                second.to_partner(k).start()
+                return carry
+
+            lax.fori_loop(1, 8 - 2 * stage, chip, 0)
+            if group:
+                first.group(group)
+                second.group(group)
+        first.group(0)
+        second.group(0)
+        first.second()
+        second.second()
+        first.third()
+        second.third()
+
         for j in near_first:
             x = (p.x + j) % 4
             region = inp_x.at[x, :, half(p.c)]
@@ -322,89 +521,51 @@
             copy = copy_to(region, region, pair_send.at[j], pair_recv.at[x], p.x, p.partner)
             copy.start()
             sent.append(copy)
+        finish_hidden()
+        finish_factors()
+        pull_out[...] = first.last()
+        sums_out[...] = second.last()
         for j in near_first:
             x = (p.x + j) % 4
             region = inp_x.at[x, :, half(1 - p.c)]
             copy_to(region, region, pair_send.at[j], pair_recv.at[x], p.x, p.partner).wait_recv()
-        finish_hidden()
         own_i.wait()
         for copy in sent:
             copy.wait_send()
 
+        def pushed(k, carry):
+            origin = k * 2 + p.c
+            copy_to(block(origin), block(origin), d_send.at[origin], recv.at[origin], p.x,
+                    p.partner).wait_send()
+            return carry
+
+        lax.fori_loop(0, 16, pushed, 0)
+
     bf = lambda *shape: jax.ShapeDtypeStruct(shape, jnp.bfloat16)
-    out, _, hid_x, inp_x = pl.pallas_call(
-        kernel,
-        out_shape=(bf(32, 4, 8, 4096), bf(4, 8, 4096), bf(4, *hidden.shape), bf(4, 256, 1024)),
-        in_specs=[ANY] * 3,
-        out_specs=[ANY] * 4,
-        scratch_shapes=[DMA((32,)), DMA((32,))] + [DMA((4,))] * 8,
-        compiler_params=params(4, 4),
-        name="gather_queries",
-    )(unit_rows, hidden, whole_input)
-    return out.reshape(1024, 4096), hid_x, inp_x
-
-
-def across_sum(place, total, stage, got, send, recv):
-    stage[...] = total.astype(stage.dtype)
-    sent = []
-    for j in near_first:
-        x = (place.x + j) % 4
-        copy = copy_to(stage.at[x], got.at[place.x], send.at[j], recv.at[place.x], x, place.f)
-        copy.start()
-        sent.append(copy)
-
-    def finish():
-        own = stage[place.x].astype(jnp.float32)
-        for j in near_first:
-            x = (place.x + j) % 4
-            copy_to(got.at[x], got.at[x], send.at[j], recv.at[x], x, place.f).wait_recv()
-            own += got[x].astype(jnp.float32)
-        for copy in sent:
-            copy.wait_send()
-        return own
-
-    return finish
-
-
-def scatter_pull(pull, sums, factors):
-    n = 11
-
-    def kernel(pull_ref, sums_ref, fac, pull_out, sums_out, fac_x, f_send, f_recv,
-               stage_p, got_p, sp, rp, stage_s, got_s, ss, rs, *scratch):
-        place = Place()
-        meet(place, True)
-        finish_factors = across_gather(place, fac, fac_x, f_send, f_recv)
-        first = PlaneScatter(place, pull_ref, row_block, scratch[:n])
-        second = PlaneScatter(place, sums_ref, row_block, scratch[n:])
-        first.start()
-        second.start()
-        finish_p = across_sum(place, first.middle(), stage_p, got_p, sp, rp)
-        finish_s = across_sum(place, second.middle(), stage_s, got_s, ss, rs)
-        pull_out[...] = finish_p()
-        sums_out[...] = finish_s()
-        finish_factors()
-
     return pl.pallas_call(
         kernel,
         out_shape=(
             jax.ShapeDtypeStruct((8, 4096), jnp.float32),
             jax.ShapeDtypeStruct((8, 128), jnp.float32),
-            jax.ShapeDtypeStruct((4,) + factors.shape, jnp.bfloat16),
+            bf(4, *hidden.shape),
+            bf(4, *factors.shape),
+            bf(4, 256, 1024),
         ),
-        in_specs=[VMEM, VMEM, ANY],
-        out_specs=[VMEM, VMEM, ANY],
+        in_specs=[ANY, VMEM, VMEM, VMEM, ANY, ANY, ANY],
+        out_specs=[VMEM, VMEM, ANY, ANY, ANY],
         scratch_shapes=[
-            DMA((4,)), DMA((4,)),
-            pltpu.VMEM((4, 8, 4096), jnp.bfloat16), pltpu.VMEM((4, 8, 4096), jnp.bfloat16),
-            DMA((4,)), DMA((4,)),
-            pltpu.VMEM((4, 8, 128), jnp.float32), pltpu.VMEM((4, 8, 128), jnp.float32),
-            DMA((4,)), DMA((4,)),
+            pltpu.VMEM((4, 8, 4096), jnp.bfloat16),
+            pltpu.VMEM((1024, 4096), jnp.bfloat16),
+            pltpu.VMEM((1024, 4096), jnp.bfloat16),
+            pltpu.VMEM((1024, 128), jnp.float32),
+            DMA((4,)), DMA((4,)), DMA((4,)), DMA((16,)), DMA((32,)), DMA((32,)),
         ]
-        + PlaneScatter.scratch((4, 8, 4096))
-        + PlaneScatter.scratch((4, 8, 128), jnp.float32),
-        compiler_params=params(5, 20),
-        name="scatter_pull",
-    )(pull, sums, factors)
+        + [DMA((4,))] * 8
+        + AllSum.scratch(4096, jnp.bfloat16)
+        + AllSum.scratch(128, jnp.float32),
+        compiler_params=params(4, 48),
+        name="attend",
+    )(unit_rows, span_index, key_scale, codes, hidden, factors, whole_input)
 
 
 def gather_head(head_grad):
@@ -474,31 +635,6 @@
         compiler_params=params(3, 12),
         name="finish_links",
     )(partial, acts, head_x)
-
-
-def owner_sums(unit_rows, span_index, codes):
-    shard_rows = span_index.shape[0]
-    wide = span_index.astype(jnp.float32)
-    key_scale = lax.rsqrt(jnp.sum(wide * wide, axis=-1) + eps)
-    raw = lax.dot_general(
-        unit_rows, span_index, contract_last, preferred_element_type=jnp.float32
-    )
-    scores = inverse_temp * raw * key_scale[None, :]
-    groups, slots = codes.shape
-    queries = unit_rows.shape[0] // groups
-    here = lax.broadcasted_iota(jnp.int32, (groups, queries, shard_rows), 2)
-    here += shard_rows * lax.broadcasted_iota(jnp.int32, (groups, queries, shard_rows), 1)
-    uses = jnp.zeros(here.shape, jnp.float32)
-    for slot in range(slots):
-        uses += (codes[:, slot][:, None, None] == here).astype(jnp.float32)
-    uses = uses.reshape(raw.shape)
-    weights = uses * jnp.exp(scores)
-    pull = jnp.dot(
-        (weights * key_scale[None, :]).astype(jnp.bfloat16),
-        span_index,
-        preferred_element_type=jnp.bfloat16,
-    )
-    return pull, jnp.sum(weights, axis=-1), jnp.sum(weights * scores, axis=-1)
 
 
 def shards(
@@ -536,9 +672,11 @@
     )
     requests = requests.reshape(dp_count, fsdp_count, slot_cap).transpose(1, 0, 2)
     requests = requests.reshape(owners, slot_cap)
-    codes = jnp.where(
-        (requests >= 0) & (user >= 0), requests + span_index.shape[0] * user, -1
-    )
+    ranks = lax.broadcasted_iota(jnp.int32, (1, rows, 1), 1)
+    codes = jnp.where(user[:, None, :] == ranks, requests[:, None, :], -1)
+    codes = codes.reshape(owners * rows, slot_cap)
+    wide = span_index.astype(jnp.float32)
+    key_scale = lax.rsqrt(jnp.sum(wide * wide, axis=-1) + eps)[None, :]
 
     gate_act = jnp.dot(whole_input, gate_weight, preferred_element_type=jnp.float32)
     up_act = jnp.dot(whole_input, up_weight, preferred_element_type=jnp.float32)
@@ -553,17 +691,15 @@
     positive_unit = positive / jnp.sqrt(jnp.sum(positive * positive, axis=-1, keepdims=True) + eps)
     positive_score = inverse_temp * jnp.sum(unit_rows * positive_unit, axis=-1)
 
-    all_units, hidden_x, input_x = gather_queries(
-        unit_rows.astype(jnp.bfloat16), hidden.T, whole_input
-    )
-    pull, exps, inners = owner_sums(all_units, span_index, codes)
-    lanes = lax.broadcasted_iota(jnp.int32, (exps.shape[0], 128), 1)
-    sums = jnp.where(lanes == 0, exps[:, None], jnp.where(lanes == 1, inners[:, None], 0.0))
     gate_factor = up_act * (sigmoid_gate * (1.0 + gate_act * (1.0 - sigmoid_gate)))
-    pull, sums, factors_x = scatter_pull(
-        pull.reshape(fsdp_count, dp_count, rows, width),
-        sums.reshape(fsdp_count, dp_count, rows, 128),
+    pull, sums, hidden_x, factors_x, input_x = attend(
+        unit_rows.astype(jnp.bfloat16),
+        span_index,
+        key_scale,
+        codes,
+        hidden.T,
         jnp.stack([gate_factor.T, silu_gate.T]).astype(jnp.bfloat16),
+        whole_input,
     )
     positive_weight = jnp.exp(positive_score)
     exp_total = sums[:, 0] + positive_weight

time: 241 us -> 245 us (1.017)
  Pallas kernels: 179 us -> 212 us
  matrix products: 35.5 us -> 16.6 us
  local copies, waits for them, and re-layouts: 13.2 us -> 5.09 us
    pallas_call x2 -> x1, Pallas kernels: 93.6 us -> 120 us  [attend(): pl.pallas_call(kernel, out_shape=(jax.ShapeDtypeStruct((8, 4096), jnp.flo...]
    dot_general x2 -> x0, matrix products: 19.5 us -> none  [the longest x1 10.3 us: owner_sums(): jnp.dot((weights * key_scale[None, :]).astype(jnp.bfloat16), span_index,...]
    unnamed x50 -> x30, local copies, waits for them, and re-layouts: 10.7 us -> 4.56 us
    pallas_call x1, Pallas kernels: 18 us -> 23.6 us  [gather_head(): pl.pallas_call(kernel, out_shape=(bf(32, 8, 4096), bf(4, 8, 1024)), in_sp...]
where the time goes in v5:
time: 245 us
  Pallas kernels  212 us (87%)
  matrix products  16.6 us (7%)
  other arithmetic  10.5 us (4%)
  local copies, waits for them, and re-layouts  5.09 us (2%)
    pallas_call x1, Pallas kernels, attend(): pl.pallas_call(kernel, out_shape=(jax.ShapeDtypeStruct((8, 4096), jnp.flo...  120 us
    pallas_call x1, Pallas kernels, finish_links(): pl.pallas_call(kernel, out_shape=(bf(256, 128), bf(4, *acts.shape), bf(4,...  29 us
    pallas_call x1, Pallas kernels, gather_head(): pl.pallas_call(kernel, out_shape=(bf(32, 8, 4096), bf(4, 8, 1024)), in_sp...  23.6 us
    pallas_call x1, Pallas kernels, gather_input(): pl.pallas_call(kernel, out_shape=(jax.ShapeDtypeStruct((rows, cols * 32),...  23.1 us
    pallas_call x1, Pallas kernels, scatter_branch(): pl.pallas_call(kernel, out_shape=jax.ShapeDtypeStruct((8, 4096), jnp.floa...  15.8 us

profile of v5, /device:TPU:1, one launch (start us, length us, event | category | flops | bytes accessed | tf_op | source)
XLA Modules:
  0.0 244.8 jit_solution(17966499709831548337)
XLA Ops:
  0.6 1.0 fusion.22
  1.6 1.4 compare_reduce_fusion
  3.1 0.1 select_reduce_fusion.1
  3.1 0.0 copy-start.1
  3.1 0.8 copy-done.1
  4.0 23.1 %gather_input.1 = (bf16[256,4096]{1,0:T(8,128)(2,1)S(1)}, s32[4,8,128]{2,1,0:T(8,128)}, s32[32,4,8,128]{3,2,1,0:T(8,128)S(1)}) custom-call(bf16[256,128]{1,0:T(8,128)(2,1)S(1)} %copy-done.1, s32[8,128]{1,0:T(8,128)S(1)} %broadcast_add_fusion.tab), custom_call_target="tpu_custom_call" | custom-call | tf_op jit(solution)/shard_map/gather_input/pallas_call | solution.py:260
  27.1 0.0 copy-start
  27.1 0.0 copy-start.2
  27.1 4.0 %fusion.34 = f32[256,448]{0,1:T(8,128)S(1)} fusion(bf16[256,4096]{1,0:T(8,128)(2,1)S(1)} %get-tuple-element.17.inp, bf16[4096,448]{0,1:T(8,128)(2,1)} %param.13), kind=kOutput, calls=%fused_computation.76 | convolution fusion | flops 939524096 | bytes 6225920 | tf_op jit(solution)/shard_map/dot_general | solution.py:682
  31.1 0.0 copy-done
  31.1 0.0 copy-done.2
  31.1 0.0 copy-start.5
  31.1 0.0 copy-start.10
  31.1 1.1 fusion.33
  32.3 0.0 copy-done.5
  32.3 1.0 copy-done.10
  33.3 1.4 convolution_bitcast_fusion.src
  34.7 0.0 copy-start.7
  34.7 0.0 copy-start.8
  34.7 15.8 %scatter_branch.1 = f32[8,4096]{1,0:T(8,128)S(1)} custom-call(bf16[32,8,4096]{2,1,0:T(8,128)(2,1)S(1)} %convolution_bitcast_fusion.src), custom_call_target="tpu_custom_call" | custom-call | tf_op jit(solution)/shard_map/scatter_branch/pallas_call | solution.py:280
  50.5 0.0 copy-done.7
  50.5 0.2 multiply_reduce_fusion.2
  50.7 0.0 copy-done.8
  50.7 0.2 fusion.32
  50.9 0.1 copy.27
  51.0 0.0 copy-start.9
  51.0 0.0 copy-start.13
  51.0 0.0 copy-start.6
  51.0 3.1 %multiply_reduce_fusion = f32[512]{0:T(512)S(1)} fusion(bf16[512,4096]{1,0:T(8,128)(2,1)} %index.1), kind=kLoop, calls=%fused_computation | loop fusion | flops 6290944 | bytes 4196352 | tf_op jit(solution)/shard_map/reduce_sum | solution.py:679
  54.2 0.0 copy-done.9
  54.2 0.1 squeeze.4
  54.3 0.1 copy.26
  54.4 0.5 broadcast.128
  54.9 0.0 copy-done.13
  54.9 0.7 reduce.11
  55.6 0.1 lt.11
  55.6 0.1 copy.25
  55.7 0.1 fusion.26
  55.9 0.1 eq.51
  56.0 2.3 select_reduce_fusion
  58.2 0.2 bitcast_select_fusion.code
  58.5 0.0 copy-done.6
  58.5 0.3 fusion.21
  58.8 0.0 copy-start.11
  58.8 120.1 %attend.1 = (f32[8,4096]{1,0:T(8,128)S(1)}, f32[8,128]{1,0:T(8,128)S(1)}, bf16[4,448,256]{2,1,0:T(8,128)(2,1)S(1)}, bf16[4,2,448,256]{3,2,1,0:T(8,128)(2,1)S(1)}, bf16[4,256,1024]{2,1,0:T(8,128)(2,1)}) custom-call(bf16[8,4096]{1,0:T(8,128)(2,1)S(1)} %get-tuple-element.36.unit, bf16[512,4096]{1,0:T(8,128)(2,1)} %index.1, f32[1,512]{1,0:T(1,128)S(1)} %bitcast.96, ...), custom_call_target="tpu_custom_call" | custom-call | tf_op jit(solution)/shard_map/attend/pallas_call | solution.py:545
  179.0 0.2 fusion.28
  179.1 0.5 log_subtract_fusion
  179.7 0.1 divide_convert_fusion.head
  179.8 23.6 %gather_head.1 = (bf16[32,8,4096]{2,1,0:T(8,128)(2,1)S(1)}, bf16[4,8,1024]{2,1,0:T(8,128)(2,1)S(1)}) custom-call(bf16[8,4096]{1,0:T(8,128)(2,1)S(1)} %divide_convert_fusion.head), custom_call_target="tpu_custom_call" | custom-call | tf_op jit(solution)/shard_map/gather_head/pallas_call | solution.py:599
  203.4 0.0 copy-done.11
  203.5 0.0 copy-start.3
  203.5 1.1 fusion.3
  204.6 0.9 copy-done.3
  205.5 0.0 copy-start.4
  205.5 1.4 fusion.19
  206.9 0.6 copy-done.4
  207.5 1.4 fusion.src
  208.9 0.0 copy-start.12
  209.0 29.0 %finish_links.1 = (bf16[256,128]{1,0:T(8,128)(2,1)S(1)}, bf16[4,448,256]{2,1,0:T(8,128)(2,1)S(1)}, bf16[4,32,8,1024]{3,2,1,0:T(8,128)(2,1)S(1)}) custom-call(bf16[256,4096]{1,0:T(8,128)(2,1)S(1)} %fusion.src, bf16[448,256]{1,0:T(8,128)(2,1)S(1)} %convert_bitcast_fusion.act, bf16[4,8,1024]{2,1,0:T(8,128)(2,1)S(1)} %get-tuple-element.22.hx), custom_call_target="tpu_custom_call" | custom-call | tf_op jit(solution)/shard_map/finish_links/pallas_call | solution.py:628
  238.0 0.0 copy-done.12
  238.0 2.1 bitcast_convert_fusion.2
  240.1 2.1 bitcast_convert_fusion.1
  242.1 2.0 bitcast_convert_fusion
  244.2 0.6 copy.38
  (11 shorter events, 0.1 us)
Async XLA Ops:
  3.1 0.8 copy-start.1
  27.1 4.0 %copy-start = (bf16[256,4096]{1,0:T(8,128)(2,1)}, bf16[256,4096]{1,0:T(8,128)(2,1)S(1)}, u32[]{:S(2)}) copy-start(bf16[256,4096]{1,0:T(8,128)(2,1)S(1)} %get-tuple-element.17.inp) | copy-start | bytes 6291460
  27.1 4.0 %copy-start.2 = (bf16[4096,448]{0,1:T(8,128)(2,1)S(1)}, bf16[4096,448]{0,1:T(8,128)(2,1)}, u32[]{:S(2)}) copy-start(bf16[4096,448]{0,1:T(8,128)(2,1)} %param.12) | copy-start | bytes 11010052
  31.1 1.2 copy-start.5
  31.1 2.2 copy-start.10
  34.7 15.8 %copy-start.7 = (bf16[8,4096]{1,0:T(8,128)(2,1)S(1)}, bf16[8,4096]{1,0:T(8,128)(2,1)}, u32[]{:S(2)}) copy-start(bf16[8,4096]{1,0:T(8,128)(2,1)} %param.11) | copy-start | bytes 196612
  34.7 16.0 %copy-start.8 = (bf16[8,4096]{1,0:T(8,128)(2,1)S(1)}, bf16[8,4096]{1,0:T(8,128)(2,1)}, u32[]{:S(2)}) copy-start(bf16[8,4096]{1,0:T(8,128)(2,1)} %param.16) | copy-start | bytes 196612
  51.0 3.2 %copy-start.9 = (s32[128,1,8]{0,2,1:T(8,128)S(1)}, s32[128,1,8]{0,2,1:T(8,128)}, u32[]{:S(2)}) copy-start(s32[128,1,8]{0,2,1:T(8,128)} %param.17) | copy-start | bytes 12292
  51.0 3.9 %copy-start.13 = (s32[128,1]{0,1:T(1,128)S(1)}, s32[128,1]{0,1:T(1,128)}, u32[]{:S(2)}) copy-start(s32[128,1]{0,1:T(1,128)} %param.18) | copy-start | bytes 1540
  51.0 7.4 %copy-start.6 = (f32[256,448]{0,1:T(8,128)S(1)}, f32[256,448]{0,1:T(8,128)}, u32[]{:S(2)}) copy-start(f32[256,448]{0,1:T(8,128)} %copy-done.5) | copy-start | bytes 1376260
  58.8 144.7 %copy-start.11 = (bf16[448,4096]{1,0:T(8,128)(2,1)S(1)}, bf16[448,4096]{1,0:T(8,128)(2,1)}, u32[]{:S(2)}) copy-start(bf16[448,4096]{1,0:T(8,128)(2,1)} %param.14) | copy-start | bytes 11010052
  203.5 2.0 copy-start.3
  205.5 2.0 copy-start.4
  208.9 29.0 %copy-start.12 = (bf16[4,256,1024]{2,1,0:T(8,128)(2,1)S(1)}, bf16[4,256,1024]{2,1,0:T(8,128)(2,1)}, u32[]{:S(2)}) copy-start(bf16[4,256,1024]{2,1,0:T(8,128)(2,1)} %get-tuple-element.24) | copy-start | bytes 6291460

commit v6 on v5

--- a/solution.py
+++ b/solution.py
@@ -292,29 +292,23 @@
     return m + m // 2 - 2 * (m // 3)
 
 
-def owner_block(rows, query_ref, index_ref, scale_ref, code_ref, pull_ref, sums_ref):
-    count = rows.size
+def owner_batch(count, batch_ref, code_ref, index_ref, scale_ref, weight_ref):
     raw = lax.dot_general(
-        query_ref[rows, :], index_ref[...], contract_last, preferred_element_type=jnp.float32
+        batch_ref[:count, :], index_ref[...], contract_last, preferred_element_type=jnp.float32
     )
     scale = scale_ref[...]
     scores = inverse_temp * raw * scale
     here = lax.broadcasted_iota(jnp.int32, scores.shape, 1)
     uses = jnp.zeros(scores.shape, jnp.float32)
-    codes = code_ref[rows, :]
+    codes = code_ref[:count, :]
     for slot in range(8):
         uses += jnp.where(codes[:, slot : slot + 1] == here, 1.0, 0.0)
     weights = uses * jnp.exp(scores)
     exps = jnp.sum(weights, axis=1, keepdims=True)
     inners = jnp.sum(weights * scores, axis=1, keepdims=True)
     lane = lax.broadcasted_iota(jnp.int32, (count, 128), 1)
-    sums_ref[rows, :] = jnp.where(lane == 0, exps, jnp.where(lane == 1, inners, 0.0))
-    weights = (weights * scale).astype(jnp.bfloat16)
-    for part in range(4):
-        cols = pl.ds(part * 1024, 1024)
-        pull_ref[rows, cols] = jnp.dot(
-            weights, index_ref[:, cols], preferred_element_type=jnp.float32
-        ).astype(jnp.bfloat16)
+    weight_ref[:count, :] = (weights * scale).astype(jnp.bfloat16)
+    return jnp.where(lane == 0, exps, jnp.where(lane == 1, inners, 0.0))
 
 
 class AllSum:
@@ -420,12 +414,12 @@
         return own
 
 
-def attend(unit_rows, span_index, key_scale, codes, hidden, factors, whole_input):
+def attend(unit_rows, span_index, codes, hidden, factors, whole_input):
     n = 15
 
-    def kernel(unit, index, scale, code, hid, fac, inp,
+    def kernel(unit, index, code, hid, fac, inp,
                pull_out, sums_out, hid_x, fac_x, inp_x,
-               unit_x, query, pull, sums, u_send, u_recv, a_send, b_send, d_send, recv,
+               unit_x, query, pull, sums, batch, batch_code, weight, scale, u_send, u_recv, a_send, b_send, d_send, recv,
                h_send, h_recv, f_send, f_recv, i_send, i_recv, pair_send, pair_recv, *scratch):
         p = place = Place()
         meet(place, True)
@@ -457,6 +451,17 @@
         for j in near_first:
             sent.append(push(p.f, p.b_peer(j), b_send.at[j]))
         push(p.f, p.partner, d_send.at[p.f])
+
+        def norms(part, carry):
+            rows = pl.ds(pl.multiple_of(part * 128, 128), 128)
+            wide = index[rows, :].astype(jnp.float32)
+            total = jnp.sum(wide * wide, axis=1, keepdims=True)
+            row = lax.broadcasted_iota(jnp.int32, (128, 128), 0)
+            col = lax.broadcasted_iota(jnp.int32, (128, 128), 1)
+            across = jnp.sum(jnp.where(row == col, total, 0.0), axis=0, keepdims=True)
+            scale[:, rows] = lax.rsqrt(across + eps)
+            return carry
+
         for j in near_first:
             origin = p.a_peer(j)
             arrive(origin)
@@ -475,36 +480,57 @@
             copy.start()
             sent.append(copy)
 
+        lax.fori_loop(0, index.shape[0] // 128, norms, 0)
         first = AllSum(place, pull, scratch[:n])
         second = AllSum(place, sums, scratch[n:])
 
-        for stage, group in enumerate((None, 1, 3, 2)):
-
-            def chip(turn, carry):
-                base, other = near_order(stage), near_order(stage + turn // 2)
-                swap = turn % 2
-                z = (p.z + base + (other - base) * swap) % 4
-                y = (p.y + base + (other - base) * (1 - swap)) % 4
-                k = z * 4 + y
-                origin = k * 2 + p.c
-
-                def forward():
-                    arrive(origin)
-                    push(origin, p.partner, d_send.at[origin])
-
-                if stage:
-                    forward()
-                else:
-                    pl.when(jnp.logical_and(turn > 1, (swap + p.c) % 2 == 1))(forward)
-                arrive(k * 2 + 1 - p.c)
-                rows = pl.ds(pl.multiple_of(k * 64, 64), 64)
-                owner_block(rows, query, index, scale, code, pull, sums)
+        def chip_of(stage, turn):
+            base, other = near_order(stage), near_order(stage + turn // 2)
+            swap = turn % 2
+            z = (p.z + base + (other - base) * swap) % 4
+            y = (p.y + base + (other - base) * (1 - swap)) % 4
+            return z * 4 + y
+
+        for stages, groups in (((0,), ()), ((1,), (1,)), ((2, 3), (3, 2))):
+            filled = 0
+            for stage in stages:
+                turns = 7 - 2 * stage
+
+                def bring(turn, carry, stage=stage, filled=filled):
+                    k = chip_of(stage, turn)
+                    origin = k * 2 + p.c
+
+                    def forward():
+                        arrive(origin)
+                        push(origin, p.partner, d_send.at[origin])
+
+                    if stage:
+                        forward()
+                    else:
+                        pl.when(jnp.logical_and(turn > 1, (turn + p.c) % 2 == 1))(forward)
+                    arrive(k * 2 + 1 - p.c)
+                    rows = pl.ds(pl.multiple_of(k * 64, 64), 64)
+                    to = pl.ds(pl.multiple_of((filled + turn - 1) * 64, 64), 64)
+                    batch[to, :] = query[rows, :]
+                    batch_code[to, :] = code[rows, :]
+                    return carry
+
+                lax.fori_loop(1, 1 + turns, bring, 0)
+                filled += turns
+            total = owner_batch(filled * 64, batch, batch_code, index, scale, weight)
+            chips = [chip_of(stage, turn) for stage in stages for turn in range(1, 8 - 2 * stage)]
+            for part in range(4):
+                cols = slice(part * 1024, part * 1024 + 1024)
+                result = jnp.dot(
+                    weight[: filled * 64, :], index[:, cols], preferred_element_type=jnp.float32
+                ).astype(jnp.bfloat16)
+                for t, k in enumerate(chips):
+                    pull[pl.ds(pl.multiple_of(k * 64, 64), 64), cols] = result[64 * t : 64 * t + 64]
+            for t, k in enumerate(chips):
+                sums[pl.ds(pl.multiple_of(k * 64, 64), 64), :] = total[64 * t : 64 * t + 64]
                 first.to_partner(k).start()
                 second.to_partner(k).start()
-                return carry
-
-            lax.fori_loop(1, 8 - 2 * stage, chip, 0)
-            if group:
+            for group in groups:
                 first.group(group)
                 second.group(group)
         first.group(0)
@@ -551,21 +577,25 @@
             bf(4, *factors.shape),
             bf(4, 256, 1024),
         ),
-        in_specs=[ANY, VMEM, VMEM, VMEM, ANY, ANY, ANY],
+        in_specs=[ANY, VMEM, VMEM, ANY, ANY, ANY],
         out_specs=[VMEM, VMEM, ANY, ANY, ANY],
         scratch_shapes=[
             pltpu.VMEM((4, 8, 4096), jnp.bfloat16),
             pltpu.VMEM((1024, 4096), jnp.bfloat16),
             pltpu.VMEM((1024, 4096), jnp.bfloat16),
             pltpu.VMEM((1024, 128), jnp.float32),
+            pltpu.VMEM((448, 4096), jnp.bfloat16),
+            pltpu.VMEM((448, 8), jnp.int32),
+            pltpu.VMEM((448, 512), jnp.bfloat16),
+            pltpu.VMEM((1, 512), jnp.float32),
             DMA((4,)), DMA((4,)), DMA((4,)), DMA((16,)), DMA((32,)), DMA((32,)),
         ]
         + [DMA((4,))] * 8
         + AllSum.scratch(4096, jnp.bfloat16)
         + AllSum.scratch(128, jnp.float32),
-        compiler_params=params(4, 48),
+        compiler_params=params(4, 52),
         name="attend",
-    )(unit_rows, span_index, key_scale, codes, hidden, factors, whole_input)
+    )(unit_rows, span_index, codes, hidden, factors, whole_input)
 
 
 def gather_head(head_grad):
@@ -675,8 +705,6 @@
     ranks = lax.broadcasted_iota(jnp.int32, (1, rows, 1), 1)
     codes = jnp.where(user[:, None, :] == ranks, requests[:, None, :], -1)
     codes = codes.reshape(owners * rows, slot_cap)
-    wide = span_index.astype(jnp.float32)
-    key_scale = lax.rsqrt(jnp.sum(wide * wide, axis=-1) + eps)[None, :]
 
     gate_act = jnp.dot(whole_input, gate_weight, preferred_element_type=jnp.float32)
     up_act = jnp.dot(whole_input, up_weight, preferred_element_type=jnp.float32)
@@ -695,7 +723,6 @@
     pull, sums, hidden_x, factors_x, input_x = attend(
         unit_rows.astype(jnp.bfloat16),
         span_index,
-        key_scale,
         codes,
         hidden.T,
         jnp.stack([gate_factor.T, silu_gate.T]).astype(jnp.bfloat16),

time: 245 us -> 227 us (0.927)
  Pallas kernels: 212 us -> 196 us
  other arithmetic: 10.5 us -> 7.31 us
    pallas_call x1, Pallas kernels: 120 us -> 99.7 us  [attend(): pl.pallas_call(kernel, out_shape=(jax.ShapeDtypeStruct((8, 4096), jnp.flo...]
    pallas_call x1, Pallas kernels: 23.6 us -> 26.9 us  [gather_head(): pl.pallas_call(kernel, out_shape=(bf(32, 8, 4096), bf(4, 8, 1024)), in_sp...]
    reduce_sum x1 -> x0, other arithmetic: 3.14 us -> none  [shards(): key_scale = lax.rsqrt(jnp.sum(wide * wide, axis=-1) + eps)[None, :]]
where the time goes in v6:
time: 227 us; the launch traced here: 226 us
  Pallas kernels  196 us (86%)
  matrix products  16.7 us (7%)
  other arithmetic  7.31 us (3%)
  local copies, waits for them, and re-layouts  4.99 us (2%)
    pallas_call x1, Pallas kernels, attend(): pl.pallas_call(kernel, out_shape=(jax.ShapeDtypeStruct((8, 4096), jnp.flo...  99.7 us
    pallas_call x1, Pallas kernels, finish_links(): pl.pallas_call(kernel, out_shape=(bf(256, 128), bf(4, *acts.shape), bf(4,...  30.9 us
    pallas_call x1, Pallas kernels, gather_head(): pl.pallas_call(kernel, out_shape=(bf(32, 8, 4096), bf(4, 8, 1024)), in_sp...  26.9 us
    pallas_call x1, Pallas kernels, gather_input(): pl.pallas_call(kernel, out_shape=(jax.ShapeDtypeStruct((rows, cols * 32),...  23.1 us
    pallas_call x1, Pallas kernels, scatter_branch(): pl.pallas_call(kernel, out_shape=jax.ShapeDtypeStruct((8, 4096), jnp.floa...  15.8 us

profile of v6, /device:TPU:1, one launch (start us, length us, event | category | flops | bytes accessed | tf_op | source)
XLA Modules:
  0.0 226.4 jit_solution(11521896202023009680)
XLA Ops:
  0.6 1.0 fusion.22
  1.6 1.4 compare_reduce_fusion
  3.1 0.1 select_reduce_fusion.1
  3.1 0.0 copy-start.1
  3.1 0.8 copy-done.1
  4.0 23.1 %gather_input.1 = (bf16[256,4096]{1,0:T(8,128)(2,1)S(1)}, s32[4,8,128]{2,1,0:T(8,128)}, s32[32,4,8,128]{3,2,1,0:T(8,128)S(1)}) custom-call(bf16[256,128]{1,0:T(8,128)(2,1)S(1)} %copy-done.1, s32[8,128]{1,0:T(8,128)S(1)} %broadcast_add_fusion.tab), custom_call_target="tpu_custom_call" | custom-call | tf_op jit(solution)/shard_map/gather_input/pallas_call | solution.py:260
  27.1 0.0 copy-start
  27.1 0.0 copy-start.2
  27.1 4.0 %fusion.34 = f32[256,448]{0,1:T(8,128)S(1)} fusion(bf16[256,4096]{1,0:T(8,128)(2,1)S(1)} %get-tuple-element.17.inp, bf16[4096,448]{0,1:T(8,128)(2,1)} %param.13), kind=kOutput, calls=%fused_computation.74 | convolution fusion | flops 939524096 | bytes 6225920 | tf_op jit(solution)/shard_map/dot_general | solution.py:710
  31.1 0.0 copy-done
  31.1 0.0 copy-done.2
  31.1 0.0 copy-start.5
  31.1 0.0 copy-start.10
  31.1 1.1 fusion.33
  32.3 0.0 copy-done.5
  32.3 1.0 copy-done.10
  33.3 1.4 convolution_bitcast_fusion.src
  34.7 0.0 copy-start.7
  34.7 0.0 copy-start.8
  34.7 0.0 copy-start.9
  34.7 0.0 copy-start.15
  34.8 0.0 copy-start.6
  34.8 15.8 %scatter_branch.1 = f32[8,4096]{1,0:T(8,128)S(1)} custom-call(bf16[32,8,4096]{2,1,0:T(8,128)(2,1)S(1)} %convolution_bitcast_fusion.src), custom_call_target="tpu_custom_call" | custom-call | tf_op jit(solution)/shard_map/scatter_branch/pallas_call | solution.py:280
  50.6 0.0 copy-done.7
  50.6 0.1 multiply_reduce_fusion.1
  50.7 0.0 copy-done.8
  50.7 0.2 fusion.32
  51.0 0.1 copy.27
  51.1 0.0 copy-done.9
  51.1 0.1 squeeze.4
  51.1 0.1 copy.26
  51.2 0.5 broadcast.119
  51.8 0.0 copy-done.15
  51.8 0.7 reduce.11
  52.4 0.1 lt.11
  52.5 0.1 copy.25
  52.6 0.1 fusion.26
  52.7 0.1 eq.51
  52.8 2.3 %select_reduce_fusion = s32[32,4,8]{2,1,0:T(4,128)S(1)} fusion(s32[32,4,8,128]{3,2,1,0:T(8,128)S(1)} %get-tuple-element.18, pred[128]{0:T(512)(128)(4,1)S(1)} %iota_compare_fusion.1), kind=kLoop, calls=%fused_computation.19 | loop fusion | flops 261120 | bytes 528512 | tf_op jit(solution)/shard_map/reduce_sum | solution.py:697
  55.1 0.2 bitcast_select_fusion.code
  55.3 0.0 copy-done.6
  55.3 0.3 fusion.21
  55.7 0.0 copy-start.11
  55.7 99.7 %attend.1 = (f32[8,4096]{1,0:T(8,128)S(1)}, f32[8,128]{1,0:T(8,128)S(1)}, bf16[4,448,256]{2,1,0:T(8,128)(2,1)}, bf16[4,2,448,256]{3,2,1,0:T(8,128)(2,1)}, bf16[4,256,1024]{2,1,0:T(8,128)(2,1)}) custom-call(bf16[8,4096]{1,0:T(8,128)(2,1)S(1)} %get-tuple-element.36.unit, bf16[512,4096]{1,0:T(8,128)(2,1)} %index.1, s32[1024,8]{1,0:T(8,128)S(1)} %bitcast_select_fusion.code, ...), custom_call_target="tpu_custom_call" | custom-call | tf_op jit(solution)/shard_map/attend/pallas_call | solution.py:571
  155.4 0.2 fusion.28
  155.6 0.5 log_subtract_fusion
  156.1 0.1 divide_convert_fusion.head
  156.2 26.9 %gather_head.1 = (bf16[32,8,4096]{2,1,0:T(8,128)(2,1)S(1)}, bf16[4,8,1024]{2,1,0:T(8,128)(2,1)S(1)}) custom-call(bf16[8,4096]{1,0:T(8,128)(2,1)S(1)} %divide_convert_fusion.head), custom_call_target="tpu_custom_call" | custom-call | tf_op jit(solution)/shard_map/gather_head/pallas_call | solution.py:629
  183.1 0.0 copy-done.11
  183.1 0.0 copy-start.3
  183.1 1.3 fusion.3
  184.4 0.8 copy-done.3
  185.2 1.4 fusion.19
  186.6 0.6 copy-done.4
  187.2 1.3 fusion.src
  188.5 0.0 copy-start.12
  188.6 30.9 %finish_links.1 = (bf16[256,128]{1,0:T(8,128)(2,1)S(1)}, bf16[4,448,256]{2,1,0:T(8,128)(2,1)S(1)}, bf16[4,32,8,1024]{3,2,1,0:T(8,128)(2,1)S(1)}) custom-call(bf16[256,4096]{1,0:T(8,128)(2,1)S(1)} %fusion.src, bf16[448,256]{1,0:T(8,128)(2,1)S(1)} %convert_bitcast_fusion.act, bf16[4,8,1024]{2,1,0:T(8,128)(2,1)S(1)} %get-tuple-element.22.hx), custom_call_target="tpu_custom_call" | custom-call | tf_op jit(solution)/shard_map/finish_links/pallas_call | solution.py:658
  219.5 0.0 copy-done.13
  219.5 0.0 copy-done.12
  219.6 2.1 bitcast_convert_fusion.2
  221.6 2.1 bitcast_convert_fusion.1
  223.7 0.0 copy-done.14
  223.7 2.0 bitcast_convert_fusion
  225.8 0.6 copy.38
  (13 shorter events, 0.1 us)
Async XLA Ops:
  3.1 0.8 copy-start.1
  27.1 4.0 %copy-start = (bf16[256,4096]{1,0:T(8,128)(2,1)}, bf16[256,4096]{1,0:T(8,128)(2,1)S(1)}, u32[]{:S(2)}) copy-start(bf16[256,4096]{1,0:T(8,128)(2,1)S(1)} %get-tuple-element.17.inp) | copy-start | bytes 6291460
  27.1 4.0 %copy-start.2 = (bf16[4096,448]{0,1:T(8,128)(2,1)S(1)}, bf16[4096,448]{0,1:T(8,128)(2,1)}, u32[]{:S(2)}) copy-start(bf16[4096,448]{0,1:T(8,128)(2,1)} %param.12) | copy-start | bytes 11010052
  31.1 1.2 copy-start.5
  31.1 2.2 copy-start.10
  34.7 15.9 %copy-start.7 = (bf16[8,4096]{1,0:T(8,128)(2,1)S(1)}, bf16[8,4096]{1,0:T(8,128)(2,1)}, u32[]{:S(2)}) copy-start(bf16[8,4096]{1,0:T(8,128)(2,1)} %param.11) | copy-start | bytes 196612
  34.7 16.0 %copy-start.8 = (bf16[8,4096]{1,0:T(8,128)(2,1)S(1)}, bf16[8,4096]{1,0:T(8,128)(2,1)}, u32[]{:S(2)}) copy-start(bf16[8,4096]{1,0:T(8,128)(2,1)} %param.16) | copy-start | bytes 196612
  34.7 16.3 %copy-start.9 = (s32[128,1,8]{0,2,1:T(8,128)S(1)}, s32[128,1,8]{0,2,1:T(8,128)}, u32[]{:S(2)}) copy-start(s32[128,1,8]{0,2,1:T(8,128)} %param.17) | copy-start | bytes 12292
  34.7 17.0 %copy-start.15 = (s32[128,1]{0,1:T(1,128)S(1)}, s32[128,1]{0,1:T(1,128)}, u32[]{:S(2)}) copy-start(s32[128,1]{0,1:T(1,128)} %param.18) | copy-start | bytes 1540
  34.8 20.6 %copy-start.6 = (f32[256,448]{0,1:T(8,128)S(1)}, f32[256,448]{0,1:T(8,128)}, u32[]{:S(2)}) copy-start(f32[256,448]{0,1:T(8,128)} %copy-done.5) | copy-start | bytes 1376260
  55.7 127.5 %copy-start.11 = (bf16[448,4096]{1,0:T(8,128)(2,1)S(1)}, bf16[448,4096]{1,0:T(8,128)(2,1)}, u32[]{:S(2)}) copy-start(bf16[448,4096]{1,0:T(8,128)(2,1)} %param.14) | copy-start | bytes 11010052
  183.1 2.0 copy-start.3
  185.2 2.0 copy-start.4
  187.2 32.3 %copy-start.13 = (bf16[4,2,448,256]{3,2,1,0:T(8,128)(2,1)S(1)}, bf16[4,2,448,256]{3,2,1,0:T(8,128)(2,1)}, u32[]{:S(2)}) copy-start(bf16[4,2,448,256]{3,2,1,0:T(8,128)(2,1)} %get-tuple-element.26) | copy-start | bytes 5505028
  188.5 31.0 %copy-start.12 = (bf16[4,256,1024]{2,1,0:T(8,128)(2,1)S(1)}, bf16[4,256,1024]{2,1,0:T(8,128)(2,1)}, u32[]{:S(2)}) copy-start(bf16[4,256,1024]{2,1,0:T(8,128)(2,1)} %get-tuple-element.24) | copy-start | bytes 6291460
  221.6 2.1 copy-start.14

commit v7 on v6

--- a/solution.py
+++ b/solution.py
@@ -64,57 +64,63 @@
 
 
 class PlaneGather:
-    copies = 32
-
     def __init__(self, place, src, out, view, send, recv):
         self.place, self.src, self.out, self.view = place, src, out, view
         self.send, self.recv = send, recv
         self.sent = []
 
-    def push(self, ref, origin, f):
+    def push(self, origin, f, half=None, src=None):
+        to = self.view(self.out, origin, half)
         copy = copy_to(
-            ref,
-            self.view(self.out, origin),
+            to if src is None else src,
+            to,
             self.send.at[len(self.sent)],
-            self.recv.at[origin],
+            self.recv.at[half or 0, origin],
             self.place.x,
             f,
         )
         copy.start()
         self.sent.append(copy)
 
-    def arrive(self, origin):
-        block = self.view(self.out, origin)
-        copy_to(
-            block, block, self.send.at[31], self.recv.at[origin], self.place.x, self.place.partner
-        ).wait_recv()
-        return block
+    def arrive(self, origin, halves=(None,)):
+        for half in halves:
+            block = self.view(self.out, origin, half)
+            copy_to(
+                block, block, self.send.at[0], self.recv.at[half or 0, origin], self.place.x,
+                self.place.partner,
+            ).wait_recv()
 
     def start(self):
         p = self.place
-        self.own = pltpu.make_async_copy(self.src, self.view(self.out, p.f), self.send.at[31])
-        for j in near_first:
-            self.push(self.src, p.f, p.a_peer(j))
-        for j in near_first:
-            self.push(self.src, p.f, p.b_peer(j))
-        self.push(self.src, p.f, p.partner)
+        self.own = pltpu.make_async_copy(self.src, self.view(self.out, p.f, None), self.send.at[40])
+        for peer in (p.a_peer(1), p.a_peer(3), p.b_peer(1), p.b_peer(3), p.partner):
+            self.push(p.f, peer, src=self.src)
         self.own.start()
 
     def relay(self):
         p = self.place
         for j in near_first:
             origin = p.a_peer(j)
-            block = self.arrive(origin)
-            for i in near_first:
-                self.push(block, origin, p.b_peer(i))
-            self.push(block, origin, p.partner)
+            if j == 2:
+                self.arrive(origin, (0, 1))
+            else:
+                self.arrive(origin)
+                self.push(origin, p.a_peer(4 - j), half=(3 - j) // 2)
+            for peer in (p.b_peer(1), p.b_peer(3), p.partner):
+                self.push(origin, peer)
 
     def finish(self):
         p = self.place
         for j in (0,) + near_first:
-            for i in near_first:
+            for i in (1, 3):
                 origin = p.at((p.b + i) % 4, (p.a + j) % 4, p.c)
-                self.push(self.arrive(origin), origin, p.partner)
+                self.arrive(origin)
+                self.push(origin, p.b_peer(4 - i), half=(3 - i) // 2)
+                self.push(origin, p.partner)
+        for j in (0,) + near_first:
+            origin = p.at((p.b + 2) % 4, (p.a + j) % 4, p.c)
+            self.arrive(origin, (0, 1))
+            self.push(origin, p.partner)
         for j in (0,) + near_first:
             for i in (0,) + near_first:
                 z, y = (p.z + i) % 4, (p.y + j) % 4
@@ -124,85 +130,135 @@
             copy.wait_send()
 
 
+gather_sems = [DMA((41,)), DMA((2, 32))]
+
+
+class RingSum:
+    def __init__(self, x, me, peer, parts, axis, scratch):
+        self.x, self.me, self.peer, self.parts, self.axis = x, me, peer, parts, axis
+        self.relay, self.got, self.relay_send, self.relay_recv, self.send, self.recv = scratch
+
+    @staticmethod
+    def scratch(part, dtype):
+        return [pltpu.VMEM((2,) + part, dtype), pltpu.VMEM((2,) + part, dtype),
+                DMA((2,)), DMA((2,)), DMA((4,)), DMA((4,))]
+
+    def cut(self, ref, at, half):
+        index = [slice(None)] * (len(ref.shape) - 1)
+        size = ref.shape[1 + self.axis] // 2
+        index[self.axis] = slice(half * size, half * size + size)
+        return ref.at[(at,) + tuple(index)]
+
+    def near_copy(self, side, half):
+        step = 3 if side else 1
+        return copy_to(
+            self.cut(self.parts, (self.me + step) % 4, half), self.cut(self.got, side, half),
+            self.send.at[side * 2 + half], self.recv.at[side * 2 + half], self.x, self.peer(step),
+        )
+
+    def far_copy(self, side):
+        step = 3 if side else 1
+        return copy_to(
+            self.cut(self.parts, (self.me + 2) % 4, side), self.cut(self.relay, side, side),
+            self.relay_send.at[side], self.relay_recv.at[side], self.x, self.peer(step),
+        )
+
+    def near(self, side):
+        self.near_copy(side, 1 - side).start()
+
+    def far(self):
+        self.far_copy(0).start()
+        self.far_copy(1).start()
+
+    def combine(self):
+        for side in range(2):
+            self.far_copy(side).wait_recv()
+            own = self.cut(self.parts, (self.me + (3 if side else 1)) % 4, side)
+            got = self.cut(self.relay, side, side)
+            for row in range(own.shape[0]):
+                total = own[row].astype(jnp.float32) + got[row].astype(jnp.float32)
+                own[row] = total.astype(own.dtype)
+            self.near_copy(side, side).start()
+
+    def arrive(self):
+        for side in range(2):
+            for half in range(2):
+                self.near_copy(side, half).wait_recv()
+
+    def total(self, row):
+        return (
+            self.parts[self.me, row].astype(jnp.float32)
+            + self.got[0, row].astype(jnp.float32)
+            + self.got[1, row].astype(jnp.float32)
+        )
+
+    def close(self):
+        for side in range(2):
+            self.far_copy(side).wait_send()
+            for half in range(2):
+                self.near_copy(side, half).wait_send()
+
+
 class PlaneScatter:
-    def __init__(self, place, src, view, scratch):
+    def __init__(self, place, src, view, axis, scratch):
         self.place, self.src, self.view = place, src, view
-        (self.got1, self.sum1, self.got2, self.sum2, self.got3, self.send1, self.recv1,
-         self.send2, self.recv2, self.send3, self.recv3) = scratch
+        p = place
+        self.got1, self.sum1, self.sum2, self.send1, self.recv1 = scratch[:5]
+        self.ring_b = RingSum(p.x, p.b, p.b_peer, self.sum1, axis + 1, scratch[5:11])
+        self.ring_a = RingSum(p.x, p.a, p.a_peer, self.sum2, axis + 1, scratch[11:17])
 
     @staticmethod
     def scratch(block, dtype=jnp.bfloat16):
         wide = lambda *lead: pltpu.VMEM(lead + block, dtype)
-        return [wide(16), wide(4, 4), wide(4, 4), wide(4), wide(4), DMA((16,)), DMA((16,)),
-                DMA((4,)), DMA((4,)), DMA((4,)), DMA((4,))]
+        return (
+            [wide(16), wide(4, 4), wide(4, 1), DMA((16,)), DMA((16,))]
+            + RingSum.scratch((4,) + block, dtype)
+            + RingSum.scratch((1,) + block, dtype)
+        )
+
+    def to_partner(self, b, a):
+        p = self.place
+        k = b * 4 + a
+        return copy_to(self.view(self.src, p.at(b, a, 1 - p.c), None), self.got1.at[k],
+                       self.send1.at[k], self.recv1.at[k], p.x, p.partner)
 
     def start(self):
         p = self.place
-        self.sent1 = []
         for i in (2, 1, 3, 0):
             for a in range(4):
-                b = (p.a + i) % 4
-                k = b * 4 + a
-                copy = copy_to(
-                    self.view(self.src, p.at(b, a, 1 - p.c)),
-                    self.got1.at[k],
-                    self.send1.at[k],
-                    self.recv1.at[k],
-                    p.x,
-                    p.partner,
-                )
-                copy.start()
-                self.sent1.append(copy)
+                self.to_partner((p.a + i) % 4, a).start()
 
     def middle(self):
         p = self.place
-        sent2 = []
         for i in (2, 1, 3, 0):
             b = (p.b + i) % 4
             for a in range(4):
                 k = b * 4 + a
-                copy_to(
-                    self.got1.at[k], self.got1.at[k], self.send1.at[k], self.recv1.at[k],
-                    p.x, p.partner,
-                ).wait_recv()
-                own = self.view(self.src, p.at(b, a, p.c))[...].astype(jnp.float32)
-                self.sum1[b, a] = (own + self.got1[k].astype(jnp.float32)).astype(self.sum1.dtype)
-            if i:
-                copy = copy_to(
-                    self.sum1.at[b], self.got2.at[p.b], self.send2.at[i], self.recv2.at[p.b],
-                    p.x, p.b_peer(i),
-                )
-                copy.start()
-                sent2.append(copy)
-        for i in near_first:
-            b = (p.b + i) % 4
-            copy_to(
-                self.got2.at[b], self.got2.at[b], self.send2.at[i], self.recv2.at[b],
-                p.x, p.b_peer(i),
-            ).wait_recv()
-        sent3 = []
+                got = self.got1.at[k]
+                copy_to(got, got, self.send1.at[k], self.recv1.at[k], p.x, p.partner).wait_recv()
+                own = self.view(self.src, p.at(b, a, p.c), None)[...].astype(jnp.float32)
+                self.sum1[b, a] = (own + got[...].astype(jnp.float32)).astype(self.sum1.dtype)
+            if i == 2:
+                self.ring_b.far()
+            elif i:
+                self.ring_b.near(i // 2)
+        self.ring_b.combine()
+        self.ring_b.arrive()
         for j in (2, 1, 3, 0):
             a = (p.a + j) % 4
-            total = self.sum1[p.b, a].astype(jnp.float32)
-            for i in near_first:
-                total += self.got2[(p.b + i) % 4, a].astype(jnp.float32)
-            if j:
-                self.sum2[a] = total.astype(self.sum2.dtype)
-                copy = copy_to(
-                    self.sum2.at[a], self.got3.at[p.a], self.send3.at[j], self.recv3.at[p.a],
-                    p.x, p.a_peer(j),
-                )
-                copy.start()
-                sent3.append(copy)
-        for j in near_first:
-            a = (p.a + j) % 4
-            copy_to(
-                self.got3.at[a], self.got3.at[a], self.send3.at[j], self.recv3.at[a],
-                p.x, p.a_peer(j),
-            ).wait_recv()
-            total += self.got3[a].astype(jnp.float32)
-        for copy in self.sent1 + sent2 + sent3:
-            copy.wait_send()
+            self.sum2[a, 0] = self.ring_b.total(a).astype(self.sum2.dtype)
+            if j == 2:
+                self.ring_a.far()
+            elif j:
+                self.ring_a.near(j // 2)
+        self.ring_a.combine()
+        self.ring_a.arrive()
+        total = self.ring_a.total(0)
+        self.ring_b.close()
+        self.ring_a.close()
+        for i in range(4):
+            for a in range(4):
+                self.to_partner(i, a).wait_send()
         return total
 
 
@@ -232,12 +288,24 @@
     )
 
 
-def column_block(ref, f):
-    return ref.at[:, pl.ds(pl.multiple_of(f * 128, 128), 128)]
-
-
-def row_block(ref, f):
-    return ref.at[f]
+def part_of(size, half):
+    return slice(None) if half is None else slice(half * size // 2, (half + 1) * size // 2)
+
+
+def column_block(ref, f, half):
+    return ref.at[part_of(256, half), pl.ds(pl.multiple_of(f * 128, 128), 128)]
+
+
+def row_block(ref, f, half):
+    return ref.at[f, :, part_of(4096, half)]
+
+
+def lead_block(ref, f, half):
+    return ref.at[f, part_of(4, half)]
+
+
+def second_block(ref, f, half):
+    return ref.at[part_of(4, half), f]
 
 
 def gather_input(mlp_input, table):
@@ -248,7 +316,7 @@
         gather = PlaneGather(place, src, out, column_block, send, recv)
         gather.start()
         finish_table()
-        tables = PlaneGather(place, tab_x, tab_all, row_block, t_send, t_recv)
+        tables = PlaneGather(place, tab_x, tab_all, lead_block, t_send, t_recv)
         tables.start()
         gather.relay()
         tables.relay()
@@ -262,7 +330,7 @@
         out_shape=(jax.ShapeDtypeStruct((rows, cols * 32), jnp.bfloat16), ints(4), ints(32, 4)),
         in_specs=[ANY] * 2,
         out_specs=[ANY] * 3,
-        scratch_shapes=[DMA((32,)), DMA((32,)), DMA((4,)), DMA((4,)), DMA((32,)), DMA((32,))],
+        scratch_shapes=gather_sems + [DMA((4,)), DMA((4,))] + gather_sems,
         compiler_params=params(0, 4),
         name="gather_input",
     )(mlp_input, table)
@@ -273,7 +341,7 @@
     def kernel(src, out, *scratch):
         place = Place()
         meet(place, False)
-        scatter = PlaneScatter(place, src, row_block, scratch)
+        scatter = PlaneScatter(place, src, row_block, 1, scratch)
         scatter.start()
         out[...] = scatter.middle()
 
@@ -314,16 +382,22 @@
 class AllSum:
     def __init__(self, place, src, scratch):
         self.place, self.src = place, src
-        (self.got1, self.sum1, self.got2, self.sum2, self.got3, self.stage, self.got4, self.send1,
-         self.recv1, self.send2, self.recv2, self.send3, self.recv3, self.send4,
-         self.recv4) = scratch
+        p = place
+        (self.got1, self.sum1, self.sum2, self.stage, self.got4, self.send1, self.recv1, self.send4,
+         self.recv4) = scratch[:9]
+        self.ring_b = RingSum(p.x, p.b, p.b_peer, self.sum1, 1, scratch[9:15])
+        self.ring_a = RingSum(p.x, p.a, p.a_peer, self.sum2, 1, scratch[15:21])
 
     @staticmethod
     def scratch(width, dtype):
         wide = lambda *lead: pltpu.VMEM(lead + (32, width), dtype)
         last = pltpu.VMEM((4, 8, width), dtype)
-        return [wide(16), wide(4, 4), wide(4, 4), wide(4), wide(4), last, last,
-                DMA((16,)), DMA((16,))] + [DMA((4,))] * 6
+        return (
+            [wide(16), wide(4, 4), wide(4, 1), last, last, DMA((16,)), DMA((16,)), DMA((4,)),
+             DMA((4,))]
+            + RingSum.scratch((4, 32, width), dtype)
+            + RingSum.scratch((1, 32, width), dtype)
+        )
 
     def rows(self, k, c):
         return self.src.at[pl.ds(pl.multiple_of(k * 64 + c * 32, 32), 32), :]
@@ -332,16 +406,6 @@
         p = self.place
         return copy_to(self.rows(k, 1 - p.c), self.got1.at[k], self.send1.at[k], self.recv1.at[k],
                        p.x, p.partner)
-
-    def to_b(self, i):
-        p = self.place
-        return copy_to(self.sum1.at[(p.b + i) % 4], self.got2.at[p.b], self.send2.at[i],
-                       self.recv2.at[p.b], p.x, p.b_peer(i))
-
-    def to_a(self, j):
-        p = self.place
-        return copy_to(self.sum2.at[(p.a + j) % 4], self.got3.at[p.a], self.send3.at[j],
-                       self.recv3.at[p.a], p.x, p.a_peer(j))
 
     def to_x(self, j):
         p = self.place
@@ -362,32 +426,26 @@
             return carry
 
         lax.fori_loop(0, 4, add, 0)
-        if i:
-            self.to_b(i).start()
+        if i == 2:
+            self.ring_b.far()
+        elif i:
+            self.ring_b.near(i // 2)
 
     def second(self):
         p = self.place
-        for i in near_first:
-            got = self.got2.at[(p.b + i) % 4]
-            copy_to(got, got, self.send2.at[i], self.recv2.at[(p.b + i) % 4], p.x,
-                    p.b_peer(i)).wait_recv()
+        self.ring_b.arrive()
         for j in (2, 1, 3, 0):
             a = (p.a + j) % 4
-            total = self.sum1[p.b, a].astype(jnp.float32)
-            for i in near_first:
-                total += self.got2[(p.b + i) % 4, a].astype(jnp.float32)
-            self.sum2[a] = total.astype(self.sum2.dtype)
-            if j:
-                self.to_a(j).start()
+            self.sum2[a, 0] = self.ring_b.total(a).astype(self.sum2.dtype)
+            if j == 2:
+                self.ring_a.far()
+            elif j:
+                self.ring_a.near(j // 2)
+        self.ring_a.combine()
 
     def third(self):
-        p = self.place
-        total = self.sum2[p.a].astype(jnp.float32)
-        for j in near_first:
-            a = (p.a + j) % 4
-            got = self.got3.at[a]
-            copy_to(got, got, self.send3.at[j], self.recv3.at[a], p.x, p.a_peer(j)).wait_recv()
-            total += got[...].astype(jnp.float32)
+        self.ring_a.arrive()
+        total = self.ring_a.total(0)
         for x in range(4):
             self.stage[x] = total[8 * x : 8 * x + 8].astype(self.stage.dtype)
         for j in near_first:
@@ -402,9 +460,9 @@
             copy_to(got, got, self.send4.at[j], self.recv4.at[x], x, p.f).wait_recv()
             own += got[...].astype(jnp.float32)
         for j in near_first:
-            self.to_b(j).wait_send()
-            self.to_a(j).wait_send()
             self.to_x(j).wait_send()
+        self.ring_b.close()
+        self.ring_a.close()
 
         def sent(k, carry):
             self.to_partner(k).wait_send()
@@ -415,11 +473,11 @@
 
 
 def attend(unit_rows, span_index, codes, hidden, factors, whole_input):
-    n = 15
+    n = 21
 
     def kernel(unit, index, code, hid, fac, inp,
                pull_out, sums_out, hid_x, fac_x, inp_x,
-               unit_x, query, pull, sums, batch, batch_code, weight, scale, u_send, u_recv, a_send, b_send, d_send, recv,
+               unit_x, query, pull, sums, batch, batch_code, weight, scale, u_send, u_recv, a_send, b_send, c_send, d_send, recv,
                h_send, h_recv, f_send, f_recv, i_send, i_recv, pair_send, pair_recv, *scratch):
         p = place = Place()
         meet(place, True)
@@ -436,20 +494,35 @@
             [unit_x[x].astype(jnp.float32) for x in range(4)], axis=0
         ).astype(jnp.bfloat16)
 
+        def half_block(f, half):
+            return query.at[pl.ds(pl.multiple_of(f * 32 + half * 16, 16), 16), :]
+
         def push(origin, f, send):
-            copy = copy_to(block(origin), block(origin), send, recv.at[origin], p.x, f)
+            copy = copy_to(block(origin), block(origin), send, recv.at[0, origin], p.x, f)
             copy.start()
             return copy
 
+        def push_half(origin, f, half, send):
+            part = half_block(origin, half)
+            copy = copy_to(part, part, send, recv.at[half, origin], p.x, f)
+            copy.start()
+            return copy
+
         def arrive(origin):
-            copy_to(block(origin), block(origin), d_send.at[origin], recv.at[origin], p.x,
+            copy_to(block(origin), block(origin), d_send.at[origin], recv.at[0, origin], p.x,
                     p.partner).wait_recv()
 
+        def arrive_halves(origin):
+            for half in range(2):
+                part = half_block(origin, half)
+                copy_to(part, part, d_send.at[origin], recv.at[half, origin], p.x,
+                        p.partner).wait_recv()
+
         sent = []
-        for j in near_first:
+        for j in (1, 3):
             sent.append(push(p.f, p.a_peer(j), a_send.at[j]))
-        for j in near_first:
-            sent.append(push(p.f, p.b_peer(j), b_send.at[j]))
+        for i in (1, 3):
+            sent.append(push(p.f, p.b_peer(i), b_send.at[i]))
         push(p.f, p.partner, d_send.at[p.f])
 
         def norms(part, carry):
@@ -464,8 +537,13 @@
 
         for j in near_first:
             origin = p.a_peer(j)
-            arrive(origin)
-            for i in near_first:
+            if j == 2:
+                arrive_halves(origin)
+            else:
+                arrive(origin)
+                side = (3 - j) // 2
+                sent.append(push_half(origin, p.a_peer(4 - j), side, a_send.at[2 * side]))
+            for i in (1, 3):
                 sent.append(push(origin, p.b_peer(i), b_send.at[4 * j + i]))
             push(origin, p.partner, d_send.at[origin])
 
@@ -500,8 +578,21 @@
                     k = chip_of(stage, turn)
                     origin = k * 2 + p.c
 
+                    away = (origin // 8 - p.z) * (1 - p.c) + (origin // 2 % 4 - p.y) * p.c
+                    away = (away + 4) % 4
+
                     def forward():
-                        arrive(origin)
+                        @pl.when(away == 2)
+                        def _():
+                            arrive_halves(origin)
+
+                        @pl.when(away != 2)
+                        def _():
+                            arrive(origin)
+                            side = (3 - away) // 2
+                            push_half(origin, p.at((p.b + 4 - away) % 4, p.a, p.c), side,
+                                      c_send.at[origin])
+
                         push(origin, p.partner, d_send.at[origin])
 
                     if stage:
@@ -535,6 +626,8 @@
                 second.group(group)
         first.group(0)
         second.group(0)
+        first.ring_b.combine()
+        second.ring_b.combine()
         first.second()
         second.second()
         first.third()
@@ -561,11 +654,21 @@
 
         def pushed(k, carry):
             origin = k * 2 + p.c
-            copy_to(block(origin), block(origin), d_send.at[origin], recv.at[origin], p.x,
+            copy_to(block(origin), block(origin), d_send.at[origin], recv.at[0, origin], p.x,
                     p.partner).wait_send()
             return carry
 
         lax.fori_loop(0, 16, pushed, 0)
+
+        def handed(a, carry):
+            for i in (1, 3):
+                origin = p.at((p.b + i) % 4, a, p.c)
+                part = half_block(origin, (3 - i) // 2)
+                copy_to(part, part, c_send.at[origin], recv.at[(3 - i) // 2, origin], p.x,
+                        p.partner).wait_send()
+            return carry
+
+        lax.fori_loop(0, 4, handed, 0)
 
     bf = lambda *shape: jax.ShapeDtypeStruct(shape, jnp.bfloat16)
     return pl.pallas_call(
@@ -588,7 +691,7 @@
             pltpu.VMEM((448, 8), jnp.int32),
             pltpu.VMEM((448, 512), jnp.bfloat16),
             pltpu.VMEM((1, 512), jnp.float32),
-            DMA((4,)), DMA((4,)), DMA((4,)), DMA((16,)), DMA((32,)), DMA((32,)),
+            DMA((4,)), DMA((4,)), DMA((4,)), DMA((16,)), DMA((32,)), DMA((32,)), DMA((2, 32)),
         ]
         + [DMA((4,))] * 8
         + AllSum.scratch(4096, jnp.bfloat16)
@@ -631,7 +734,7 @@
         out_shape=(bf(32, 8, 4096), bf(4, 8, 1024)),
         in_specs=[ANY],
         out_specs=[ANY] * 2,
-        scratch_shapes=[DMA((32,)), DMA((32,)), DMA((4,)), DMA((4,))],
+        scratch_shapes=gather_sems + [DMA((4,)), DMA((4,))],
         compiler_params=params(2, 4),
         name="gather_head",
     )(head_grad)
@@ -643,11 +746,9 @@
         place = Place()
         meet(place, True)
         finish_acts = across_gather(place, act, act_x, x_send, x_recv)
-        scatter = PlaneScatter(place, src, column_block, scratch)
+        scatter = PlaneScatter(place, src, column_block, 0, scratch)
         scatter.start()
-        gather = PlaneGather(
-            place, hx, head_cols, lambda ref, f: ref.at[:, f], send, recv
-        )
+        gather = PlaneGather(place, hx, head_cols, second_block, send, recv)
         gather.start()
         gather.relay()
         out[...] = scatter.middle().astype(jnp.bfloat16)
@@ -660,7 +761,8 @@
         out_shape=(bf(256, 128), bf(4, *acts.shape), bf(4, 32, 8, 1024)),
         in_specs=[VMEM, ANY, ANY],
         out_specs=[VMEM, ANY, ANY],
-        scratch_shapes=[DMA((32,)), DMA((32,)), DMA((4,)), DMA((4,))]
+        scratch_shapes=gather_sems
+        + [DMA((4,)), DMA((4,))]
         + PlaneScatter.scratch((256, 128)),
         compiler_params=params(3, 12),
         name="finish_links",

time: 227 us -> 248 us (1.093)
  Pallas kernels: 196 us -> 217 us
    pallas_call x1, Pallas kernels: 99.7 us -> 115 us  [attend(): pl.pallas_call(kernel, out_shape=(jax.ShapeDtypeStruct((8, 4096), jnp.flo...]
    pallas_call x1, Pallas kernels: 23.1 us -> 29.9 us  [gather_input(): pl.pallas_call(kernel, out_shape=(jax.ShapeDtypeStruct((rows, cols * 32),...]
    pallas_call x1, Pallas kernels: 26.9 us -> 22.8 us  [gather_head(): pl.pallas_call(kernel, out_shape=(bf(32, 8, 4096), bf(4, 8, 1024)), in_sp...]
    pallas_call x1, Pallas kernels: 30.9 us -> 33.6 us  [finish_links(): pl.pallas_call(kernel, out_shape=(bf(256, 128), bf(4, *acts.shape), bf(4,...]
where the time goes in v7:
time: 248 us; the launch traced here: 247 us
  Pallas kernels  217 us (88%)
  matrix products  16.7 us (7%)
  other arithmetic  7.31 us (3%)
  local copies, waits for them, and re-layouts  4.97 us (2%)
    pallas_call x1, Pallas kernels, attend(): pl.pallas_call(kernel, out_shape=(jax.ShapeDtypeStruct((8, 4096), jnp.flo...  115 us
    pallas_call x1, Pallas kernels, finish_links(): pl.pallas_call(kernel, out_shape=(bf(256, 128), bf(4, *acts.shape), bf(4,...  33.6 us
    pallas_call x1, Pallas kernels, gather_input(): pl.pallas_call(kernel, out_shape=(jax.ShapeDtypeStruct((rows, cols * 32),...  29.9 us
    pallas_call x1, Pallas kernels, gather_head(): pl.pallas_call(kernel, out_shape=(bf(32, 8, 4096), bf(4, 8, 1024)), in_sp...  22.8 us
    pallas_call x1, Pallas kernels, scatter_branch(): pl.pallas_call(kernel, out_shape=jax.ShapeDtypeStruct((8, 4096), jnp.floa...  16.4 us

profile of v7, /device:TPU:1, one launch (start us, length us, event | category | flops | bytes accessed | tf_op | source)
XLA Modules:
  0.0 247.3 jit_solution(16541295726334632337)
XLA Ops:
  0.6 1.0 fusion.22
  1.6 1.4 compare_reduce_fusion
  3.1 0.1 select_reduce_fusion.1
  3.1 0.0 copy-start.1
  3.1 0.8 copy-done.1
  4.0 29.9 %gather_input.1 = (bf16[256,4096]{1,0:T(8,128)(2,1)S(1)}, s32[4,8,128]{2,1,0:T(8,128)}, s32[32,4,8,128]{3,2,1,0:T(8,128)S(1)}) custom-call(bf16[256,128]{1,0:T(8,128)(2,1)S(1)} %copy-done.1, s32[8,128]{1,0:T(8,128)S(1)} %broadcast_add_fusion.tab), custom_call_target="tpu_custom_call" | custom-call | tf_op jit(solution)/shard_map/gather_input/pallas_call | solution.py:328
  33.9 0.0 copy-start
  33.9 0.0 copy-start.2
  33.9 4.0 %fusion.34 = f32[256,448]{0,1:T(8,128)S(1)} fusion(bf16[256,4096]{1,0:T(8,128)(2,1)S(1)} %get-tuple-element.17.inp, bf16[4096,448]{0,1:T(8,128)(2,1)} %param.13), kind=kOutput, calls=%fused_computation.74 | convolution fusion | flops 939524096 | bytes 6225920 | tf_op jit(solution)/shard_map/dot_general | solution.py:812
  37.9 0.0 copy-done
  37.9 0.0 copy-done.2
  37.9 0.0 copy-start.5
  38.0 0.0 copy-start.10
  38.0 1.1 fusion.33
  39.1 0.0 copy-done.5
  39.1 1.0 copy-done.10
  40.2 1.4 convolution_bitcast_fusion.src
  41.5 0.0 copy-start.7
  41.5 0.0 copy-start.8
  41.6 0.0 copy-start.9
  41.6 0.0 copy-start.15
  41.6 0.0 copy-start.6
  41.6 16.4 %scatter_branch.1 = f32[8,4096]{1,0:T(8,128)S(1)} custom-call(bf16[32,8,4096]{2,1,0:T(8,128)(2,1)S(1)} %convolution_bitcast_fusion.src), custom_call_target="tpu_custom_call" | custom-call | tf_op jit(solution)/shard_map/scatter_branch/pallas_call | solution.py:348
  58.0 0.0 copy-done.7
  58.0 0.1 multiply_reduce_fusion.1
  58.2 0.0 copy-done.8
  58.2 0.2 fusion.32
  58.4 0.1 copy.27
  58.5 0.0 copy-done.9
  58.5 0.1 squeeze.4
  58.6 0.1 copy.26
  58.7 0.5 broadcast.119
  59.2 0.0 copy-done.15
  59.2 0.7 reduce.11
  59.9 0.1 lt.11
  60.0 0.1 copy.25
  60.1 0.1 fusion.26
  60.2 0.1 eq.51
  60.3 2.3 select_reduce_fusion
  62.6 0.2 bitcast_select_fusion.code
  62.8 0.0 copy-done.6
  62.8 0.3 fusion.21
  63.1 0.0 copy-start.11
  63.1 114.5 %attend.1 = (f32[8,4096]{1,0:T(8,128)S(1)}, f32[8,128]{1,0:T(8,128)S(1)}, bf16[4,448,256]{2,1,0:T(8,128)(2,1)}, bf16[4,2,448,256]{3,2,1,0:T(8,128)(2,1)}, bf16[4,256,1024]{2,1,0:T(8,128)(2,1)}) custom-call(bf16[8,4096]{1,0:T(8,128)(2,1)S(1)} %get-tuple-element.36.unit, bf16[512,4096]{1,0:T(8,128)(2,1)} %index.1, s32[1024,8]{1,0:T(8,128)S(1)} %bitcast_select_fusion.code, ...), custom_call_target="tpu_custom_call" | custom-call | tf_op jit(solution)/shard_map/attend/pallas_call | solution.py:674
  177.7 0.2 fusion.28
  177.9 0.5 log_subtract_fusion
  178.4 0.1 divide_convert_fusion.head
  178.5 22.8 %gather_head.1 = (bf16[32,8,4096]{2,1,0:T(8,128)(2,1)S(1)}, bf16[4,8,1024]{2,1,0:T(8,128)(2,1)S(1)}) custom-call(bf16[8,4096]{1,0:T(8,128)(2,1)S(1)} %divide_convert_fusion.head), custom_call_target="tpu_custom_call" | custom-call | tf_op jit(solution)/shard_map/gather_head/pallas_call | solution.py:732
  201.3 0.0 copy-done.11
  201.4 0.0 copy-start.3
  201.4 1.3 fusion.3
  202.6 0.7 copy-done.3
  203.4 1.4 fusion.19
  204.8 0.6 copy-done.4
  205.4 1.3 fusion.src
  206.8 0.0 copy-start.12
  206.8 33.6 %finish_links.1 = (bf16[256,128]{1,0:T(8,128)(2,1)S(1)}, bf16[4,448,256]{2,1,0:T(8,128)(2,1)S(1)}, bf16[4,32,8,1024]{3,2,1,0:T(8,128)(2,1)S(1)}) custom-call(bf16[256,4096]{1,0:T(8,128)(2,1)S(1)} %fusion.src, bf16[448,256]{1,0:T(8,128)(2,1)S(1)} %convert_bitcast_fusion.act, bf16[4,8,1024]{2,1,0:T(8,128)(2,1)S(1)} %get-tuple-element.22.hx), custom_call_target="tpu_custom_call" | custom-call | tf_op jit(solution)/shard_map/finish_links/pallas_call | solution.py:759
  240.4 0.0 copy-done.13
  240.4 0.0 copy-done.12
  240.4 2.1 bitcast_convert_fusion.2
  242.5 2.1 bitcast_convert_fusion.1
  244.6 0.0 copy-done.14
  244.6 2.1 bitcast_convert_fusion
  246.6 0.6 copy.38
  (13 shorter events, 0.1 us)
Async XLA Ops:
  3.1 0.8 copy-start.1
  33.9 4.0 %copy-start = (bf16[256,4096]{1,0:T(8,128)(2,1)}, bf16[256,4096]{1,0:T(8,128)(2,1)S(1)}, u32[]{:S(2)}) copy-start(bf16[256,4096]{1,0:T(8,128)(2,1)S(1)} %get-tuple-element.17.inp) | copy-start | bytes 6291460
  33.9 4.0 %copy-start.2 = (bf16[4096,448]{0,1:T(8,128)(2,1)S(1)}, bf16[4096,448]{0,1:T(8,128)(2,1)}, u32[]{:S(2)}) copy-start(bf16[4096,448]{0,1:T(8,128)(2,1)} %param.12) | copy-start | bytes 11010052
  37.9 1.2 copy-start.5
  38.0 2.2 copy-start.10
  41.5 16.5 %copy-start.7 = (bf16[8,4096]{1,0:T(8,128)(2,1)S(1)}, bf16[8,4096]{1,0:T(8,128)(2,1)}, u32[]{:S(2)}) copy-start(bf16[8,4096]{1,0:T(8,128)(2,1)} %param.11) | copy-start | bytes 196612
  41.5 16.7 %copy-start.8 = (bf16[8,4096]{1,0:T(8,128)(2,1)S(1)}, bf16[8,4096]{1,0:T(8,128)(2,1)}, u32[]{:S(2)}) copy-start(bf16[8,4096]{1,0:T(8,128)(2,1)} %param.16) | copy-start | bytes 196612
  41.6 17.0 %copy-start.9 = (s32[128,1,8]{0,2,1:T(8,128)S(1)}, s32[128,1,8]{0,2,1:T(8,128)}, u32[]{:S(2)}) copy-start(s32[128,1,8]{0,2,1:T(8,128)} %param.17) | copy-start | bytes 12292
  41.6 17.7 %copy-start.15 = (s32[128,1]{0,1:T(1,128)S(1)}, s32[128,1]{0,1:T(1,128)}, u32[]{:S(2)}) copy-start(s32[128,1]{0,1:T(1,128)} %param.18) | copy-start | bytes 1540
  41.6 21.2 %copy-start.6 = (f32[256,448]{0,1:T(8,128)S(1)}, f32[256,448]{0,1:T(8,128)}, u32[]{:S(2)}) copy-start(f32[256,448]{0,1:T(8,128)} %copy-done.5) | copy-start | bytes 1376260
  63.1 138.2 %copy-start.11 = (bf16[448,4096]{1,0:T(8,128)(2,1)S(1)}, bf16[448,4096]{1,0:T(8,128)(2,1)}, u32[]{:S(2)}) copy-start(bf16[448,4096]{1,0:T(8,128)(2,1)} %param.14) | copy-start | bytes 11010052
  201.4 2.0 copy-start.3
  203.4 2.0 copy-start.4
  205.4 35.0 %copy-start.13 = (bf16[4,2,448,256]{3,2,1,0:T(8,128)(2,1)S(1)}, bf16[4,2,448,256]{3,2,1,0:T(8,128)(2,1)}, u32[]{:S(2)}) copy-start(bf16[4,2,448,256]{3,2,1,0:T(8,128)(2,1)} %get-tuple-element.26) | copy-start | bytes 5505028
  206.8 33.7 %copy-start.12 = (bf16[4,256,1024]{2,1,0:T(8,128)(2,1)S(1)}, bf16[4,256,1024]{2,1,0:T(8,128)(2,1)}, u32[]{:S(2)}) copy-start(bf16[4,256,1024]{2,1,0:T(8,128)(2,1)} %get-tuple-element.24) | copy-start | bytes 6291460
  242.5 2.1 copy-start.14

commit v8 on v6

--- a/solution.py
+++ b/solution.py
@@ -15,6 +15,7 @@
 VMEM = pl.BlockSpec(memory_space=pltpu.VMEM)
 DMA = pltpu.SemaphoreType.DMA
 near_first = (1, 3, 2)
+far_first = (2, 3, 1, 0)
 
 
 class Place:
@@ -109,12 +110,15 @@
                 self.push(block, origin, p.b_peer(i))
             self.push(block, origin, p.partner)
 
-    def finish(self):
+    def hand(self):
         p = self.place
         for j in (0,) + near_first:
             for i in near_first:
                 origin = p.at((p.b + i) % 4, (p.a + j) % 4, p.c)
                 self.push(self.arrive(origin), origin, p.partner)
+
+    def close(self):
+        p = self.place
         for j in (0,) + near_first:
             for i in (0,) + near_first:
                 z, y = (p.z + i) % 4, (p.y + j) % 4
@@ -134,14 +138,14 @@
     def scratch(block, dtype=jnp.bfloat16):
         wide = lambda *lead: pltpu.VMEM(lead + block, dtype)
         return [wide(16), wide(4, 4), wide(4, 4), wide(4), wide(4), DMA((16,)), DMA((16,)),
-                DMA((4,)), DMA((4,)), DMA((4,)), DMA((4,))]
+                DMA((4, 4)), DMA((4, 4)), DMA((4,)), DMA((4,))]
 
     def start(self):
         p = self.place
         self.sent1 = []
-        for i in (2, 1, 3, 0):
-            for a in range(4):
-                b = (p.a + i) % 4
+        for i in far_first:
+            for j in far_first:
+                b, a = (p.a + i) % 4, (p.b + j) % 4
                 k = b * 4 + a
                 copy = copy_to(
                     self.view(self.src, p.at(b, a, 1 - p.c)),
@@ -157,9 +161,10 @@
     def middle(self):
         p = self.place
         sent2 = []
-        for i in (2, 1, 3, 0):
+        for i in far_first:
             b = (p.b + i) % 4
-            for a in range(4):
+            for j in far_first:
+                a = (p.a + j) % 4
                 k = b * 4 + a
                 copy_to(
                     self.got1.at[k], self.got1.at[k], self.send1.at[k], self.recv1.at[k],
@@ -167,25 +172,24 @@
                 ).wait_recv()
                 own = self.view(self.src, p.at(b, a, p.c))[...].astype(jnp.float32)
                 self.sum1[b, a] = (own + self.got1[k].astype(jnp.float32)).astype(self.sum1.dtype)
-            if i:
-                copy = copy_to(
-                    self.sum1.at[b], self.got2.at[p.b], self.send2.at[i], self.recv2.at[p.b],
-                    p.x, p.b_peer(i),
-                )
-                copy.start()
-                sent2.append(copy)
-        for i in near_first:
-            b = (p.b + i) % 4
-            copy_to(
-                self.got2.at[b], self.got2.at[b], self.send2.at[i], self.recv2.at[b],
-                p.x, p.b_peer(i),
-            ).wait_recv()
+                if i:
+                    copy = copy_to(
+                        self.sum1.at[b, a], self.got2.at[p.b, a], self.send2.at[i, j],
+                        self.recv2.at[p.b, a], p.x, p.b_peer(i),
+                    )
+                    copy.start()
+                    sent2.append(copy)
         sent3 = []
-        for j in (2, 1, 3, 0):
+        for j in far_first:
             a = (p.a + j) % 4
             total = self.sum1[p.b, a].astype(jnp.float32)
-            for i in near_first:
-                total += self.got2[(p.b + i) % 4, a].astype(jnp.float32)
+            for i in far_first[:3]:
+                b = (p.b + i) % 4
+                got = self.got2.at[b, a]
+                copy_to(
+                    got, got, self.send2.at[i, j], self.recv2.at[b, a], p.x, p.b_peer(i)
+                ).wait_recv()
+                total += got[...].astype(jnp.float32)
             if j:
                 self.sum2[a] = total.astype(self.sum2.dtype)
                 copy = copy_to(
@@ -252,8 +256,10 @@
         tables.start()
         gather.relay()
         tables.relay()
-        gather.finish()
-        tables.finish()
+        gather.hand()
+        tables.hand()
+        gather.close()
+        tables.close()
 
     rows, cols = mlp_input.shape
     ints = lambda *lead: jax.ShapeDtypeStruct(lead + table.shape, jnp.int32)
@@ -323,7 +329,7 @@
         wide = lambda *lead: pltpu.VMEM(lead + (32, width), dtype)
         last = pltpu.VMEM((4, 8, width), dtype)
         return [wide(16), wide(4, 4), wide(4, 4), wide(4), wide(4), last, last,
-                DMA((16,)), DMA((16,))] + [DMA((4,))] * 6
+                DMA((16,)), DMA((16,)), DMA((4, 4)), DMA((4, 4))] + [DMA((4,))] * 4
 
     def rows(self, k, c):
         return self.src.at[pl.ds(pl.multiple_of(k * 64 + c * 32, 32), 32), :]
@@ -333,10 +339,11 @@
         return copy_to(self.rows(k, 1 - p.c), self.got1.at[k], self.send1.at[k], self.recv1.at[k],
                        p.x, p.partner)
 
-    def to_b(self, i):
-        p = self.place
-        return copy_to(self.sum1.at[(p.b + i) % 4], self.got2.at[p.b], self.send2.at[i],
-                       self.recv2.at[p.b], p.x, p.b_peer(i))
+    def to_b(self, i, j):
+        p = self.place
+        b, a = (p.b + i) % 4, (p.a + j) % 4
+        return copy_to(self.sum1.at[b, a], self.got2.at[p.b, a], self.send2.at[i, j],
+                       self.recv2.at[p.b, a], p.x, p.b_peer(i))
 
     def to_a(self, j):
         p = self.place
@@ -353,29 +360,31 @@
         p = self.place
         b = (p.b + i) % 4
 
-        def add(a, carry):
+        def add(turn, carry):
+            j = near_order(3 - turn)
+            a = (p.a + j) % 4
             k = p.at(b, a, p.c) // 2
             got = self.got1.at[k]
             copy_to(got, got, self.send1.at[k], self.recv1.at[k], p.x, p.partner).wait_recv()
             own = self.rows(k, p.c)[...].astype(jnp.float32)
             self.sum1[b, a] = (own + got[...].astype(jnp.float32)).astype(self.sum1.dtype)
+            if i:
+                self.to_b(i, j).start()
             return carry
 
         lax.fori_loop(0, 4, add, 0)
-        if i:
-            self.to_b(i).start()
 
     def second(self):
         p = self.place
-        for i in near_first:
-            got = self.got2.at[(p.b + i) % 4]
-            copy_to(got, got, self.send2.at[i], self.recv2.at[(p.b + i) % 4], p.x,
-                    p.b_peer(i)).wait_recv()
-        for j in (2, 1, 3, 0):
+        for j in far_first:
             a = (p.a + j) % 4
             total = self.sum1[p.b, a].astype(jnp.float32)
             for i in near_first:
-                total += self.got2[(p.b + i) % 4, a].astype(jnp.float32)
+                b = (p.b + i) % 4
+                got = self.got2.at[b, a]
+                copy_to(got, got, self.send2.at[i, j], self.recv2.at[b, a], p.x,
+                        p.b_peer(i)).wait_recv()
+                total += got[...].astype(jnp.float32)
             self.sum2[a] = total.astype(self.sum2.dtype)
             if j:
                 self.to_a(j).start()
@@ -402,7 +411,8 @@
             copy_to(got, got, self.send4.at[j], self.recv4.at[x], x, p.f).wait_recv()
             own += got[...].astype(jnp.float32)
         for j in near_first:
-            self.to_b(j).wait_send()
+            for i in (0,) + near_first:
+                self.to_b(j, i).wait_send()
             self.to_a(j).wait_send()
             self.to_x(j).wait_send()
 
@@ -599,72 +609,97 @@
 
 
 def gather_head(head_grad):
-    def kernel(head, out, head_x, send, recv, hx_send, hx_recv):
+    def kernel(head, out, send, recv):
         place = Place()
-        p = place
-        meet(place, True)
+        meet(place, False)
         gather = PlaneGather(place, head, out, row_block, send, recv)
         gather.start()
-        wide = lambda x: pl.ds(pl.multiple_of(x * 1024, 1024), 1024)
-        own = pltpu.make_async_copy(head.at[:, wide(p.x)], head_x.at[p.x], hx_send.at[0])
-        own.start()
-        sent = []
-        for j in near_first:
-            x = (p.x + j) % 4
-            copy = copy_to(head.at[:, wide(x)], head_x.at[p.x], hx_send.at[j], hx_recv.at[p.x], x, p.f)
-            copy.start()
-            sent.append(copy)
         gather.relay()
-        gather.finish()
-        for j in near_first:
-            x = (p.x + j) % 4
-            copy_to(
-                head_x.at[x], head_x.at[x], hx_send.at[j], hx_recv.at[x], x, p.f
-            ).wait_recv()
-        own.wait()
-        for copy in sent:
-            copy.wait_send()
-
-    bf = lambda *shape: jax.ShapeDtypeStruct(shape, jnp.bfloat16)
-    out, head_x = pl.pallas_call(
+        gather.hand()
+        gather.close()
+
+    return pl.pallas_call(
         kernel,
-        out_shape=(bf(32, 8, 4096), bf(4, 8, 1024)),
+        out_shape=jax.ShapeDtypeStruct((32, 8, 4096), jnp.bfloat16),
         in_specs=[ANY],
-        out_specs=[ANY] * 2,
-        scratch_shapes=[DMA((32,)), DMA((32,)), DMA((4,)), DMA((4,))],
+        out_specs=ANY,
+        scratch_shapes=[DMA((32,)), DMA((32,))],
         compiler_params=params(2, 4),
         name="gather_head",
-    )(head_grad)
-    return out.reshape(256, 4096), head_x
-
-
-def finish_links(partial, acts, head_x):
-    def kernel(src, act, hx, out, act_x, head_cols, send, recv, x_send, x_recv, *scratch):
+    )(head_grad).reshape(256, 4096)
+
+
+class ColumnExchange:
+    def __init__(self, place, src, out, sems):
+        self.place, self.src, self.out = place, src, out
+        self.send, self.recv, self.pair_send, self.pair_recv = sems
+
+    def half(self, x, c):
+        return self.out.at[x, :, pl.ds(pl.multiple_of(c * 512, 512), 512)]
+
+    def start(self):
+        p = self.place
+        self.own = pltpu.make_async_copy(
+            self.src.at[:, pl.ds(pl.multiple_of(p.x * 1024, 1024), 1024)], self.out.at[p.x],
+            self.send.at[0],
+        )
+        self.own.start()
+        self.sent = []
+        for j in near_first:
+            x = (p.x + j) % 4
+            copy = copy_to(
+                self.src.at[:, pl.ds(pl.multiple_of(x * 1024 + p.c * 512, 512), 512)],
+                self.half(p.x, p.c), self.send.at[j], self.recv.at[p.x], x, p.f,
+            )
+            copy.start()
+            self.sent.append(copy)
+
+    def share(self):
+        p = self.place
+        for j in near_first:
+            x = (p.x + j) % 4
+            part = self.half(x, p.c)
+            copy_to(part, part, self.send.at[j], self.recv.at[x], x, p.f).wait_recv()
+            copy = copy_to(part, part, self.pair_send.at[j], self.pair_recv.at[x], p.x, p.partner)
+            copy.start()
+            self.sent.append(copy)
+
+    def finish(self):
+        p = self.place
+        for j in near_first:
+            x = (p.x + j) % 4
+            part = self.half(x, 1 - p.c)
+            copy_to(part, part, self.pair_send.at[j], self.pair_recv.at[x], p.x,
+                    p.partner).wait_recv()
+        self.own.wait()
+        for copy in self.sent:
+            copy.wait_send()
+
+
+def finish_links(partial, acts, head):
+    def kernel(src, act, head_ref, out, act_x, head_cols, x_send, x_recv, c0, c1, c2, c3, *scratch):
         place = Place()
         meet(place, True)
-        finish_acts = across_gather(place, act, act_x, x_send, x_recv)
         scatter = PlaneScatter(place, src, column_block, scratch)
         scatter.start()
-        gather = PlaneGather(
-            place, hx, head_cols, lambda ref, f: ref.at[:, f], send, recv
-        )
-        gather.start()
-        gather.relay()
+        finish_acts = across_gather(place, act, act_x, x_send, x_recv)
+        columns = ColumnExchange(place, head_ref, head_cols, (c0, c1, c2, c3))
+        columns.start()
         out[...] = scatter.middle().astype(jnp.bfloat16)
-        gather.finish()
         finish_acts()
+        columns.share()
+        columns.finish()
 
     bf = lambda *shape: jax.ShapeDtypeStruct(shape, jnp.bfloat16)
     return pl.pallas_call(
         kernel,
-        out_shape=(bf(256, 128), bf(4, *acts.shape), bf(4, 32, 8, 1024)),
+        out_shape=(bf(256, 128), bf(4, *acts.shape), bf(4, 256, 1024)),
         in_specs=[VMEM, ANY, ANY],
         out_specs=[VMEM, ANY, ANY],
-        scratch_shapes=[DMA((32,)), DMA((32,)), DMA((4,)), DMA((4,))]
-        + PlaneScatter.scratch((256, 128)),
+        scratch_shapes=[DMA((4,))] * 6 + PlaneScatter.scratch((256, 128)),
         compiler_params=params(3, 12),
         name="finish_links",
-    )(partial, acts, head_x)
+    )(partial, acts, head)
 
 
 def shards(
@@ -736,7 +771,7 @@
     pull = inverse_temp * (pull / exp_total[:, None] + positive_coeff[:, None] * positive_unit)
     head_grad = ((pull - inner[:, None] * unit_rows) / row_norm[:, None]).astype(jnp.bfloat16)
 
-    gathered_grad, head_x = gather_head(head_grad)
+    gathered_grad = gather_head(head_grad)
     hidden_grad = lax.dot_general(
         gathered_grad, down_weight, contract_last, preferred_element_type=jnp.float32
     )
@@ -746,7 +781,7 @@
         gate_grad_act, gate_weight, contract_last, preferred_element_type=jnp.float32
     ) + lax.dot_general(up_grad_act, up_weight, contract_last, preferred_element_type=jnp.float32)
     input_grad, hidden_grad_x, head_cols = finish_links(
-        input_term.astype(jnp.bfloat16), hidden_grad.T.astype(jnp.bfloat16), head_x
+        input_term.astype(jnp.bfloat16), hidden_grad.T.astype(jnp.bfloat16), gathered_grad
     )
     over_groups = (((0, 2), (0, 1)), ((), ()))
     hidden_grad_x = hidden_grad_x.astype(jnp.float32)
@@ -760,7 +795,7 @@
         for k in range(2)
     ]
     down_grad = lax.dot_general(
-        hidden_x, head_cols.reshape(4, 256, 1024), over_groups, preferred_element_type=jnp.float32
+        hidden_x, head_cols, over_groups, preferred_element_type=jnp.float32
     ).astype(jnp.bfloat16)
     return (query_loss, input_grad, weight_grads[0].T, weight_grads[1].T, down_grad)
 

time: 227 us -> 219 us (0.965)
  Pallas kernels: 196 us -> 188 us
    pallas_call x1, Pallas kernels: 99.7 us -> 92.8 us  [attend(): pl.pallas_call(kernel, out_shape=(jax.ShapeDtypeStruct((8, 4096), jnp.flo...]
    pallas_call x1, Pallas kernels: 26.9 us -> 29.4 us  [gather_head(): pl.pallas_call(kernel, out_shape=jax.ShapeDtypeStruct((32, 8, 4096), jnp....]
where the time goes in v8:
time: 219 us; the launch traced here: 218 us
  Pallas kernels  188 us (86%)
  matrix products  16.6 us (8%)
  other arithmetic  7.31 us (3%)
  local copies, waits for them, and re-layouts  5.11 us (2%)
    pallas_call x1, Pallas kernels, attend(): pl.pallas_call(kernel, out_shape=(jax.ShapeDtypeStruct((8, 4096), jnp.flo...  92.8 us
    pallas_call x1, Pallas kernels, finish_links(): pl.pallas_call(kernel, out_shape=(bf(256, 128), bf(4, *acts.shape), bf(4,...  29.4 us
    pallas_call x1, Pallas kernels, gather_head(): pl.pallas_call(kernel, out_shape=jax.ShapeDtypeStruct((32, 8, 4096), jnp....  29.4 us
    pallas_call x1, Pallas kernels, gather_input(): pl.pallas_call(kernel, out_shape=(jax.ShapeDtypeStruct((rows, cols * 32),...  22.9 us
    pallas_call x1, Pallas kernels, scatter_branch(): pl.pallas_call(kernel, out_shape=jax.ShapeDtypeStruct((8, 4096), jnp.floa...  14 us
    unnamed x34, local copies, waits for them, and re-layouts  4.58 us

profile of v8, /device:TPU:1, one launch (start us, length us, event | category | flops | bytes accessed | tf_op | source)
XLA Modules:
  0.0 218.4 jit_solution(9299710841298193364)
XLA Ops:
  0.6 1.0 fusion.16
  1.6 1.4 compare_reduce_fusion
  3.1 0.1 select_reduce_fusion.1
  3.1 0.0 copy-start.1
  3.1 0.8 copy-done.1
  4.0 22.9 %gather_input.1 = (bf16[256,4096]{1,0:T(8,128)(2,1)S(1)}, s32[4,8,128]{2,1,0:T(8,128)}, s32[32,4,8,128]{3,2,1,0:T(8,128)S(1)}) custom-call(bf16[256,128]{1,0:T(8,128)(2,1)S(1)} %copy-done.1, s32[8,128]{1,0:T(8,128)S(1)} %broadcast_add_fusion.tab), custom_call_target="tpu_custom_call" | custom-call | tf_op jit(solution)/shard_map/gather_input/pallas_call | solution.py:266
  26.9 0.0 copy-start
  26.9 0.0 copy-start.2
  26.9 4.0 %fusion.30 = f32[256,448]{0,1:T(8,128)S(1)} fusion(bf16[256,4096]{1,0:T(8,128)(2,1)S(1)} %get-tuple-element.15.inp, bf16[4096,448]{0,1:T(8,128)(2,1)} %param.13), kind=kOutput, calls=%fused_computation.72 | convolution fusion | flops 939524096 | bytes 6225920 | tf_op jit(solution)/shard_map/dot_general | solution.py:745
  30.9 0.0 copy-done
  30.9 0.0 copy-done.2
  30.9 0.0 copy-start.5
  31.0 0.0 copy-start.10
  31.0 1.1 fusion.29
  32.1 0.0 copy-done.5
  32.1 1.0 copy-done.10
  33.2 1.4 convolution_bitcast_fusion.src
  34.5 0.0 copy-start.7
  34.5 0.0 copy-start.8
  34.6 0.0 copy-start.9
  34.6 0.0 copy-start.15
  34.6 0.0 copy-start.6
  34.6 14.0 %scatter_branch.1 = f32[8,4096]{1,0:T(8,128)S(1)} custom-call(bf16[32,8,4096]{2,1,0:T(8,128)(2,1)S(1)} %convolution_bitcast_fusion.src), custom_call_target="tpu_custom_call" | custom-call | tf_op jit(solution)/shard_map/scatter_branch/pallas_call | solution.py:286
  48.6 0.0 copy-done.7
  48.6 0.1 multiply_reduce_fusion.1
  48.7 0.0 copy-done.8
  48.7 0.2 fusion.28
  49.0 0.1 copy.27
  49.1 0.0 copy-done.9
  49.1 0.1 squeeze.4
  49.1 0.1 copy.26
  49.2 0.5 broadcast.119
  49.8 0.0 copy-done.15
  49.8 0.7 reduce.11
  50.4 0.1 lt.11
  50.5 0.1 copy.25
  50.6 0.1 fusion.20
  50.7 0.1 eq.51
  50.8 2.3 %select_reduce_fusion = s32[32,4,8]{2,1,0:T(4,128)S(1)} fusion(s32[32,4,8,128]{3,2,1,0:T(8,128)S(1)} %get-tuple-element.16, pred[128]{0:T(512)(128)(4,1)S(1)} %iota_compare_fusion.1), kind=kLoop, calls=%fused_computation.15 | loop fusion | flops 261120 | bytes 528512 | tf_op jit(solution)/shard_map/reduce_sum | solution.py:732
  53.1 0.2 bitcast_select_fusion.code
  53.3 0.0 copy-done.6
  53.3 0.3 fusion.15
  53.7 0.0 copy-start.11
  53.7 92.8 %attend.1 = (f32[8,4096]{1,0:T(8,128)S(1)}, f32[8,128]{1,0:T(8,128)S(1)}, bf16[4,448,256]{2,1,0:T(8,128)(2,1)}, bf16[4,2,448,256]{3,2,1,0:T(8,128)(2,1)}, bf16[4,256,1024]{2,1,0:T(8,128)(2,1)}) custom-call(bf16[8,4096]{1,0:T(8,128)(2,1)S(1)} %get-tuple-element.32.unit, bf16[512,4096]{1,0:T(8,128)(2,1)} %index.1, s32[1024,8]{1,0:T(8,128)S(1)} %bitcast_select_fusion.code, ...), custom_call_target="tpu_custom_call" | custom-call | tf_op jit(solution)/shard_map/attend/pallas_call | solution.py:581
  146.4 0.2 fusion.22
  146.6 0.5 log_subtract_fusion
  147.2 0.1 divide_convert_fusion.head
  147.3 29.4 %gather_head.1 = bf16[32,8,4096]{2,1,0:T(8,128)(2,1)S(1)} custom-call(bf16[8,4096]{1,0:T(8,128)(2,1)S(1)} %divide_convert_fusion.head), custom_call_target="tpu_custom_call" | custom-call | tf_op jit(solution)/shard_map/gather_head/pallas_call | solution.py:621
  176.7 0.0 copy-done.11
  176.7 0.0 copy-start.3
  176.7 1.1 fusion.23
  177.9 0.9 copy-done.3
  178.7 1.4 fusion.13
  180.2 0.6 copy-done.4
  180.8 1.3 fusion.src
  182.1 0.0 copy-start.12
  182.1 0.0 copy-start.13
  182.2 29.4 %finish_links.1 = (bf16[256,128]{1,0:T(8,128)(2,1)S(1)}, bf16[4,448,256]{2,1,0:T(8,128)(2,1)S(1)}, bf16[4,256,1024]{2,1,0:T(8,128)(2,1)S(1)}) custom-call(bf16[256,4096]{1,0:T(8,128)(2,1)S(1)} %fusion.src, bf16[448,256]{1,0:T(8,128)(2,1)S(1)} %convert_bitcast_fusion.act, bf16[256,4096]{1,0:T(8,128)(2,1)S(1)} %bitcast.91), custom_call_target="tpu_custom_call" | custom-call | tf_op jit(solution)/shard_map/finish_links/pallas_call | solution.py:694
  211.6 0.0 copy-done.12
  211.6 0.0 copy-done.13
  211.6 2.1 bitcast_convert_fusion.2
  213.7 2.1 bitcast_convert_fusion.1
  215.7 2.0 bitcast_convert_fusion
  217.8 0.6 copy.38
  (13 shorter events, 0.1 us)
Async XLA Ops:
  3.1 0.8 copy-start.1
  26.9 4.0 %copy-start = (bf16[256,4096]{1,0:T(8,128)(2,1)}, bf16[256,4096]{1,0:T(8,128)(2,1)S(1)}, u32[]{:S(2)}) copy-start(bf16[256,4096]{1,0:T(8,128)(2,1)S(1)} %get-tuple-element.15.inp) | copy-start | bytes 6291460
  26.9 4.0 %copy-start.2 = (bf16[4096,448]{0,1:T(8,128)(2,1)S(1)}, bf16[4096,448]{0,1:T(8,128)(2,1)}, u32[]{:S(2)}) copy-start(bf16[4096,448]{0,1:T(8,128)(2,1)} %param.12) | copy-start | bytes 11010052
  30.9 1.2 copy-start.5
  31.0 2.2 %copy-start.10 = (bf16[448,4096]{1,0:T(8,128)(2,1)S(1)}, bf16[448,4096]{1,0:T(8,128)(2,1)}, u32[]{:S(2)}) copy-start(bf16[448,4096]{1,0:T(8,128)(2,1)} %param.14) | copy-start | bytes 11010052
  34.5 14.0 %copy-start.7 = (bf16[8,4096]{1,0:T(8,128)(2,1)S(1)}, bf16[8,4096]{1,0:T(8,128)(2,1)}, u32[]{:S(2)}) copy-start(bf16[8,4096]{1,0:T(8,128)(2,1)} %param.11) | copy-start | bytes 196612
  34.5 14.2 %copy-start.8 = (bf16[8,4096]{1,0:T(8,128)(2,1)S(1)}, bf16[8,4096]{1,0:T(8,128)(2,1)}, u32[]{:S(2)}) copy-start(bf16[8,4096]{1,0:T(8,128)(2,1)} %param.16) | copy-start | bytes 196612
  34.6 14.5 %copy-start.9 = (s32[128,1,8]{0,2,1:T(8,128)S(1)}, s32[128,1,8]{0,2,1:T(8,128)}, u32[]{:S(2)}) copy-start(s32[128,1,8]{0,2,1:T(8,128)} %param.17) | copy-start | bytes 12292
  34.6 15.2 %copy-start.15 = (s32[128,1]{0,1:T(1,128)S(1)}, s32[128,1]{0,1:T(1,128)}, u32[]{:S(2)}) copy-start(s32[128,1]{0,1:T(1,128)} %param.18) | copy-start | bytes 1540
  34.6 18.7 %copy-start.6 = (f32[256,448]{0,1:T(8,128)S(1)}, f32[256,448]{0,1:T(8,128)}, u32[]{:S(2)}) copy-start(f32[256,448]{0,1:T(8,128)} %copy-done.5) | copy-start | bytes 1376260
  53.7 123.0 %copy-start.11 = (bf16[448,4096]{1,0:T(8,128)(2,1)S(1)}, bf16[448,4096]{1,0:T(8,128)(2,1)}, u32[]{:S(2)}) copy-start(bf16[448,4096]{1,0:T(8,128)(2,1)} %param.14) | copy-start | bytes 11010052
  176.7 2.0 copy-start.3
  178.7 2.0 copy-start.4
  182.1 29.4 %copy-start.12 = (bf16[4,256,1024]{2,1,0:T(8,128)(2,1)S(1)}, bf16[4,256,1024]{2,1,0:T(8,128)(2,1)}, u32[]{:S(2)}) copy-start(bf16[4,256,1024]{2,1,0:T(8,128)(2,1)} %get-tuple-element.20) | copy-start | bytes 6291460
  182.1 29.4 %copy-start.13 = (bf16[4,2,448,256]{3,2,1,0:T(8,128)(2,1)S(1)}, bf16[4,2,448,256]{3,2,1,0:T(8,128)(2,1)}, u32[]{:S(2)}) copy-start(bf16[4,2,448,256]{3,2,1,0:T(8,128)(2,1)} %get-tuple-element.22) | copy-start | bytes 5505028
  213.7 2.1 copy-start.14

commit v9 on v8

--- a/solution.py
+++ b/solution.py
@@ -501,7 +501,7 @@
             y = (p.y + base + (other - base) * (1 - swap)) % 4
             return z * 4 + y
 
-        for stages, groups in (((0,), ()), ((1,), (1,)), ((2, 3), (3, 2))):
+        for stages, groups in (((0,), ()), ((1,), (1,)), ((2, 3), (2, 3))):
             filled = 0
             for stage in stages:
                 turns = 7 - 2 * stage

time: 219 us -> 219 us (level)
    pallas_call x1, Pallas kernels: 92.8 us -> 105 us  [attend(): pl.pallas_call(kernel, out_shape=(jax.ShapeDtypeStruct((8, 4096), jnp.flo...]
    pallas_call x1, Pallas kernels: 29.4 us -> 17.3 us  [gather_head(): pl.pallas_call(kernel, out_shape=jax.ShapeDtypeStruct((32, 8, 4096), jnp....]
where the time goes in v9:
time: 219 us; the launch traced here: 218 us
  Pallas kernels  188 us (86%)
  matrix products  16.6 us (8%)
  other arithmetic  7.31 us (3%)
  local copies, waits for them, and re-layouts  5.11 us (2%)
    pallas_call x1, Pallas kernels, attend(): pl.pallas_call(kernel, out_shape=(jax.ShapeDtypeStruct((8, 4096), jnp.flo...  105 us
    pallas_call x1, Pallas kernels, finish_links(): pl.pallas_call(kernel, out_shape=(bf(256, 128), bf(4, *acts.shape), bf(4,...  28.9 us
    pallas_call x1, Pallas kernels, gather_input(): pl.pallas_call(kernel, out_shape=(jax.ShapeDtypeStruct((rows, cols * 32),...  22.9 us
    pallas_call x1, Pallas kernels, gather_head(): pl.pallas_call(kernel, out_shape=jax.ShapeDtypeStruct((32, 8, 4096), jnp....  17.3 us
    pallas_call x1, Pallas kernels, scatter_branch(): pl.pallas_call(kernel, out_shape=jax.ShapeDtypeStruct((8, 4096), jnp.floa...  14 us
    unnamed x34, local copies, waits for them, and re-layouts  4.58 us

profile of v9, /device:TPU:1, one launch (start us, length us, event | category | flops | bytes accessed | tf_op | source)
XLA Modules:
  0.0 218.2 jit_solution(277859339251480754)
XLA Ops:
  0.6 1.0 fusion.16
  1.6 1.4 compare_reduce_fusion
  3.1 0.1 select_reduce_fusion.1
  3.1 0.0 copy-start.1
  3.1 0.8 copy-done.1
  4.0 22.9 %gather_input.1 = (bf16[256,4096]{1,0:T(8,128)(2,1)S(1)}, s32[4,8,128]{2,1,0:T(8,128)}, s32[32,4,8,128]{3,2,1,0:T(8,128)S(1)}) custom-call(bf16[256,128]{1,0:T(8,128)(2,1)S(1)} %copy-done.1, s32[8,128]{1,0:T(8,128)S(1)} %broadcast_add_fusion.tab), custom_call_target="tpu_custom_call" | custom-call | tf_op jit(solution)/shard_map/gather_input/pallas_call | solution.py:266
  26.9 0.0 copy-start
  26.9 0.0 copy-start.2
  26.9 4.0 %fusion.30 = f32[256,448]{0,1:T(8,128)S(1)} fusion(bf16[256,4096]{1,0:T(8,128)(2,1)S(1)} %get-tuple-element.15.inp, bf16[4096,448]{0,1:T(8,128)(2,1)} %param.13), kind=kOutput, calls=%fused_computation.72 | convolution fusion | flops 939524096 | bytes 6225920 | tf_op jit(solution)/shard_map/dot_general | solution.py:745
  30.9 0.0 copy-done
  30.9 0.0 copy-done.2
  30.9 0.0 copy-start.5
  31.0 0.0 copy-start.10
  31.0 1.1 fusion.29
  32.1 0.0 copy-done.5
  32.1 1.0 copy-done.10
  33.2 1.4 convolution_bitcast_fusion.src
  34.5 0.0 copy-start.7
  34.5 0.0 copy-start.8
  34.6 0.0 copy-start.9
  34.6 0.0 copy-start.15
  34.6 0.0 copy-start.6
  34.6 14.0 %scatter_branch.1 = f32[8,4096]{1,0:T(8,128)S(1)} custom-call(bf16[32,8,4096]{2,1,0:T(8,128)(2,1)S(1)} %convolution_bitcast_fusion.src), custom_call_target="tpu_custom_call" | custom-call | tf_op jit(solution)/shard_map/scatter_branch/pallas_call | solution.py:286
  48.6 0.0 copy-done.7
  48.6 0.1 multiply_reduce_fusion.1
  48.7 0.0 copy-done.8
  48.7 0.2 fusion.28
  49.0 0.1 copy.27
  49.1 0.0 copy-done.9
  49.1 0.1 squeeze.4
  49.1 0.1 copy.26
  49.2 0.5 broadcast.119
  49.8 0.0 copy-done.15
  49.8 0.7 reduce.11
  50.4 0.1 lt.11
  50.5 0.1 copy.25
  50.6 0.1 fusion.20
  50.7 0.1 eq.51
  50.8 2.3 %select_reduce_fusion = s32[32,4,8]{2,1,0:T(4,128)S(1)} fusion(s32[32,4,8,128]{3,2,1,0:T(8,128)S(1)} %get-tuple-element.16, pred[128]{0:T(512)(128)(4,1)S(1)} %iota_compare_fusion.1), kind=kLoop, calls=%fused_computation.15 | loop fusion | flops 261120 | bytes 528512 | tf_op jit(solution)/shard_map/reduce_sum | solution.py:732
  53.1 0.2 bitcast_select_fusion.code
  53.3 0.0 copy-done.6
  53.3 0.3 fusion.15
  53.7 0.0 copy-start.11
  53.7 105.1 %attend.1 = (f32[8,4096]{1,0:T(8,128)S(1)}, f32[8,128]{1,0:T(8,128)S(1)}, bf16[4,448,256]{2,1,0:T(8,128)(2,1)}, bf16[4,2,448,256]{3,2,1,0:T(8,128)(2,1)}, bf16[4,256,1024]{2,1,0:T(8,128)(2,1)}) custom-call(bf16[8,4096]{1,0:T(8,128)(2,1)S(1)} %get-tuple-element.32.unit, bf16[512,4096]{1,0:T(8,128)(2,1)} %index.1, s32[1024,8]{1,0:T(8,128)S(1)} %bitcast_select_fusion.code, ...), custom_call_target="tpu_custom_call" | custom-call | tf_op jit(solution)/shard_map/attend/pallas_call | solution.py:581
  158.8 0.2 fusion.22
  159.0 0.5 log_subtract_fusion
  159.5 0.1 divide_convert_fusion.head
  159.6 17.3 %gather_head.1 = bf16[32,8,4096]{2,1,0:T(8,128)(2,1)S(1)} custom-call(bf16[8,4096]{1,0:T(8,128)(2,1)S(1)} %divide_convert_fusion.head), custom_call_target="tpu_custom_call" | custom-call | tf_op jit(solution)/shard_map/gather_head/pallas_call | solution.py:621
  177.0 0.0 copy-done.11
  177.0 0.0 copy-start.3
  177.0 1.1 fusion.23
  178.1 0.9 copy-done.3
  179.0 1.4 fusion.13
  180.4 0.6 copy-done.4
  181.0 1.3 fusion.src
  182.4 0.0 copy-start.12
  182.4 0.0 copy-start.13
  182.4 28.9 %finish_links.1 = (bf16[256,128]{1,0:T(8,128)(2,1)S(1)}, bf16[4,448,256]{2,1,0:T(8,128)(2,1)S(1)}, bf16[4,256,1024]{2,1,0:T(8,128)(2,1)S(1)}) custom-call(bf16[256,4096]{1,0:T(8,128)(2,1)S(1)} %fusion.src, bf16[448,256]{1,0:T(8,128)(2,1)S(1)} %convert_bitcast_fusion.act, bf16[256,4096]{1,0:T(8,128)(2,1)S(1)} %bitcast.91), custom_call_target="tpu_custom_call" | custom-call | tf_op jit(solution)/shard_map/finish_links/pallas_call | solution.py:694
  211.4 0.0 copy-done.12
  211.4 0.0 copy-done.13
  211.4 2.1 bitcast_convert_fusion.2
  213.5 2.1 bitcast_convert_fusion.1
  215.6 2.0 bitcast_convert_fusion
  217.6 0.6 copy.38
  (13 shorter events, 0.1 us)
Async XLA Ops:
  3.1 0.8 copy-start.1
  26.9 4.0 %copy-start = (bf16[256,4096]{1,0:T(8,128)(2,1)}, bf16[256,4096]{1,0:T(8,128)(2,1)S(1)}, u32[]{:S(2)}) copy-start(bf16[256,4096]{1,0:T(8,128)(2,1)S(1)} %get-tuple-element.15.inp) | copy-start | bytes 6291460
  26.9 4.0 %copy-start.2 = (bf16[4096,448]{0,1:T(8,128)(2,1)S(1)}, bf16[4096,448]{0,1:T(8,128)(2,1)}, u32[]{:S(2)}) copy-start(bf16[4096,448]{0,1:T(8,128)(2,1)} %param.12) | copy-start | bytes 11010052
  30.9 1.2 copy-start.5
  31.0 2.2 %copy-start.10 = (bf16[448,4096]{1,0:T(8,128)(2,1)S(1)}, bf16[448,4096]{1,0:T(8,128)(2,1)}, u32[]{:S(2)}) copy-start(bf16[448,4096]{1,0:T(8,128)(2,1)} %param.14) | copy-start | bytes 11010052
  34.5 14.0 %copy-start.7 = (bf16[8,4096]{1,0:T(8,128)(2,1)S(1)}, bf16[8,4096]{1,0:T(8,128)(2,1)}, u32[]{:S(2)}) copy-start(bf16[8,4096]{1,0:T(8,128)(2,1)} %param.11) | copy-start | bytes 196612
  34.5 14.2 %copy-start.8 = (bf16[8,4096]{1,0:T(8,128)(2,1)S(1)}, bf16[8,4096]{1,0:T(8,128)(2,1)}, u32[]{:S(2)}) copy-start(bf16[8,4096]{1,0:T(8,128)(2,1)} %param.16) | copy-start | bytes 196612
  34.6 14.5 %copy-start.9 = (s32[128,1,8]{0,2,1:T(8,128)S(1)}, s32[128,1,8]{0,2,1:T(8,128)}, u32[]{:S(2)}) copy-start(s32[128,1,8]{0,2,1:T(8,128)} %param.17) | copy-start | bytes 12292
  34.6 15.2 %copy-start.15 = (s32[128,1]{0,1:T(1,128)S(1)}, s32[128,1]{0,1:T(1,128)}, u32[]{:S(2)}) copy-start(s32[128,1]{0,1:T(1,128)} %param.18) | copy-start | bytes 1540
  34.6 18.7 %copy-start.6 = (f32[256,448]{0,1:T(8,128)S(1)}, f32[256,448]{0,1:T(8,128)}, u32[]{:S(2)}) copy-start(f32[256,448]{0,1:T(8,128)} %copy-done.5) | copy-start | bytes 1376260
  53.7 123.3 %copy-start.11 = (bf16[448,4096]{1,0:T(8,128)(2,1)S(1)}, bf16[448,4096]{1,0:T(8,128)(2,1)}, u32[]{:S(2)}) copy-start(bf16[448,4096]{1,0:T(8,128)(2,1)} %param.14) | copy-start | bytes 11010052
  177.0 2.0 copy-start.3
  179.0 2.0 copy-start.4
  182.4 29.0 %copy-start.12 = (bf16[4,256,1024]{2,1,0:T(8,128)(2,1)S(1)}, bf16[4,256,1024]{2,1,0:T(8,128)(2,1)}, u32[]{:S(2)}) copy-start(bf16[4,256,1024]{2,1,0:T(8,128)(2,1)} %get-tuple-element.20) | copy-start | bytes 6291460
  182.4 29.0 %copy-start.13 = (bf16[4,2,448,256]{3,2,1,0:T(8,128)(2,1)S(1)}, bf16[4,2,448,256]{3,2,1,0:T(8,128)(2,1)}, u32[]{:S(2)}) copy-start(bf16[4,2,448,256]{3,2,1,0:T(8,128)(2,1)} %get-tuple-element.22) | copy-start | bytes 5505028
  213.5 2.1 copy-start.14
